TPU v7x, 256 devices: a whole 4x4x8 slice. The times are simulated.
256 devices in a mesh: seq: 32 (over x, z), head: 8 (over y, core).
Axes of the slice: x: 4, y: 4, z: 8, core: 2. Of those that a mesh axis runs over, the one named last changes fastest.
Arguments:
- tokens: bfloat16 [32768, 3072], P(('seq', 'head')), may hold values from -150 to 150
- norm_gain: float32 [3072], replicated, may hold values from 0.1 to 1.9
- w_query: bfloat16 [3072, 3072], P(None, 'head'), may hold values from -0.15625 to 0.15625
- w_key: bfloat16 [3072, 1024], P(None, 'head'), may hold values from -0.15625 to 0.15625
- w_value: bfloat16 [3072, 1024], P(None, 'head'), may hold values from -0.109375 to 0.109375
- w_out: bfloat16 [3072, 3072], P('head'), may hold values from -1.5 to 1.5
- long_cache: bfloat16 [2, 32768, 1024], P(None, 'seq', 'head'), may hold values from -244 to 244
- short_cache: bfloat16 [2, 8192, 1024], P(None, 'seq', 'head'), may hold values from -244 to 244
- slot_owner: int32 [8192], P('seq'), may hold values from -1 to 63, as said below
- new_len: int32 [64], replicated, may hold values from 2 to 1024, as said below
- cache_len: int32 [64], replicated, may hold values from 32 to 85, as said below
Outputs:
- layer_out: bfloat16 [32768, 3072], P(('seq', 'head'))
Inputs may be any that keep to these rules, and one draw needn't show every extreme that they name: `new_len`: lengths in order after the lead request's 64 tokens; they sum to 32704, and one request has exactly 1024 new tokens. `cache_len`: equals the number of short-cache slots that the request owns; one request has exactly 85. `slot_owner`: A request's slots are contiguous and lie in the block of 256 slots whose index equals that of the block of 1024 tokens holding the request's first new token.
All inputs are finite; a program needn't handle non-finite values.
Results may differ from a plain program's by a relative error of at most 0.02.
The roundings to bfloat16 on the way count: a program that leaves them out, or rounds other values in their place, can miss the bound.
Values may be sent and summed in bfloat16 or wider, within the bound.
A program may use at most 128 MiB of HBM per device.

v0:
```python
import math

import jax
import jax.numpy as jnp
from jax import lax
from jax.sharding import PartitionSpec as P

HD = 128
LEAD = 64


THETA_LOG = math.log(500000.0)


def from_behind(block, axis, distance):
    devices = range(lax.axis_size(axis))
    route = [(i - distance, i) for i in devices if i - distance in devices]
    return lax.ppermute(block, axis, route)


def rotate(field, position):
    half = field.shape[-1] // 2
    frequency = jnp.exp(jnp.arange(half, dtype=jnp.float32) * (-2.0 * THETA_LOG / field.shape[-1]))
    angle = position.astype(jnp.float32)[:, None] * frequency[None, :]
    cosine = jnp.cos(angle)[:, None, :]
    sine_part = jnp.sin(angle)[:, None, :]
    first_half = field[..., :half]
    second_half = field[..., half:]
    return jnp.concatenate(
        [
            first_half * cosine - second_half * sine_part,
            second_half * cosine + first_half * sine_part,
        ],
        axis=-1,
    )


def request_starts(new_len):
    return LEAD + jnp.cumsum(new_len) - new_len


def request_of(position_index, starts):
    passed = (starts[None, :] <= position_index[:, None]).astype(jnp.int32)
    request = jnp.sum(passed, axis=1) - 1
    return jnp.where(request < 0, starts.shape[0], request)


def position_of(position_index, request, starts, cache_len, long_len):
    number = starts.shape[0]
    select = jnp.arange(number, dtype=jnp.int32)[None, :] == request[:, None]
    begin = jnp.sum(jnp.where(select, starts[None, :], 0), axis=1)
    cached = jnp.sum(jnp.where(select, cache_len[None, :], 0), axis=1)
    return jnp.where(request == number, position_index + long_len, position_index - begin + cached)


def normalize(tokens, norm_gain):
    values = tokens.astype(jnp.float32)
    mean_square = jnp.mean(values * values, axis=-1, keepdims=True)
    return (values * lax.rsqrt(mean_square + 1e-05) * norm_gain).astype(jnp.bfloat16)


def raw_scores(queries, keys):
    return jnp.einsum("bgph,ngh->bgpn", queries, keys, preferred_element_type=jnp.float32) * (
        1.0 / math.sqrt(keys.shape[-1])
    )


def finish_state(scores, values):
    highest = jnp.max(scores, axis=-1)
    weights = jnp.exp(scores - highest[..., None])
    summed = jnp.sum(weights, axis=-1)
    mixture = jnp.einsum(
        "bgpn,ngh->bgph", weights.astype(jnp.bfloat16), values, preferred_element_type=jnp.float32
    )
    return (highest, summed, mixture)


def masked_state(queries, keys, values, valid):
    scores = jnp.where(valid[:, None, None, :], raw_scores(queries, keys), -jnp.inf)
    return finish_state(scores, values)


def plain_state(queries, keys, values):
    return finish_state(raw_scores(queries, keys), values)


def combine(former, latter):
    highest = jnp.maximum(former[0], latter[0])
    scale_former = jnp.exp(former[0] - highest)
    scale_latter = jnp.exp(latter[0] - highest)
    summed = former[1] * scale_former + latter[1] * scale_latter
    mixture = former[2] * scale_former[..., None] + latter[2] * scale_latter[..., None]
    return (highest, summed, mixture)


def on_device(
    tokens,
    norm_gain,
    w_query,
    w_key,
    w_value,
    w_out,
    long_cache,
    short_cache,
    slot_owner,
    new_len,
    cache_len,
):
    seq_index = lax.axis_index("seq")
    long_len = long_cache.shape[1] * lax.axis_size("seq")
    kv_heads = w_key.shape[1] // HD
    q_heads = w_query.shape[1] // HD
    per_kv = q_heads // kv_heads
    slots = short_cache.shape[1]
    q_width = w_query.shape[1]
    k_width = w_key.shape[1]
    earlier_slots, earlier_owner = from_behind((short_cache, slot_owner), "seq", 1)
    normed = normalize(tokens, norm_gain)
    piece = lax.all_gather(normed, "head", axis=0, tiled=True)
    projected = jnp.concatenate(
        [
            jnp.dot(piece, w_query, preferred_element_type=jnp.float32),
            jnp.dot(piece, w_key, preferred_element_type=jnp.float32),
            jnp.dot(piece, w_value, preferred_element_type=jnp.float32),
        ],
        axis=1,
    )
    local_rows = projected.shape[0]
    starts = request_starts(new_len)
    token_index = seq_index * local_rows + jnp.arange(local_rows, dtype=jnp.int32)
    request = request_of(token_index, starts)
    position = position_of(token_index, request, starts, cache_len, long_len)
    before_index = token_index - local_rows
    before_request = request_of(before_index, starts)
    queries = rotate(projected[:, :q_width].reshape(local_rows, q_heads, HD), position).astype(
        jnp.bfloat16
    )
    queries = queries.reshape(local_rows, kv_heads, per_kv, HD)
    keys = rotate(
        projected[:, q_width : q_width + k_width].reshape(local_rows, kv_heads, HD), position
    ).astype(jnp.bfloat16)
    values = projected[:, q_width + k_width :].astype(jnp.bfloat16)
    fresh = jnp.stack([keys.reshape(local_rows, k_width), values])
    earlier_fresh = from_behind(fresh, "seq", 1)
    has_before = seq_index > 0
    new_rows = jnp.concatenate([earlier_fresh, fresh], axis=1)
    new_keys = new_rows[0].reshape(-1, kv_heads, HD)
    new_values = new_rows[1].reshape(-1, kv_heads, HD)
    slot_rows = jnp.concatenate([earlier_slots, short_cache], axis=1)
    slot_keys = slot_rows[0].reshape(-1, kv_heads, HD)
    slot_values = slot_rows[1].reshape(-1, kv_heads, HD)
    new_request = jnp.concatenate([jnp.where(has_before, before_request, -1), request])
    new_index = jnp.concatenate([before_index, token_index])
    slot_request = jnp.concatenate([jnp.where(has_before, earlier_owner, -1), slot_owner]).astype(
        jnp.int32
    )
    slot_index = jnp.full((2 * slots,), -1, jnp.int32)
    block_rows = min(local_rows, 512)
    block_count = local_rows // block_rows
    window = local_rows + block_rows

    def local_block(item):
        block_queries, block_request, block_index, block_number = item
        begin = block_number * block_rows
        window_keys = jnp.concatenate(
            [lax.dynamic_slice_in_dim(new_keys, begin, window, 0), slot_keys], axis=0
        )
        window_values = jnp.concatenate(
            [lax.dynamic_slice_in_dim(new_values, begin, window, 0), slot_values], axis=0
        )
        window_request = jnp.concatenate(
            [lax.dynamic_slice_in_dim(new_request, begin, window, 0), slot_request]
        )
        window_index = jnp.concatenate(
            [lax.dynamic_slice_in_dim(new_index, begin, window, 0), slot_index]
        )
        valid = (window_request[None, :] == block_request[:, None]) & (
            window_index[None, :] <= block_index[:, None]
        )
        return masked_state(block_queries, window_keys, window_values, valid)

    highest, summed, mixture = lax.map(
        local_block,
        (
            queries.reshape(block_count, block_rows, kv_heads, per_kv, HD),
            request.reshape(block_count, block_rows),
            token_index.reshape(block_count, block_rows),
            jnp.arange(block_count, dtype=jnp.int32),
        ),
    )
    highest = highest.reshape(local_rows, kv_heads, per_kv)
    summed = summed.reshape(local_rows, kv_heads, per_kv)
    mixture = mixture.reshape(local_rows, kv_heads, per_kv, HD)
    lead_queries = queries[:LEAD]
    start_state = (
        jnp.full((LEAD, kv_heads, per_kv), -1e30, jnp.float32),
        jnp.zeros((LEAD, kv_heads, per_kv), jnp.float32),
        jnp.zeros((LEAD, kv_heads, per_kv, HD), jnp.float32),
    )
    piece = lax.all_gather(long_cache, "seq", axis=1, tiled=True)
    long_state = combine(
        start_state,
        plain_state(
            lead_queries, piece[0].reshape(-1, kv_heads, HD), piece[1].reshape(-1, kv_heads, HD)
        ),
    )
    long_highest = jnp.where(seq_index == 0, long_state[0], -1e30)
    joined = combine(
        (highest[:LEAD], summed[:LEAD], mixture[:LEAD]),
        (long_highest, long_state[1], long_state[2]),
    )
    summed = jnp.concatenate([joined[1], summed[LEAD:]], axis=0)
    mixture = jnp.concatenate([joined[2], mixture[LEAD:]], axis=0)
    attended = (mixture / summed[..., None]).astype(jnp.bfloat16).reshape(local_rows, q_width)
    gathered_sum = lax.psum_scatter(
        jnp.dot(attended, w_out, preferred_element_type=jnp.float32).astype(jnp.bfloat16),
        "head",
        scatter_dimension=0,
        tiled=True,
    )
    return gathered_sum


def solution(mesh):
    placed = (
        P(("seq", "head"), None),
        P(),
        P(None, "head"),
        P(None, "head"),
        P(None, "head"),
        P("head", None),
        P(None, "seq", "head"),
        P(None, "seq", "head"),
        P("seq"),
        P(),
        P(),
    )
    return jax.shard_map(
        on_device, mesh=mesh, in_specs=placed, out_specs=P(("seq", "head"), None), check_vma=False
    )
```

profile of v0, /device:TPU:1, one launch (start us, length us, event | category | flops | bytes accessed | tf_op | source)
XLA Modules:
  0.0 298.3 jit_solution(11702035966844528671)
XLA Ops:
  8.1 2.3 fusion.31
  11.2 4.4 %collective-permute-start = (s32[256]{0:T(256)}, s32[256]{0:T(256)S(1)}, u32[]{:S(2)}, u32[]{:S(2)}) collective-permute-start(s32[256]{0:T(256)} %param.21), channel_id=1, source_target_pairs={{0,8},{8,16},{16,24},{24,32},{32,40},{40,48},{48,56},{56,64},{64,7... | collective-permute-start | bytes 3080 | tf_op jit(solution)/shard_map/ppermute | solution.py:18
  15.6 3.6 %collective-permute-start.2 = (bf16[2,256,128]{2,1,0:T(8,128)(2,1)}, bf16[2,256,128]{2,1,0:T(8,128)(2,1)S(1)}, u32[]{:S(2)}, u32[]{:S(2)}) collective-permute-start(bf16[2,256,128]{2,1,0:T(8,128)(2,1)} %param.20), channel_id=1, source_target_pairs={{0,8},{8,16},{16,24},{24,32},{32,40},{40,48},{48,56},{56,64},{64,7... | collective-permute-start | bytes 393224 | tf_op jit(solution)/shard_map/ppermute | solution.py:18
  22.4 3.1 %multiply_cosine_fusion = (f32[1024,64]{1,0:T(8,128)}, f32[1024,64]{1,0:T(8,128)}) fusion(f32[64]{0:T(128)S(1)} %multiply_exponential_fusion, f32[1024]{0:T(1024)S(1)} %get-tuple-element.196), kind=kLoop, calls=%fused_computation.63 | loop fusion | flops 65536 | bytes 528640 | tf_op jit(solution)/shard_map/cos | solution.py:25
  28.1 30.1 %all-gather.3.cloned.1.call-done = bf16[1024,3072]{1,0:T(8,128)(2,1)} async-done(((bf16[128,3072]{1,0:T(8,128)(2,1)}), bf16[1024,3072]{1,0:T(8,128)(2,1)}) %all-gather.3.cloned.1.call-update) | async-done | bytes 6291472 | tf_op jit(solution)/shard_map/all_gather | solution.py:119
  58.3 5.3 %convolution_bitcast_fusion = f32[1024,1,128]{0,2,1:T(8,128)S(1)} fusion(bf16[1024,3072]{1,0:T(8,128)(2,1)} %all-gather.3.cloned.1.call-done, bf16[3072,128]{1,0:T(8,128)(2,1)} %param.16), kind=kOutput, calls=%fused_computation.51 | convolution fusion | flops 805306368 | bytes 7602176 | tf_op jit(solution)/shard_map/dot_general | solution.py:123
  64.8 2.2 fusion.33
  67.9 4.0 %collective-permute-start.1 = (bf16[2,1024,128]{1,2,0:T(8,128)(2,1)}, bf16[2,1024,128]{1,2,0:T(8,128)(2,1)}, u32[]{:S(2)}, u32[]{:S(2)}) collective-permute-start(bf16[2,1024,128]{1,2,0:T(8,128)(2,1)} %pad_maximum_fusion.1), channel_id=1, source_target_pairs={{0,8},{8,16},{16,24},{24,32},{32,40},{40,48},{48,56},{56,64},{64,7... | collective-permute-start | bytes 1572872 | tf_op jit(solution)/shard_map/ppermute | solution.py:18
  71.9 2.7 fusion.76
  75.6 2.8 copy.74
  80.0 2.6 subtract_convert_fusion
  84.9 4.6 %collective-permute-done.1 = bf16[2,1024,128]{1,2,0:T(8,128)(2,1)} collective-permute-done((bf16[2,1024,128]{1,2,0:T(8,128)(2,1)}, bf16[2,1024,128]{1,2,0:T(8,128)(2,1)}, u32[]{:S(2)}, u32[]{:S(2)}) %collective-permute-start.1) | collective-permute-done | bytes 524320 | tf_op jit(solution)/shard_map/ppermute | solution.py:18
  91.7 73.2 %while.14 = (s32[]{:T(128)}, f32[2,512,1,3]{1,0,3,2:T(2,128)}, f32[2,512,1,3]{1,0,2,3:T(2,128)}, f32[2,512,1,3,128]{4,1,0,3,2:T(8,128)}, s32[2]{0:T(128)S(1)}, /...) while((s32[]{:T(128)}, f32[2,512,1,3]{1,0,3,2:T(2,128)}, ...), condition=%wide.region_9.10_spmd, body=%wide.region_6.9_spmd.sunk | while | flops 1650459648 | bytes 50030996 | solution.py:182
  96.2 2.1 constant_dynamic-slice_fusion.7
  98.2 1.9 copy.86
  100.2 8.1 %fusion.90 = (f32[512,3]{0,1:T(4,128)S(1)}, f32[2048,512,3]{1,0,2:T(8,128)}) fusion(pred[512,2048]{0,1:T(8,128)(4,1)S(1)} %compare_and_fusion.2, bf16[2,512,1,3,128]{4,1,0,3,2:T(8,128)(2,1)} %get-tuple-element.368, s32[]{:T(128)S(6)} %copy.97, bf16[512,1,128]{2,0,1:T(8,128)(2,1)} %get-tuple-element.367, bf16[1536,1,128]{2,0,1:T(8,128)(2,1)} %copy.86), kind=kOutput, calls=%fused_computation.4.clone.1 | convolution fusion | flops 815790592 | bytes 14555140 | tf_op jit(solution)/shard_map/while/body/eval_jaxpr/bgph,ngh->bgpn/dot_general | solution.py:63
  108.4 7.3 %fusion.91 = f32[512,3]{0,1:T(4,128)S(1)} fusion(f32[2048,512,3]{1,0,2:T(8,128)} %get-tuple-element.311, f32[512,3]{0,1:T(4,128)S(1)} %get-tuple-element.310, pred[512,2048]{0,1:T(8,128)(4,1)S(1)} %compare_and_fusion.2), kind=kLoop, calls=%fused_computation.3.clone.1 | loop fusion | flops 12581376 | bytes 13643776 | tf_op jit(solution)/shard_map/while/body/eval_jaxpr/reduce_sum | solution.py:71
  115.8 10.4 %fusion.92 = f32[1,512,1,3,128]{1,4,3,2,0:T(8,128)} fusion(f32[2048,512,3]{1,0,2:T(8,128)} %get-tuple-element.311, f32[512,3]{0,1:T(4,128)S(1)} %get-tuple-element.310, pred[512,2048]{0,1:T(8,128)(4,1)S(1)} %compare_and_fusion.2, bf16[512,1,128]{0,2,1:T(8,128)(2,1)} %get-tuple-element.370, bf16[1536,1,128]{0,2,1:T(8,128)(2,1)} %get-tuple-element.312), kind=kOutput, calls=%fused_computation.9.clone.1 | convolution fusion | flops 818937856 | bytes 14948352 | tf_op jit(solution)/shard_map/while/body/eval_jaxpr/bgpn,ngh->bgph/dot_general | solution.py:72
  133.0 2.1 constant_dynamic-slice_fusion.7
  135.1 1.9 copy.86
  137.0 8.1 %fusion.90 = (f32[512,3]{0,1:T(4,128)S(1)}, f32[2048,512,3]{1,0,2:T(8,128)}) fusion(pred[512,2048]{0,1:T(8,128)(4,1)S(1)} %compare_and_fusion.2, bf16[2,512,1,3,128]{4,1,0,3,2:T(8,128)(2,1)} %get-tuple-element.368, s32[]{:T(128)S(6)} %copy.97, bf16[512,1,128]{2,0,1:T(8,128)(2,1)} %get-tuple-element.367, bf16[1536,1,128]{2,0,1:T(8,128)(2,1)} %copy.86), kind=kOutput, calls=%fused_computation.4.clone.1 | convolution fusion | flops 815790592 | bytes 14555140 | tf_op jit(solution)/shard_map/while/body/eval_jaxpr/bgph,ngh->bgpn/dot_general | solution.py:63
  145.2 7.6 %fusion.91 = f32[512,3]{0,1:T(4,128)S(1)} fusion(f32[2048,512,3]{1,0,2:T(8,128)} %get-tuple-element.311, f32[512,3]{0,1:T(4,128)S(1)} %get-tuple-element.310, pred[512,2048]{0,1:T(8,128)(4,1)S(1)} %compare_and_fusion.2), kind=kLoop, calls=%fused_computation.3.clone.1 | loop fusion | flops 12581376 | bytes 13643776 | tf_op jit(solution)/shard_map/while/body/eval_jaxpr/reduce_sum | solution.py:71
  152.9 9.6 %fusion.92 = f32[1,512,1,3,128]{1,4,3,2,0:T(8,128)} fusion(f32[2048,512,3]{1,0,2:T(8,128)} %get-tuple-element.311, f32[512,3]{0,1:T(4,128)S(1)} %get-tuple-element.310, pred[512,2048]{0,1:T(8,128)(4,1)S(1)} %compare_and_fusion.2, bf16[512,1,128]{0,2,1:T(8,128)(2,1)} %get-tuple-element.370, bf16[1536,1,128]{0,2,1:T(8,128)(2,1)} %get-tuple-element.312), kind=kOutput, calls=%fused_computation.9.clone.1 | convolution fusion | flops 818937856 | bytes 14948352 | tf_op jit(solution)/shard_map/while/body/eval_jaxpr/bgpn,ngh->bgph/dot_general | solution.py:72
  164.9 2.7 slice.77
  167.6 3.1 %copy.54 = f32[960,1,3,128]{0,3,2,1:T(8,128)} copy(f32[960,1,3,128]{3,0,2,1:T(8,128)} %slice.77) | data formatting | bytes 2949120 | tf_op jit(solution)/shard_map/slice | solution.py:213
  170.8 33.9 %all-gather.5.cloned.1.call-done = bf16[2,32768,128]{2,1,0:T(8,128)(2,1)} async-done(((bf16[2,1024,128]{2,1,0:T(8,128)(2,1)}), bf16[2,32768,128]{2,1,0:T(8,128)(2,1)}) %all-gather.5.cloned.1.call-update) | async-done | bytes 16777232 | tf_op jit(solution)/shard_map/all_gather | solution.py:200
  204.8 12.3 %fusion.75 = (f32[64,3]{0,1:T(4,128)S(1)}, f32[64,1,3,32768]{3,0,2,1:T(8,128)}) fusion(bf16[2,32768,128]{2,1,0:T(8,128)(2,1)} %all-gather.5.cloned.1.call-done, bf16[1024,3,64]{2,0,1:T(8,128)(2,1)} %copy-done.4, bf16[1024,3,64]{2,0,1:T(8,128)(2,1)S(1)} %copy-done.3), kind=kOutput, calls=%fused_computation.124 | convolution fusion | flops 1623293696 | bytes 34734848 | tf_op jit(solution)/shard_map/bgph,ngh->bgpn/dot_general | solution.py:63
  217.0 10.6 %fusion.23 = f32[64,3]{0,1:T(4,128)S(1)} fusion(f32[64,1,3,32768]{3,0,2,1:T(8,128)} %get-tuple-element.201, f32[64,3]{0,1:T(4,128)S(1)} %get-tuple-element.200), kind=kLoop, calls=%fused_computation.34 | loop fusion | flops 12582720 | bytes 25167360 | tf_op jit(solution)/shard_map/reduce_sum | solution.py:71
  227.7 14.4 %fusion.49 = f32[64,1,3,128]{3,0,2,1:T(8,128)S(1)} fusion(bf16[2,32768,128]{2,1,0:T(8,128)(2,1)} %all-gather.5.cloned.1.call-done, f32[64,1,3,32768]{3,0,2,1:T(8,128)} %get-tuple-element.201, f32[64,3]{0,1:T(4,128)S(1)} %get-tuple-element.200, f32[1024,1,3,128]{3,0,2,1:T(8,128)} %bitcast.189, f32[64,3]{0,1:T(4,128)S(1)} %bitcast.196, ...), kind=kOutput, calls=%fused_computation.59 | convolution fusion | flops 1623318528 | bytes 33754880 | tf_op jit(solution)/shard_map/bgpn,ngh->bgph/dot_general | solution.py:72
  242.4 1.9 fusion.32
  244.3 5.4 %convolution_convert_fusion = bf16[1024,3072]{1,0:T(8,128)(2,1)} fusion(bf16[1024,384]{0,1:T(8,128)(2,1)S(1)} %fusion.32, bf16[384,3072]{1,0:T(8,128)(2,1)S(1)} %copy-done), kind=kOutput, calls=%fused_computation.41 | convolution fusion | flops 2419064832 | bytes 9437184 | tf_op jit(solution)/shard_map/dot_general | solution.py:216
  249.7 42.1 %reduce-scatter.2.cloned.1.call-done = bf16[128,3072]{1,0:T(8,128)(2,1)} async-done(((bf16[1024,3072]{1,0:T(8,128)(2,1)}), bf16[128,3072]{1,0:T(8,128)(2,1)}) %reduce-scatter.2.cloned.1.call-update) | async-done | bytes 786448 | tf_op jit(solution)/shard_map/reduce_scatter | solution.py:215
  (118 shorter events, 30.3 us)
Async XLA Ops:
  6.5 237.7 %copy-start = (bf16[384,3072]{1,0:T(8,128)(2,1)S(1)}, bf16[384,3072]{1,0:T(8,128)(2,1)}, u32[]{:S(2)}) copy-start(bf16[384,3072]{1,0:T(8,128)(2,1)} %param.18) | copy-start | bytes 7077892
  6.5 20.1 %copy-start.8 = (bf16[2,256,128]{2,1,0:T(8,128)(2,1)S(1)}, bf16[2,256,128]{2,1,0:T(8,128)(2,1)}, u32[]{:S(2)}) copy-start(bf16[2,256,128]{2,1,0:T(8,128)(2,1)} %param.20) | copy-start | bytes 393220
  6.5 51.7 %all-gather.3.cloned.1.call-start = ((), (), s32[]{:S(2)}) async-start(), calls=%async_computation.1 | async-start | bytes 7077888 | tf_op jit(solution)/shard_map/all_gather | solution.py:119
  10.4 194.4 %all-gather.5.cloned.1.call-start = ((), (), s32[]{:S(2)}) async-start(), calls=%async_computation.2 | async-start | bytes 17301504 | tf_op jit(solution)/shard_map/all_gather | solution.py:200
  11.1 280.7 %reduce-scatter.2.cloned.1.call-start = ((), (), s32[]{:S(2)}) async-start(), calls=%async_computation.3 | async-start | bytes 7077888 | tf_op jit(solution)/shard_map/reduce_scatter | solution.py:215
  11.2 14.8 %collective-permute-start = (s32[256]{0:T(256)}, s32[256]{0:T(256)S(1)}, u32[]{:S(2)}, u32[]{:S(2)}) collective-permute-start(s32[256]{0:T(256)} %param.21), channel_id=1, source_target_pairs={{0,8},{8,16},{16,24},{24,32},{32,40},{40,48},{48,56},{56,64},{64,7... | collective-permute-start | bytes 3080 | tf_op jit(solution)/shard_map/ppermute | solution.py:18
  15.6 11.1 %collective-permute-start.2 = (bf16[2,256,128]{2,1,0:T(8,128)(2,1)}, bf16[2,256,128]{2,1,0:T(8,128)(2,1)S(1)}, u32[]{:S(2)}, u32[]{:S(2)}) collective-permute-start(bf16[2,256,128]{2,1,0:T(8,128)(2,1)} %param.20), channel_id=1, source_target_pairs={{0,8},{8,16},{16,24},{24,32},{32,40},{40,48},{48,56},{56,64},{64,7... | collective-permute-start | bytes 393224 | tf_op jit(solution)/shard_map/ppermute | solution.py:18
  28.1 36.6 %copy-start.7 = (bf16[3072,128]{1,0:T(8,128)(2,1)S(1)}, bf16[3072,128]{1,0:T(8,128)(2,1)}, u32[]{:S(2)}) copy-start(bf16[3072,128]{1,0:T(8,128)(2,1)} %param.17) | copy-start | bytes 2359300
  58.3 6.5 %copy-start.1 = (bf16[1024,3072]{1,0:T(8,128)(2,1)S(1)}, bf16[1024,3072]{1,0:T(8,128)(2,1)}, u32[]{:S(2)}) copy-start(bf16[1024,3072]{1,0:T(8,128)(2,1)} %all-gather.3.cloned.1.call-done) | copy-start | bytes 18874372
  64.8 2.2 copy-start.5
  64.8 7.1 %copy-start.15 = (bf16[3072,384]{1,0:T(8,128)(2,1)S(1)}, bf16[3072,384]{1,0:T(8,128)(2,1)}, u32[]{:S(2)}) copy-start(bf16[3072,384]{1,0:T(8,128)(2,1)} %param.15) | copy-start | bytes 7077892
  67.9 21.6 %collective-permute-start.1 = (bf16[2,1024,128]{1,2,0:T(8,128)(2,1)}, bf16[2,1024,128]{1,2,0:T(8,128)(2,1)}, u32[]{:S(2)}, u32[]{:S(2)}) collective-permute-start(bf16[2,1024,128]{1,2,0:T(8,128)(2,1)} %pad_maximum_fusion.1), channel_id=1, source_target_pairs={{0,8},{8,16},{16,24},{24,32},{32,40},{40,48},{48,56},{56,64},{64,7... | collective-permute-start | bytes 1572872 | tf_op jit(solution)/shard_map/ppermute | solution.py:18
  80.0 9.5 %copy-start.6 = (bf16[1,1024,64]{1,2,0:T(8,128)(2,1)S(1)}, bf16[1,1024,64]{1,2,0:T(8,128)(2,1)}, u32[]{:S(2)}) copy-start(bf16[1,1024,64]{1,2,0:T(8,128)(2,1)} %copy-done.5) | copy-start | bytes 393220
  82.6 0.9 copy-start.2
  82.6 2.2 copy-start.4
  100.2 8.1 %copy-start.9 = (f32[2,512,1,3]{1,0,3,2:T(2,128)S(1)}, f32[2,512,1,3]{1,0,3,2:T(2,128)}, u32[]{:S(2)}) copy-start(f32[2,512,1,3]{1,0,3,2:T(2,128)} %get-tuple-element.335) | copy-start | bytes 36868 | tf_op jit(solution)/shard_map/while
  108.4 7.3 %copy-start.10 = (f32[2,512,1,3]{1,0,3,2:T(2,128)}, f32[2,512,1,3]{1,0,3,2:T(2,128)S(1)}, u32[]{:S(2)}) copy-start(f32[2,512,1,3]{1,0,3,2:T(2,128)S(1)} %dynamic_update_slice.16) | copy-start | bytes 36868 | tf_op jit(solution)/shard_map/while
  108.4 7.3 %copy-start.12 = (f32[2,512,1,3]{1,0,2,3:T(2,128)S(1)}, f32[2,512,1,3]{1,0,2,3:T(2,128)}, u32[]{:S(2)}) copy-start(f32[2,512,1,3]{1,0,2,3:T(2,128)} %get-tuple-element.336) | copy-start | bytes 36868 | tf_op jit(solution)/shard_map/while
  115.8 10.4 %copy-start.13 = (f32[2,512,1,3]{1,0,2,3:T(2,128)}, f32[2,512,1,3]{1,0,2,3:T(2,128)S(1)}, u32[]{:S(2)}) copy-start(f32[2,512,1,3]{1,0,2,3:T(2,128)S(1)} %dynamic_update_slice.17) | copy-start | bytes 36868 | tf_op jit(solution)/shard_map/while
  137.0 8.1 %copy-start.9 = (f32[2,512,1,3]{1,0,3,2:T(2,128)S(1)}, f32[2,512,1,3]{1,0,3,2:T(2,128)}, u32[]{:S(2)}) copy-start(f32[2,512,1,3]{1,0,3,2:T(2,128)} %get-tuple-element.335) | copy-start | bytes 36868 | tf_op jit(solution)/shard_map/while
  145.2 7.6 %copy-start.10 = (f32[2,512,1,3]{1,0,3,2:T(2,128)}, f32[2,512,1,3]{1,0,3,2:T(2,128)S(1)}, u32[]{:S(2)}) copy-start(f32[2,512,1,3]{1,0,3,2:T(2,128)S(1)} %dynamic_update_slice.16) | copy-start | bytes 36868 | tf_op jit(solution)/shard_map/while
  145.2 7.6 %copy-start.12 = (f32[2,512,1,3]{1,0,2,3:T(2,128)S(1)}, f32[2,512,1,3]{1,0,2,3:T(2,128)}, u32[]{:S(2)}) copy-start(f32[2,512,1,3]{1,0,2,3:T(2,128)} %get-tuple-element.336) | copy-start | bytes 36868 | tf_op jit(solution)/shard_map/while
  152.9 9.6 %copy-start.13 = (f32[2,512,1,3]{1,0,2,3:T(2,128)}, f32[2,512,1,3]{1,0,2,3:T(2,128)S(1)}, u32[]{:S(2)}) copy-start(f32[2,512,1,3]{1,0,2,3:T(2,128)S(1)} %dynamic_update_slice.17) | copy-start | bytes 36868 | tf_op jit(solution)/shard_map/while
  164.9 5.8 %copy-start.14 = (f32[2,512,1,3]{1,0,2,3:T(2,128)S(1)}, f32[2,512,1,3]{1,0,2,3:T(2,128)}, u32[]{:S(2)}) copy-start(f32[2,512,1,3]{1,0,2,3:T(2,128)} %get-tuple-element.91) | copy-start | bytes 36868
  164.9 5.8 %copy-start.11 = (f32[2,512,1,3]{1,0,3,2:T(2,128)S(1)}, f32[2,512,1,3]{1,0,3,2:T(2,128)}, u32[]{:S(2)}) copy-start(f32[2,512,1,3]{1,0,3,2:T(2,128)} %get-tuple-element.90) | copy-start | bytes 36868
  164.9 39.9 %copy-start.3 = (bf16[1024,3,64]{2,0,1:T(8,128)(2,1)S(1)}, bf16[1024,3,64]{2,0,1:T(8,128)(2,1)}, u32[]{:S(2)}) copy-start(bf16[1024,3,64]{2,0,1:T(8,128)(2,1)} %copy-done.2) | copy-start | bytes 1179652
Sparse Core Ops, SparseCore 0:
  10.5 47.6 all-gather.2
  60.8 143.8 all-gather.4
  249.8 41.9 reduce-scatter.1
where the time goes:
time: 299 us; the launch traced here: 298 us
  waiting for transfers between devices  111 us (37%)
  matrix products  78.4 us (26%)
  other arithmetic  49.5 us (17%)
  local copies, waits for them, and re-layouts  31.9 us (11%)
  between operations  13.4 us (4%)
  starting transfers between devices  12 us (4%)
    reduce_scatter x1, waiting for transfers between devices, on_device(): lax.psum_scatter(jnp.dot(attended, w_out, preferred_element_type=jnp.floa...  42.1 us
    dot_general x3, matrix products, finish_state(): jnp.einsum('bgpn,ngh->bgph', weights.astype(jnp.bfloat16), values, prefer...  34.4 us
    all_gather x1, waiting for transfers between devices, on_device(): piece = lax.all_gather(long_cache, 'seq', axis=1, tiled=True)  33.9 us
    all_gather x1, waiting for transfers between devices, on_device(): piece = lax.all_gather(normed, 'head', axis=0, tiled=True)  30.1 us
    dot_general x3, matrix products, raw_scores(): jnp.einsum('bgph,ngh->bgpn', queries, keys, preferred_element_type=jnp.fl...  28.4 us
    reduce_sum x3, other arithmetic, finish_state(): summed = jnp.sum(weights, axis=-1)  25.5 us
    ppermute x3, starting transfers between devices, from_behind(): return lax.ppermute(block, axis, route)  11.9 us
  transfers between devices with their start and end apart: 6, of which 4 were waited for; matrix products, arithmetic and copies ran while one was open for 37% of the time, Pallas kernels for 0%

commit v1 on v0

v1 whole, which is shorter than its diff:
```python
import math

import jax
import jax.numpy as jnp
from jax import lax
from jax.experimental import pallas as pl
from jax.experimental.pallas import tpu as pltpu
from jax.sharding import PartitionSpec as P

HD = 128
LEAD = 64
THETA_LOG = math.log(500000.0)
SCALE = 1.0 / math.sqrt(HD)
LOW = -1e30
TILE = 256


def from_behind(block, axis, distance):
    devices = range(lax.axis_size(axis))
    route = [(i - distance, i) for i in devices if i - distance in devices]
    return lax.ppermute(block, axis, route)


def request_starts(new_len):
    return LEAD + jnp.cumsum(new_len) - new_len


def token_facts(token_index, starts, cache_len, long_len):
    number = starts.shape[0]
    passed = (starts[None, :] <= token_index[:, None]).astype(jnp.int32)
    request = jnp.sum(passed, axis=1) - 1
    select = jnp.arange(number, dtype=jnp.int32)[None, :] == request[:, None]
    begin = jnp.sum(jnp.where(select, starts[None, :], 0), axis=1)
    cached = jnp.sum(jnp.where(select, cache_len[None, :], 0), axis=1)
    lead = request < 0
    position = jnp.where(lead, token_index + long_len, token_index - begin + cached)
    return jnp.where(lead, number, request), begin, position


def normalize(tokens, norm_gain):
    values = tokens.astype(jnp.float32)
    mean_square = jnp.mean(values * values, axis=-1, keepdims=True)
    return (values * lax.rsqrt(mean_square + 1e-05) * norm_gain).astype(jnp.bfloat16)


def rotate_tables(position):
    half = HD // 2
    frequency = jnp.exp(jnp.arange(half, dtype=jnp.float32) * (-2.0 * THETA_LOG / HD))
    angle = position.astype(jnp.float32)[:, None] * frequency[None, :]
    cosine = jnp.cos(angle)
    sine = jnp.sin(angle)
    return (
        jnp.concatenate([cosine, cosine], axis=1),
        jnp.concatenate([-sine, sine], axis=1),
    )


def dot32(a, b):
    return jnp.dot(a, b, preferred_element_type=jnp.float32)


def dot_t(a, b):
    return lax.dot_general(a, b, (((1,), (1,)), ((), ())), preferred_element_type=jnp.float32)


def kv_kernel(x_ref, wk_ref, wv_ref, cos_ref, sin_ref, kv_ref):
    x = x_ref[...]
    key = dot32(x, wk_ref[...])
    kv_ref[0] = (key * cos_ref[...] + pltpu.roll(key, HD // 2, 1) * sin_ref[...]).astype(jnp.bfloat16)
    kv_ref[1] = dot32(x, wv_ref[...]).astype(jnp.bfloat16)


def q_kernel(x_ref, wq_ref, cos_ref, sin_ref, q_ref):
    product = dot32(x_ref[...], wq_ref[...])
    cosine = cos_ref[...]
    sine = sin_ref[...]
    for head in range(q_ref.shape[0]):
        query = product[:, head * HD : (head + 1) * HD]
        q_ref[head] = (query * cosine + pltpu.roll(query, HD // 2, 1) * sine).astype(jnp.bfloat16)


def project_kv(x, w_key, w_value, cosine, sine):
    rows, width = x.shape
    tile = TILE
    return pl.pallas_call(
        kv_kernel,
        grid=(rows // tile,),
        in_specs=[
            pl.BlockSpec((tile, width), lambda i: (i, 0)),
            pl.BlockSpec(w_key.shape, lambda i: (0, 0)),
            pl.BlockSpec(w_value.shape, lambda i: (0, 0)),
            pl.BlockSpec((tile, HD), lambda i: (i, 0)),
            pl.BlockSpec((tile, HD), lambda i: (i, 0)),
        ],
        out_specs=pl.BlockSpec((2, tile, HD), lambda i: (0, i, 0)),
        out_shape=jax.ShapeDtypeStruct((2, rows, HD), jnp.bfloat16),
        cost_estimate=pl.CostEstimate(
            flops=4 * rows * width * HD, bytes_accessed=rows * width * 2, transcendentals=0
        ),
        name="project_kv",
    )(x, w_key, w_value, cosine, sine)


def project_q(x, w_query, cosine, sine):
    rows, width = x.shape
    heads = w_query.shape[1] // HD
    tile = TILE
    return pl.pallas_call(
        q_kernel,
        grid=(rows // tile,),
        in_specs=[
            pl.BlockSpec((tile, width), lambda i: (i, 0)),
            pl.BlockSpec(w_query.shape, lambda i: (0, 0)),
            pl.BlockSpec((tile, HD), lambda i: (i, 0)),
            pl.BlockSpec((tile, HD), lambda i: (i, 0)),
        ],
        out_specs=pl.BlockSpec((heads, tile, HD), lambda i: (0, i, 0)),
        out_shape=jax.ShapeDtypeStruct((heads, rows, HD), jnp.bfloat16),
        cost_estimate=pl.CostEstimate(
            flops=2 * heads * rows * width * HD, bytes_accessed=rows * width * 2, transcendentals=0
        ),
        name="project_q",
    )(x, w_query, cosine, sine)


def local_kernel(
    first_ref,
    q_ref,
    before_ref,
    here_ref,
    slot_before_ref,
    slot_here_ref,
    owner_ref,
    facts_ref,
    out_ref,
    lead_mix_ref,
    lead_top_ref,
    lead_sum_ref,
    window,
    top_ref,
    sum_ref,
    mix_ref,
):
    step = pl.program_id(0)
    rows = here_ref.shape[1]
    slots = slot_here_ref.shape[1]
    heads, tile, _ = q_ref.shape

    @pl.when(step == 0)
    def _():
        window[:, pl.ds(0, rows)] = before_ref[...]
        window[:, pl.ds(rows, rows)] = here_ref[...]
        window[:, pl.ds(2 * rows, slots)] = slot_before_ref[...]
        window[:, pl.ds(2 * rows + slots, slots)] = slot_here_ref[...]

    request = facts_ref[:, 0:1]
    begin = facts_ref[:, 1:2]
    index = facts_ref[:, 2:3]

    def take(keys, values, valid, fresh):
        for head in range(heads):
            scores = jnp.where(valid, dot_t(q_ref[head], keys) * SCALE, LOW)
            top = jnp.max(scores, axis=1, keepdims=True)
            if not fresh:
                old = top_ref[head]
                top = jnp.maximum(top, old)
                keep = jnp.exp(old - top)
            weights = jnp.exp(scores - top)
            total = jnp.sum(weights, axis=1, keepdims=True)
            mixed = dot32(weights.astype(jnp.bfloat16), values)
            top_ref[head] = top
            if fresh:
                sum_ref[head] = total
                mix_ref[head] = mixed
            else:
                sum_ref[head] = sum_ref[head] * keep + total
                mix_ref[head] = mix_ref[head] * keep + mixed

    def new_chunk(number, fresh):
        at = pl.multiple_of(number * tile, tile)
        key_at = at + lax.broadcasted_iota(jnp.int32, (tile, tile), 1)
        valid = (key_at >= begin) & (key_at <= index)
        take(window[0, pl.ds(at, tile), :], window[1, pl.ds(at, tile), :], valid, fresh)

    last = rows // tile + step
    new_chunk(last, True)
    first = first_ref[step]

    @pl.loop(first, last)
    def _(number):
        new_chunk(number, False)

    valid = owner_ref[...] == request
    take(window[0, pl.ds(2 * rows, 2 * slots), :], window[1, pl.ds(2 * rows, 2 * slots), :], valid, False)
    for head in range(heads):
        out_ref[:, head * HD : (head + 1) * HD] = (mix_ref[head] / sum_ref[head]).astype(jnp.bfloat16)

    @pl.when(step == 0)
    def _():
        lead_mix_ref[...] = mix_ref[:, pl.ds(0, LEAD), :]
        lead_top_ref[...] = jnp.broadcast_to(top_ref[:, pl.ds(0, LEAD), :], lead_top_ref.shape)
        lead_sum_ref[...] = jnp.broadcast_to(sum_ref[:, pl.ds(0, LEAD), :], lead_sum_ref.shape)


def local_attention(first, queries, before, here, slot_before, slot_here, owner, facts):
    heads, rows, _ = queries.shape
    slots = slot_here.shape[1]
    tile = TILE

    def whole(array):
        return pl.BlockSpec(array.shape, lambda i, first: (0,) * array.ndim)

    lead_shape = jax.ShapeDtypeStruct((heads, LEAD, HD), jnp.float32)
    return pl.pallas_call(
        local_kernel,
        grid_spec=pltpu.PrefetchScalarGridSpec(
            num_scalar_prefetch=1,
            grid=(rows // tile,),
            in_specs=[
                pl.BlockSpec((heads, tile, HD), lambda i, first: (0, i, 0)),
                whole(before),
                whole(here),
                whole(slot_before),
                whole(slot_here),
                whole(owner),
                pl.BlockSpec((tile, facts.shape[1]), lambda i, first: (i, 0)),
            ],
            out_specs=[
                pl.BlockSpec((tile, heads * HD), lambda i, first: (i, 0)),
                whole(lead_shape),
                whole(lead_shape),
                whole(lead_shape),
            ],
            scratch_shapes=[
                pltpu.VMEM((2, 2 * rows + 2 * slots, HD), jnp.bfloat16),
                pltpu.VMEM((heads, tile, 1), jnp.float32),
                pltpu.VMEM((heads, tile, 1), jnp.float32),
                pltpu.VMEM((heads, tile, HD), jnp.float32),
            ],
        ),
        out_shape=[
            jax.ShapeDtypeStruct((rows, heads * HD), jnp.bfloat16),
            lead_shape,
            lead_shape,
            lead_shape,
        ],
        cost_estimate=pl.CostEstimate(
            flops=4 * heads * rows * (rows + 2 * slots) * HD,
            bytes_accessed=8 * rows * HD * heads,
            transcendentals=heads * rows * (rows + 2 * slots),
        ),
        name="local_attention",
    )(first, queries, before, here, slot_before, slot_here, owner, facts)


def long_kernel(q_ref, cache_ref, mix_ref, top_ref, sum_ref):
    for head in range(q_ref.shape[0]):
        scores = dot_t(q_ref[head], cache_ref[0]) * SCALE
        top = jnp.max(scores, axis=1, keepdims=True)
        weights = jnp.exp(scores - top)
        mix_ref[head] = dot32(weights.astype(jnp.bfloat16), cache_ref[1])
        top_ref[head] = jnp.broadcast_to(top, top_ref.shape[1:])
        sum_ref[head] = jnp.broadcast_to(jnp.sum(weights, axis=1, keepdims=True), sum_ref.shape[1:])


def long_part(lead_queries, cache):
    shape = jax.ShapeDtypeStruct(lead_queries.shape, jnp.float32)
    return pl.pallas_call(
        long_kernel,
        out_shape=[shape, shape, shape],
        cost_estimate=pl.CostEstimate(
            flops=4 * 192 * cache.shape[1] * HD, bytes_accessed=cache.size * 2, transcendentals=192 * 1024
        ),
        name="long_part",
    )(lead_queries, cache)


def on_device(
    tokens,
    norm_gain,
    w_query,
    w_key,
    w_value,
    w_out,
    long_cache,
    short_cache,
    slot_owner,
    new_len,
    cache_len,
):
    seq_index = lax.axis_index("seq")
    long_len = long_cache.shape[1] * lax.axis_size("seq")
    heads = w_query.shape[1] // HD
    earlier_slots, earlier_owner = from_behind((short_cache, slot_owner), "seq", 1)
    normed = normalize(tokens, norm_gain)
    piece = lax.all_gather(normed, "head", axis=0, tiled=True)
    rows = piece.shape[0]
    starts = request_starts(new_len)
    token_index = seq_index * rows + jnp.arange(rows, dtype=jnp.int32)
    request, begin, position = token_facts(token_index, starts, cache_len, long_len)
    cosine, sine = rotate_tables(position)
    here = project_kv(piece, w_key, w_value, cosine, sine)
    before = from_behind(here, "seq", 1)
    queries = project_q(piece, w_query, cosine, sine)

    lead_queries = queries[:, :LEAD]
    lead_queries = lax.psum(jnp.where(seq_index == 0, lead_queries, jnp.zeros_like(lead_queries)), "seq")
    long_mix, long_top, long_sum = long_part(lead_queries, long_cache)
    long_high = lax.pmax(long_top[:, :, 0], "seq")
    shrink = jnp.exp(long_top[:, :, 0] - long_high)
    packed = jnp.concatenate(
        [long_mix * shrink[..., None], jnp.tile((long_sum[:, :, 0] * shrink)[:, None, :], (1, 1, HD // LEAD))],
        axis=1,
    )
    packed = lax.psum(packed, "seq")
    long_mix = packed[:, :LEAD]
    long_sum = packed[:, LEAD, :LEAD]

    shift = (seq_index - 1) * rows
    window_begin = jnp.maximum(begin - shift, 0)
    window_index = token_index - shift
    window_begin = jnp.where(request == starts.shape[0], -shift, window_begin)
    facts = jnp.stack([request, window_begin, window_index] + [window_index] * 5, axis=1)
    owner = jnp.concatenate([jnp.where(seq_index > 0, earlier_owner, -1), slot_owner])[None, :]
    first = window_begin[::TILE] // TILE
    attended, lead_mix, lead_top, lead_sum = local_attention(
        first, queries, before, here, earlier_slots, short_cache, owner, facts
    )
    lead_top = lead_top[:, :, 0]
    lead_sum = lead_sum[:, :, 0]
    highest = jnp.maximum(lead_top, long_high)
    scale_near = jnp.exp(lead_top - highest)
    scale_long = jnp.exp(long_high - highest)
    total = lead_sum * scale_near + long_sum * scale_long
    mixture = lead_mix * scale_near[..., None] + long_mix * scale_long[..., None]
    lead_out = (mixture / total[..., None]).astype(jnp.bfloat16)
    lead_out = jnp.transpose(lead_out, (1, 0, 2)).reshape(LEAD, heads * HD)
    lead_out = jnp.where(seq_index == 0, lead_out, attended[:LEAD])
    attended = lax.dynamic_update_slice(attended, lead_out, (0, 0))
    return lax.psum_scatter(
        dot32(attended, w_out).astype(jnp.bfloat16), "head", scatter_dimension=0, tiled=True
    )


def solution(mesh):
    placed = (
        P(("seq", "head"), None),
        P(),
        P(None, "head"),
        P(None, "head"),
        P(None, "head"),
        P("head", None),
        P(None, "seq", "head"),
        P(None, "seq", "head"),
        P("seq"),
        P(),
        P(),
    )
    return jax.shard_map(
        on_device, mesh=mesh, in_specs=placed, out_specs=P(("seq", "head"), None), check_vma=False
    )
```

time: 299 us -> 520 us (1.74)
  blocking collectives: 0 us -> 172 us
  waiting for transfers between devices: 111 us -> 260 us
  matrix products: 78.4 us -> 6.41 us
  other arithmetic: 49.5 us -> 12 us
  Pallas kernels: 0 us -> 36.8 us
  local copies, waits for them, and re-layouts: 31.9 us -> 6.95 us
    psum x0 -> x1, waiting for transfers between devices: none -> 170 us  [on_device(): packed = lax.psum(packed, 'seq')]
    psum x0 -> x1, blocking collectives: none -> 116 us  [on_device(): lax.psum(jnp.where(seq_index == 0, lead_queries, jnp.zeros_like(lead_quer...]
    dot_general x10 -> x1, matrix products: 78.4 us -> 6.41 us  [dot32(): return jnp.dot(a, b, preferred_element_type=jnp.float32)]
    pmax x0 -> x1, blocking collectives: none -> 56.1 us  [on_device(): long_high = lax.pmax(long_top[:, :, 0], 'seq')]
    pallas_call x0 -> x4, Pallas kernels: none -> 36.8 us  [the longest x1 18.8 us: local_attention(): pl.pallas_call(local_kernel, grid_spec=pltpu.PrefetchScalarGridSpec(num_s...]
    all_gather x1 -> x0, waiting for transfers between devices: 33.9 us -> none  [on_device(): piece = lax.all_gather(long_cache, 'seq', axis=1, tiled=True)]
    reduce_sum x5 -> x2, other arithmetic: 26.4 us -> 0.22 us  [the longest x1 0.12 us: token_facts(): cached = jnp.sum(jnp.where(select, cache_len[None, :], 0), axis=1)]
    reduce_scatter x1, waiting for transfers between devices: 42.1 us -> 55.8 us  [on_device(): lax.psum_scatter(dot32(attended, w_out).astype(jnp.bfloat16), 'head', sca...]
  transfers between devices with their start and end apart: 6 -> 6, of which waited for: 4 -> 3; matrix products, arithmetic and copies ran while one was open for 37% -> 2% of each run, Pallas kernels for 0% -> 3%
where the time goes in v1:
time: 520 us; the launch traced here: 519 us
  waiting for transfers between devices  260 us (50%)
  blocking collectives  172 us (33%)
  Pallas kernels  36.8 us (7%)
  between operations  13.4 us (3%)
  other arithmetic  12 us (2%)
  starting transfers between devices  11.7 us (2%)
  local copies, waits for them, and re-layouts  6.95 us (1%)
  matrix products  6.41 us (1%)
    psum x1, waiting for transfers between devices, on_device(): packed = lax.psum(packed, 'seq')  170 us
    psum x1, blocking collectives, on_device(): lax.psum(jnp.where(seq_index == 0, lead_queries, jnp.zeros_like(lead_quer...  116 us
    pmax x1, blocking collectives, on_device(): long_high = lax.pmax(long_top[:, :, 0], 'seq')  56.1 us
    reduce_scatter x1, waiting for transfers between devices, on_device(): lax.psum_scatter(dot32(attended, w_out).astype(jnp.bfloat16), 'head', sca...  55.8 us
    all_gather x1, waiting for transfers between devices, on_device(): piece = lax.all_gather(normed, 'head', axis=0, tiled=True)  34.2 us
    pallas_call x1, Pallas kernels, local_attention(): pl.pallas_call(local_kernel, grid_spec=pltpu.PrefetchScalarGridSpec(num_s...  18.8 us
    ppermute x3, starting transfers between devices, from_behind(): return lax.ppermute(block, axis, route)  11.4 us
  transfers between devices with their start and end apart: 6, of which 3 were waited for; matrix products, arithmetic and copies ran while one was open for 2% of the time, Pallas kernels for 3%

profile of v1, /device:TPU:1, one launch (start us, length us, event | category | flops | bytes accessed | tf_op | source)
XLA Modules:
  0.0 518.9 jit_solution(4418710062831646515)
XLA Ops:
  6.6 1.5 fusion
  8.1 2.3 fusion.2
  10.5 4.4 collective-permute-start.2
  14.9 3.6 collective-permute-start.1
  18.9 0.1 select_reduce_fusion
  19.2 1.9 fusion.3
  21.1 1.3 pad_maximum_fusion
  22.4 0.6 and_select_fusion.first_ref
  23.1 1.0 copy.49.facts_ref
  24.1 34.2 %all-gather.2.cloned.1.call-done.x_ref = bf16[1024,3072]{1,0:T(8,128)(2,1)} async-done(((bf16[128,3072]{1,0:T(8,128)(2,1)}), bf16[1024,3072]{1,0:T(8,128)(2,1)}) %all-gather.2.cloned.1.call-update) | async-done | bytes 6291472 | tf_op jit(solution)/shard_map/all_gather | solution.py:296
  58.3 7.9 %project_q.1.q_ref = bf16[3,1024,128]{2,1,0:T(8,128)(2,1)} custom-call(bf16[1024,3072]{1,0:T(8,128)(2,1)} %all-gather.2.cloned.1.call-done.x_ref, bf16[3072,384]{1,0:T(8,128)(2,1)} %wq_ref.1, f32[1024,128]{1,0:T(8,128)} %get-tuple-element.34.cos_ref, f32[1024,128]{1,0:T(8,128)} %get-tuple-element.35.sin_ref), custom_call_target="tpu_custom_call" | custom-call | flops 2415919104 | bytes 6291456 | tf_op jit(solution)/shard_map/project_q/pallas_call | solution.py:108
  66.2 0.8 slice_select_fusion
  67.0 115.8 %psum.14.q_ref = bf16[3,64,128]{2,1,0:T(8,128)(2,1)} all-reduce(bf16[3,64,128]{2,1,0:T(8,128)(2,1)S(1)} %slice_select_fusion), channel_id=1, replica_groups=mesh['seq'=32,'head'=8] {'seq'}, use_global_device_ids=true, to_apply=%region_5.6 | all-reduce | flops 24576 | bytes 98304 | tf_op jit(solution)/shard_map/psum | solution.py:307
  182.8 2.8 long_part.1
  185.6 1.0 slice_reduce_fusion.1
  186.6 56.1 %pmax.7 = f32[3,64]{1,0:T(4,128)S(1)} all-reduce(f32[3,64]{1,0:T(4,128)S(1)} %slice_reduce_fusion.1), channel_id=1, replica_groups=mesh['seq'=32,'head'=8] {'seq'}, use_global_device_ids=true, to_apply=%region_6.7 | all-reduce | flops 192 | bytes 1536 | tf_op jit(solution)/shard_map/pmax | solution.py:309
  242.7 1.0 slice_reduce_fusion
  243.7 7.3 %project_kv.1.here_ref = bf16[2,1024,128]{2,1,0:T(8,128)(2,1)} custom-call(bf16[1024,3072]{1,0:T(8,128)(2,1)} %all-gather.2.cloned.1.call-done.x_ref, bf16[3072,128]{1,0:T(8,128)(2,1)} %wk_ref.1, bf16[3072,128]{1,0:T(8,128)(2,1)} %wv_ref.1, f32[1024,128]{1,0:T(8,128)} %get-tuple-element.34.cos_ref, f32[1024,128]{1,0:T(8,128)} %get-tuple-element.35.sin_ref), custom_call_target="tpu_custom_call" | custom-call | flops 1610612736 | bytes 6291456 | tf_op jit(solution)/shard_map/project_kv/pallas_call | solution.py:85
  251.0 3.5 collective-permute-start
  254.7 0.7 pad_maximum_fusion.2
  255.4 0.2 reduce-scatter.2.cloned.1.call-start
  255.6 0.6 pad_add_fusion
  256.2 169.7 %all-reduce.2.cloned.1.call-done = f32[3,65,128]{2,1,0:T(8,128)} async-done(((f32[3,65,128]{2,1,0:T(8,128)}), f32[3,65,128]{2,1,0:T(8,128)}) %all-reduce.2.cloned.1.call-update) | async-done | bytes 99856 | tf_op jit(solution)/shard_map/psum | solution.py:315
  425.9 0.7 slice.41
  426.7 0.6 copy-done.8
  427.3 0.2 copy-done.6
  427.5 18.8 %local_attention.1 = (bf16[1024,384]{1,0:T(8,128)(2,1)}, f32[3,64,128]{2,1,0:T(8,128)}, f32[3,64,128]{2,1,0:T(8,128)}, f32[3,64,128]{2,1,0:T(8,128)}) custom-call(s32[4]{0:T(128)} %and_select_fusion.first_ref, bf16[3,1024,128]{2,1,0:T(8,128)(2,1)} %project_q.1.q_ref, bf16[2,1024,128]{2,1,0:T(8,128)(2,1)} %copy-done.6, ...), custom_call_target="tpu_custom_call" | custom-call | flops 2415919104 | bytes 3145728 | tf_op jit(solution)/shard_map/local_attention/pallas_call | solution.py:214
  446.3 1.0 copy.50
  447.4 1.0 copy.52
  448.4 1.7 fusion.7
  450.1 6.4 %convolution_convert_fusion = bf16[1024,3072]{1,0:T(8,128)(2,1)} fusion(bf16[1024,384]{1,0:T(8,128)(2,1)} %fusion.7, bf16[384,3072]{1,0:T(8,128)(2,1)S(1)} %copy-done), kind=kOutput, calls=%fused_computation | convolution fusion | flops 2419064832 | bytes 9437184 | tf_op jit(solution)/shard_map/dot_general | solution.py:59
  456.6 55.8 %reduce-scatter.2.cloned.1.call-done = bf16[128,3072]{1,0:T(8,128)(2,1)} async-done(((bf16[1024,3072]{1,0:T(8,128)(2,1)}), bf16[128,3072]{1,0:T(8,128)(2,1)}) %reduce-scatter.2.cloned.1.call-update) | async-done | bytes 786448 | tf_op jit(solution)/shard_map/reduce_scatter | solution.py:340
  (44 shorter events, 1.0 us)
Async XLA Ops:
  6.5 443.6 %copy-start = (bf16[384,3072]{1,0:T(8,128)(2,1)S(1)}, bf16[384,3072]{1,0:T(8,128)(2,1)}, u32[]{:S(2)}) copy-start(bf16[384,3072]{1,0:T(8,128)(2,1)} %param.16) | copy-start | bytes 7077892
  6.5 4.0 copy-start.3
  6.5 8.3 %copy-start.7 = (bf16[2,256,128]{2,1,0:T(8,128)(2,1)S(1)}, bf16[2,256,128]{2,1,0:T(8,128)(2,1)}, u32[]{:S(2)}) copy-start(bf16[2,256,128]{2,1,0:T(8,128)(2,1)} %slot_here_ref.1) | copy-start | bytes 393220
  6.5 11.9 %copy-start.4 = (s32[64]{0:T(128)S(1)}, s32[64]{0:T(128)}, u32[]{:S(2)}) copy-start(s32[64]{0:T(128)} %param.20) | copy-start | bytes 772
  6.5 12.4 %copy-start.5 = (s32[64]{0:T(128)S(1)}, s32[64]{0:T(128)}, u32[]{:S(2)}) copy-start(s32[64]{0:T(128)} %param.21) | copy-start | bytes 772
  6.5 51.8 %all-gather.2.cloned.1.call-start = ((), (), s32[]{:S(2)}) async-start(), calls=%async_computation.1 | async-start | bytes 7077888 | tf_op jit(solution)/shard_map/all_gather | solution.py:296
  10.4 415.5 %all-reduce.2.cloned.1.call-start = ((), (), s32[]{:S(2)}) async-start(), calls=%async_computation.2 | async-start | bytes 221184 | tf_op jit(solution)/shard_map/psum | solution.py:315
  10.5 13.6 %collective-permute-start.2 = (s32[256]{0:T(256)S(1)}, s32[256]{0:T(256)S(1)}, u32[]{:S(2)}, u32[]{:S(2)}) collective-permute-start(s32[256]{0:T(256)S(1)} %copy-done.3), channel_id=1, source_target_pairs={{0,8},{8,16},{16,24},{24,32},{32,40},{40,48},{48,56},{56,64},{64,7... | collective-permute-start | bytes 3080 | tf_op jit(solution)/shard_map/ppermute | solution.py:21
  14.9 411.8 %collective-permute-start.1 = (bf16[2,256,128]{2,1,0:T(8,128)(2,1)S(1)}, bf16[2,256,128]{2,1,0:T(8,128)(2,1)S(1)}, u32[]{:S(2)}, u32[]{:S(2)}) collective-permute-start(bf16[2,256,128]{2,1,0:T(8,128)(2,1)S(1)} %copy-done.7), channel_id=1, source_target_pairs={{0,8},{8,16},{16,24},{24,32},{32,40},{40,48},{48,56},{56,64},{64,7... | collective-permute-start | bytes 393224 | tf_op jit(solution)/shard_map/ppermute | solution.py:21
  243.7 10.9 %copy-start.1 = (f32[3,64,128]{2,1,0:T(8,128)S(1)}, f32[3,64,128]{2,1,0:T(8,128)}, u32[]{:S(2)}) copy-start(f32[3,64,128]{2,1,0:T(8,128)} %get-tuple-element.16) | copy-start | bytes 294916
  251.0 175.7 %collective-permute-start = (bf16[2,1024,128]{2,1,0:T(8,128)(2,1)}, bf16[2,1024,128]{2,1,0:T(8,128)(2,1)S(1)}, u32[]{:S(2)}, u32[]{:S(2)}) collective-permute-start(bf16[2,1024,128]{2,1,0:T(8,128)(2,1)} %project_kv.1.here_ref), channel_id=1, source_target_pairs={{0,8},{8,16},{16,24},{24,32},{32,40},{40,48},{48,56},{56,64},{64,7... | collective-permute-start | bytes 1572872 | tf_op jit(solution)/shard_map/ppermute | solution.py:21
  255.4 257.0 %reduce-scatter.2.cloned.1.call-start = ((), (), s32[]{:S(2)}) async-start(), calls=%async_computation.3 | async-start | bytes 7077888 | tf_op jit(solution)/shard_map/reduce_scatter | solution.py:340
  426.7 0.6 copy-start.8
  426.7 0.8 copy-start.6
  427.5 20.9 %copy-start.2 = (f32[3,65,128]{2,1,0:T(8,128)S(1)}, f32[3,65,128]{2,1,0:T(8,128)}, u32[]{:S(2)}) copy-start(f32[3,65,128]{2,1,0:T(8,128)} %all-reduce.2.cloned.1.call-done) | copy-start | bytes 299524
Sparse Core Ops, SparseCore 0:
  10.6 47.6 all-gather.1
  255.5 170.3 all-reduce.1
  456.7 55.6 reduce-scatter.1

commit v2 on v1

--- a/solution.py
+++ b/solution.py
@@ -63,64 +63,346 @@
     return lax.dot_general(a, b, (((1,), (1,)), ((), ())), preferred_element_type=jnp.float32)
 
 
-def kv_kernel(x_ref, wk_ref, wv_ref, cos_ref, sin_ref, kv_ref):
-    x = x_ref[...]
-    key = dot32(x, wk_ref[...])
-    kv_ref[0] = (key * cos_ref[...] + pltpu.roll(key, HD // 2, 1) * sin_ref[...]).astype(jnp.bfloat16)
-    kv_ref[1] = dot32(x, wv_ref[...]).astype(jnp.bfloat16)
-
-
-def q_kernel(x_ref, wq_ref, cos_ref, sin_ref, q_ref):
-    product = dot32(x_ref[...], wq_ref[...])
-    cosine = cos_ref[...]
-    sine = sin_ref[...]
-    for head in range(q_ref.shape[0]):
-        query = product[:, head * HD : (head + 1) * HD]
-        q_ref[head] = (query * cosine + pltpu.roll(query, HD // 2, 1) * sine).astype(jnp.bfloat16)
-
-
-def project_kv(x, w_key, w_value, cosine, sine):
-    rows, width = x.shape
-    tile = TILE
+MESH = pl.DeviceIdType.MESH
+LIMIT = 60 * 1024 * 1024
+Z = 8
+Y = 4
+UNITS = [(0, 0), (0, 1), (1, 0), (3, 0), (1, 1), (2, 0), (2, 1), (3, 1)]
+SLOT = {unit: number for number, unit in enumerate(UNITS)}
+
+
+def place():
+    seq = lax.axis_index("seq")
+    head = lax.axis_index("head")
+    return seq, head, head // 2, lax.rem(head, 2)
+
+
+def pick(number, table):
+    value = jnp.int32(table[0])
+    for at, entry in enumerate(table):
+        value = jnp.where(number == at, jnp.int32(entry), value)
+    return value
+
+
+def greet(device):
+    pl.semaphore_signal(
+        pltpu.get_barrier_semaphore(), inc=1, device_id=device, device_id_type=MESH
+    )
+
+
+def gather_kernel(
+    normed_ref,
+    wq_ref,
+    wk_ref,
+    wv_ref,
+    cos_ref,
+    sin_ref,
+    slots_ref,
+    owner_ref,
+    q_ref,
+    kv_ref,
+    before_ref,
+    slots_before_ref,
+    owner_before_ref,
+    lead_ref,
+    held,
+    ring_send,
+    ring_recv,
+    pair_send,
+    pair_recv,
+    kv_send,
+    kv_recv,
+    slot_send,
+    slot_recv,
+    lead_send,
+    lead_recv,
+):
+    seq, head, y, core = place()
+    n_seq = lax.axis_size("seq")
+    x, z = seq // Z, lax.rem(seq, Z)
+    way = 1 - 2 * core
+    right = (seq, lax.rem(y + way + Y, Y) * 2 + core)
+    left = (seq, lax.rem(y - way + Y, Y) * 2 + core)
+    pair = (seq, head + way)
+    following = (lax.rem(seq + 1, n_seq), head)
+    previous = (lax.rem(seq + n_seq - 1, n_seq), head)
+    heads = q_ref.shape[0]
+    half = held.shape[2]
+
+    for device in (right, left, pair, following, previous):
+        greet(device)
+
+    @pl.when(seq == 0)
+    def _():
+        for to in range(1, Z):
+            greet((to, head))
+
+    @pl.when(x == 0)
+    def _():
+        for to in range(1, n_seq // Z):
+            greet((to * Z + z, head))
+
+    @pl.when((x == 0) & (z > 0))
+    def _():
+        greet((0, head))
+
+    @pl.when(x > 0)
+    def _():
+        greet((z, head))
+
+    barrier = pltpu.get_barrier_semaphore()
+    others = n_seq // Z - 1
+
+    @pl.when(seq == 0)
+    def _():
+        pl.semaphore_wait(barrier, 5 + Z - 1 + others)
+
+    @pl.when((x == 0) & (z > 0))
+    def _():
+        pl.semaphore_wait(barrier, 5 + 1 + others)
+
+    @pl.when(x > 0)
+    def _():
+        pl.semaphore_wait(barrier, 5 + 1)
+
+    def ring(number, source, to, unit):
+        slot = SLOT[unit]
+        return pltpu.make_async_remote_copy(
+            src_ref=source,
+            dst_ref=held.at[slot, core],
+            send_sem=ring_send.at[number],
+            recv_sem=ring_recv.at[slot],
+            device_id=to,
+            device_id_type=MESH,
+        )
+
+    def mine(unit):
+        return held.at[SLOT[unit], core]
+
+    def to_pair(unit):
+        slot = SLOT[unit]
+        return pltpu.make_async_remote_copy(
+            src_ref=normed_ref.at[unit[1]] if unit[0] == 0 else mine(unit),
+            dst_ref=held.at[slot, core],
+            send_sem=pair_send.at[slot],
+            recv_sem=pair_recv.at[slot],
+            device_id=pair,
+            device_id_type=MESH,
+        )
+
+    rings = [
+        ring(0, normed_ref.at[0], right, (1, 0)),
+        ring(1, normed_ref.at[0], left, (3, 0)),
+        ring(2, normed_ref.at[1], right, (1, 1)),
+        ring(3, mine((1, 0)), right, (2, 0)),
+        ring(4, mine((1, 1)), right, (2, 1)),
+        ring(5, mine((2, 1)), right, (3, 1)),
+    ]
+    pairs = {unit: to_pair(unit) for unit in UNITS}
+    side = [
+        pltpu.make_async_remote_copy(
+            src_ref=source,
+            dst_ref=target,
+            send_sem=slot_send.at[number],
+            recv_sem=slot_recv.at[number],
+            device_id=following,
+            device_id_type=MESH,
+        )
+        for number, (source, target) in enumerate(
+            [(slots_ref, slots_before_ref), (owner_ref, owner_before_ref)]
+        )
+    ]
+
+    def lead_copy(number, to):
+        return pltpu.make_async_remote_copy(
+            src_ref=lead_ref,
+            dst_ref=lead_ref,
+            send_sem=lead_send.at[number],
+            recv_sem=lead_recv,
+            device_id=(to, head),
+            device_id_type=MESH,
+        )
+
+    along_z = [lead_copy(to - 1, jnp.int32(to)) for to in range(1, Z)]
+    along_x = [lead_copy(Z - 2 + to, to * Z + z) for to in range(1, n_seq // Z)]
+
+    def row_starts(number):
+        distance = pick(number, [unit[0] for unit in UNITS])
+        later = pick(number, [unit[1] for unit in UNITS])
+        first = lax.rem(y - distance + Y, Y) * (4 * half) + later * half
+        second = lax.rem(y + distance, Y) * (4 * half) + 2 * half + later * half
+        return pl.multiple_of(first, half), pl.multiple_of(second, half)
+
+    def kv_copies(number):
+        return [
+            pltpu.make_async_remote_copy(
+                src_ref=kv_ref.at[:, pl.ds(start, half), :],
+                dst_ref=before_ref.at[:, pl.ds(start, half), :],
+                send_sem=kv_send.at[2 * number + part],
+                recv_sem=kv_recv.at[2 * number + part],
+                device_id=following,
+                device_id_type=MESH,
+            )
+            for part, start in enumerate(row_starts(number))
+        ]
+
+    rings[0].start()
+    pairs[(0, 0)].start()
+    rings[1].start()
+    rings[2].start()
+    pairs[(0, 1)].start()
+    for copy in side:
+        copy.start()
+    for later in range(2):
+        held[SLOT[(0, later)], core] = normed_ref[later]
+
+    def event_0():
+        pairs[(0, 0)].wait_recv()
+
+    def event_1():
+        pairs[(0, 1)].wait_recv()
+
+    def event_2():
+        rings[0].wait_recv()
+        rings[3].start()
+        pairs[(1, 0)].start()
+        pairs[(1, 0)].wait_recv()
+
+    def event_3():
+        rings[1].wait_recv()
+        pairs[(3, 0)].start()
+        rings[2].wait_recv()
+        rings[4].start()
+        pairs[(1, 1)].start()
+        pairs[(3, 0)].wait_recv()
+
+    def event_4():
+        pairs[(1, 1)].wait_recv()
+
+    def event_5():
+        rings[3].wait_recv()
+        pairs[(2, 0)].start()
+        pairs[(2, 0)].wait_recv()
+
+    def event_6():
+        @pl.when(seq == 0)
+        def _():
+            lead_ref[...] = q_ref[:, pl.ds(0, LEAD), :]
+            for copy in along_z:
+                copy.start()
+            for copy in along_x:
+                copy.start()
+
+        rings[4].wait_recv()
+        rings[5].start()
+        pairs[(2, 1)].start()
+        pairs[(2, 1)].wait_recv()
+
+    def event_7():
+        rings[5].wait_recv()
+        pairs[(3, 1)].start()
+
+        @pl.when((x == 0) & (z > 0))
+        def _():
+            along_z[0].wait_recv()
+            for copy in along_x:
+                copy.start()
+
+        pairs[(3, 1)].wait_recv()
+
+    events = [event_0, event_1, event_2, event_3, event_4, event_5, event_6, event_7]
+
+    @pl.loop(0, len(UNITS))
+    def _(number):
+        for at, event in enumerate(events):
+            pl.when(number == at)(event)
+        block = held[number].reshape(2 * half, held.shape[3])
+        starts = row_starts(number)
+        cosine = jnp.concatenate([cos_ref[pl.ds(start, half), :] for start in starts], axis=0)
+        sine = jnp.concatenate([sin_ref[pl.ds(start, half), :] for start in starts], axis=0)
+
+        def turned(product):
+            return (product * cosine + pltpu.roll(product, HD // 2, 1) * sine).astype(jnp.bfloat16)
+
+        def put(ref, at, rows):
+            for part, start in enumerate(starts):
+                ref[at, pl.ds(start, half), :] = rows[part * half : (part + 1) * half]
+
+        both = dot32(block, jnp.concatenate([wk_ref[...], wv_ref[...]], axis=1))
+        put(kv_ref, 0, turned(both[:, :HD]))
+        put(kv_ref, 1, both[:, HD:].astype(jnp.bfloat16))
+        product = dot32(block, wq_ref[...])
+        for at in range(heads):
+            put(q_ref, at, turned(product[:, at * HD : (at + 1) * HD]))
+        for copy in kv_copies(number):
+            copy.start()
+
+    @pl.loop(0, len(UNITS))
+    def _(number):
+        for copy in kv_copies(number):
+            copy.wait_recv()
+            copy.wait_send()
+
+    for copy in rings:
+        copy.wait_send()
+    for unit in UNITS:
+        pairs[unit].wait_send()
+    for copy in side:
+        copy.wait_recv()
+        copy.wait_send()
+
+    @pl.when(seq == 0)
+    def _():
+        for copy in along_z:
+            copy.wait_send()
+
+    @pl.when(x == 0)
+    def _():
+        for copy in along_x:
+            copy.wait_send()
+
+    @pl.when(x > 0)
+    def _():
+        along_x[0].wait_recv()
+
+
+def gather_project(normed, w_query, w_key, w_value, cosine, sine, slots, owner):
+    rows, width = cosine.shape[0], normed.shape[-1]
+    heads = w_query.shape[1] // HD
+    half = normed.shape[1]
+    vmem = pl.BlockSpec(memory_space=pltpu.VMEM)
+    dma = pltpu.SemaphoreType.DMA
+    shape = jax.ShapeDtypeStruct
     return pl.pallas_call(
-        kv_kernel,
-        grid=(rows // tile,),
-        in_specs=[
-            pl.BlockSpec((tile, width), lambda i: (i, 0)),
-            pl.BlockSpec(w_key.shape, lambda i: (0, 0)),
-            pl.BlockSpec(w_value.shape, lambda i: (0, 0)),
-            pl.BlockSpec((tile, HD), lambda i: (i, 0)),
-            pl.BlockSpec((tile, HD), lambda i: (i, 0)),
+        gather_kernel,
+        in_specs=[vmem] * 8,
+        out_specs=[vmem] * 6,
+        out_shape=[
+            shape((heads, rows, HD), jnp.bfloat16),
+            shape((2, rows, HD), jnp.bfloat16),
+            shape((2, rows, HD), jnp.bfloat16),
+            shape(slots.shape, jnp.bfloat16),
+            shape(owner.shape, jnp.int32),
+            shape((heads, LEAD, HD), jnp.bfloat16),
         ],
-        out_specs=pl.BlockSpec((2, tile, HD), lambda i: (0, i, 0)),
-        out_shape=jax.ShapeDtypeStruct((2, rows, HD), jnp.bfloat16),
-        cost_estimate=pl.CostEstimate(
-            flops=4 * rows * width * HD, bytes_accessed=rows * width * 2, transcendentals=0
+        scratch_shapes=[
+            pltpu.VMEM((len(UNITS), 2, half, width), jnp.bfloat16),
+            dma((6,)),
+            dma((len(UNITS),)),
+            dma((len(UNITS),)),
+            dma((len(UNITS),)),
+            dma((2 * len(UNITS),)),
+            dma((2 * len(UNITS),)),
+            dma((2,)),
+            dma((2,)),
+            dma((Z + 2,)),
+            dma,
+        ],
+        compiler_params=pltpu.CompilerParams(
+            collective_id=0, has_side_effects=True, vmem_limit_bytes=LIMIT
         ),
-        name="project_kv",
-    )(x, w_key, w_value, cosine, sine)
-
-
-def project_q(x, w_query, cosine, sine):
-    rows, width = x.shape
-    heads = w_query.shape[1] // HD
-    tile = TILE
-    return pl.pallas_call(
-        q_kernel,
-        grid=(rows // tile,),
-        in_specs=[
-            pl.BlockSpec((tile, width), lambda i: (i, 0)),
-            pl.BlockSpec(w_query.shape, lambda i: (0, 0)),
-            pl.BlockSpec((tile, HD), lambda i: (i, 0)),
-            pl.BlockSpec((tile, HD), lambda i: (i, 0)),
-        ],
-        out_specs=pl.BlockSpec((heads, tile, HD), lambda i: (0, i, 0)),
-        out_shape=jax.ShapeDtypeStruct((heads, rows, HD), jnp.bfloat16),
-        cost_estimate=pl.CostEstimate(
-            flops=2 * heads * rows * width * HD, bytes_accessed=rows * width * 2, transcendentals=0
-        ),
-        name="project_q",
-    )(x, w_query, cosine, sine)
+        name="gather_project",
+    )(normed, w_query, w_key, w_value, cosine, sine, slots, owner)
 
 
 def local_kernel(
@@ -253,23 +535,145 @@
     )(first, queries, before, here, slot_before, slot_here, owner, facts)
 
 
-def long_kernel(q_ref, cache_ref, mix_ref, top_ref, sum_ref):
-    for head in range(q_ref.shape[0]):
-        scores = dot_t(q_ref[head], cache_ref[0]) * SCALE
-        top = jnp.max(scores, axis=1, keepdims=True)
-        weights = jnp.exp(scores - top)
-        mix_ref[head] = dot32(weights.astype(jnp.bfloat16), cache_ref[1])
-        top_ref[head] = jnp.broadcast_to(top, top_ref.shape[1:])
-        sum_ref[head] = jnp.broadcast_to(jnp.sum(weights, axis=1, keepdims=True), sum_ref.shape[1:])
+def merge(into, top, total, part, part_top, part_total):
+    highest = jnp.maximum(top, part_top)
+    keep, add = jnp.exp(top - highest), jnp.exp(part_top - highest)
+    return into * keep + part * add, highest, total * keep + part_total * add
+
+
+def long_kernel(q_ref, cache_ref, mix_ref, stat_ref, mix_out, stat_out, mix_in, stat_in, sends, recvs):
+    seq, head, _, _ = place()
+    n_x = lax.axis_size("seq") // Z
+    x, z = seq // Z, lax.rem(seq, Z)
+    barrier = pltpu.get_barrier_semaphore()
+
+    @pl.when(z > 0)
+    def _():
+        greet((x * Z, head))
+        pl.semaphore_wait(barrier, 1)
+
+    @pl.when((z == 0) & (x > 0))
+    def _():
+        for at in range(1, Z):
+            greet((x * Z + at, head))
+        greet((0, head))
+        pl.semaphore_wait(barrier, Z)
+
+    @pl.when(seq == 0)
+    def _():
+        for at in range(1, Z):
+            greet((at, head))
+        for at in range(1, n_x):
+            greet((at * Z, head))
+        pl.semaphore_wait(barrier, Z - 1 + n_x - 1)
+
+    scores = dot_t(cache_ref[0], q_ref[...]) * SCALE
+    top = jnp.max(scores, axis=0, keepdims=True)
+    weights = jnp.exp(scores - top)
+    total = jnp.sum(weights, axis=0, keepdims=True)
+    mixed = lax.dot_general(
+        cache_ref[1],
+        weights.astype(jnp.bfloat16),
+        (((0,), (0,)), ((), ())),
+        preferred_element_type=jnp.float32,
+    )
+
+    def keep_state(mixed, top, total):
+        mix_out[...] = mixed.astype(jnp.bfloat16)
+        stat_out[0:1, :] = top
+        stat_out[1:2, :] = total
+
+    def copies(slot, to):
+        return [
+            pltpu.make_async_remote_copy(
+                src_ref=source,
+                dst_ref=target.at[slot],
+                send_sem=sends.at[number],
+                recv_sem=recvs.at[number, slot],
+                device_id=(to, head),
+                device_id_type=MESH,
+            )
+            for number, (source, target) in enumerate([(mix_out, mix_in), (stat_out, stat_in)])
+        ]
+
+    def collect(slots, mixed, top, total):
+        for slot in slots:
+            for copy in copies(slot, jnp.int32(0)):
+                copy.wait_recv()
+            mixed, top, total = merge(
+                mixed,
+                top,
+                total,
+                mix_in[slot].astype(jnp.float32),
+                stat_in[slot, 0:1, :],
+                stat_in[slot, 1:2, :],
+            )
+        return mixed, top, total
+
+    stat_out[...] = jnp.zeros_like(stat_out)
+    keep_state(mixed, top, total)
+    mix_ref[...] = mixed
+    stat_ref[0:1, :] = top
+    stat_ref[1:2, :] = total
+
+    for at in range(1, Z):
+        @pl.when(z == at)
+        def _():
+            for copy in copies(at - 1, x * Z):
+                copy.start()
+            for copy in copies(at - 1, x * Z):
+                copy.wait_send()
+
+    @pl.when(z == 0)
+    def _():
+        state = collect(range(Z - 1), mix_ref[...], stat_ref[0:1, :], stat_ref[1:2, :])
+
+        @pl.when(x > 0)
+        def _():
+            keep_state(*state)
+
+        mix_ref[...] = state[0]
+        stat_ref[0:1, :] = state[1]
+        stat_ref[1:2, :] = state[2]
+
+    for at in range(1, n_x):
+        @pl.when((z == 0) & (x == at))
+        def _():
+            for copy in copies(Z - 2 + at, jnp.int32(0)):
+                copy.start()
+            for copy in copies(Z - 2 + at, jnp.int32(0)):
+                copy.wait_send()
+
+    @pl.when(seq == 0)
+    def _():
+        state = collect(
+            range(Z - 1, Z + n_x - 2), mix_ref[...], stat_ref[0:1, :], stat_ref[1:2, :]
+        )
+        mix_ref[...] = state[0]
+        stat_ref[0:1, :] = state[1]
+        stat_ref[1:2, :] = state[2]
 
 
 def long_part(lead_queries, cache):
-    shape = jax.ShapeDtypeStruct(lead_queries.shape, jnp.float32)
+    queries = lead_queries.shape[0]
+    slots = Z - 1 + 3
+    shape = jax.ShapeDtypeStruct
+    dma = pltpu.SemaphoreType.DMA
     return pl.pallas_call(
         long_kernel,
-        out_shape=[shape, shape, shape],
-        cost_estimate=pl.CostEstimate(
-            flops=4 * 192 * cache.shape[1] * HD, bytes_accessed=cache.size * 2, transcendentals=192 * 1024
+        in_specs=[pl.BlockSpec(memory_space=pltpu.VMEM)] * 2,
+        out_specs=[pl.BlockSpec(memory_space=pltpu.VMEM)] * 2,
+        out_shape=[shape((HD, queries), jnp.float32), shape((8, queries), jnp.float32)],
+        scratch_shapes=[
+            pltpu.VMEM((HD, queries), jnp.bfloat16),
+            pltpu.VMEM((8, queries), jnp.float32),
+            pltpu.VMEM((slots, HD, queries), jnp.bfloat16),
+            pltpu.VMEM((slots, 8, queries), jnp.float32),
+            dma((2,)),
+            dma((2, slots)),
+        ],
+        compiler_params=pltpu.CompilerParams(
+            collective_id=1, has_side_effects=True, vmem_limit_bytes=LIMIT
         ),
         name="long_part",
     )(lead_queries, cache)
@@ -291,37 +695,27 @@
     seq_index = lax.axis_index("seq")
     long_len = long_cache.shape[1] * lax.axis_size("seq")
     heads = w_query.shape[1] // HD
-    earlier_slots, earlier_owner = from_behind((short_cache, slot_owner), "seq", 1)
-    normed = normalize(tokens, norm_gain)
-    piece = lax.all_gather(normed, "head", axis=0, tiled=True)
-    rows = piece.shape[0]
+    rows = tokens.shape[0] * lax.axis_size("head")
     starts = request_starts(new_len)
     token_index = seq_index * rows + jnp.arange(rows, dtype=jnp.int32)
     request, begin, position = token_facts(token_index, starts, cache_len, long_len)
     cosine, sine = rotate_tables(position)
-    here = project_kv(piece, w_key, w_value, cosine, sine)
-    before = from_behind(here, "seq", 1)
-    queries = project_q(piece, w_query, cosine, sine)
-
-    lead_queries = queries[:, :LEAD]
-    lead_queries = lax.psum(jnp.where(seq_index == 0, lead_queries, jnp.zeros_like(lead_queries)), "seq")
-    long_mix, long_top, long_sum = long_part(lead_queries, long_cache)
-    long_high = lax.pmax(long_top[:, :, 0], "seq")
-    shrink = jnp.exp(long_top[:, :, 0] - long_high)
-    packed = jnp.concatenate(
-        [long_mix * shrink[..., None], jnp.tile((long_sum[:, :, 0] * shrink)[:, None, :], (1, 1, HD // LEAD))],
-        axis=1,
+    normed = normalize(tokens, norm_gain).reshape(2, LEAD, tokens.shape[1])
+    queries, here, before, earlier_slots, earlier_owner, lead_queries = gather_project(
+        normed, w_query, w_key, w_value, cosine, sine, short_cache, slot_owner[None, :]
     )
-    packed = lax.psum(packed, "seq")
-    long_mix = packed[:, :LEAD]
-    long_sum = packed[:, LEAD, :LEAD]
+    lead_queries = jnp.pad(lead_queries.reshape(heads * LEAD, HD), ((0, LEAD), (0, 0)))
+    long_mix, long_stat = long_part(lead_queries, long_cache)
+    long_mix = long_mix[:, : heads * LEAD].reshape(HD, heads, LEAD).transpose(1, 2, 0)
+    long_high = long_stat[0, : heads * LEAD].reshape(heads, LEAD)
+    long_sum = long_stat[1, : heads * LEAD].reshape(heads, LEAD)
 
     shift = (seq_index - 1) * rows
     window_begin = jnp.maximum(begin - shift, 0)
     window_index = token_index - shift
     window_begin = jnp.where(request == starts.shape[0], -shift, window_begin)
     facts = jnp.stack([request, window_begin, window_index] + [window_index] * 5, axis=1)
-    owner = jnp.concatenate([jnp.where(seq_index > 0, earlier_owner, -1), slot_owner])[None, :]
+    owner = jnp.concatenate([jnp.where(seq_index > 0, earlier_owner[0], -1), slot_owner])[None, :]
     first = window_begin[::TILE] // TILE
     attended, lead_mix, lead_top, lead_sum = local_attention(
         first, queries, before, here, earlier_slots, short_cache, owner, facts

time: 520 us -> 168 us (0.32)
  waiting for transfers between devices: 260 us -> 41.9 us
  blocking collectives: 172 us -> 0 us
  Pallas kernels: 36.8 us -> 86.9 us
  starting transfers between devices: 11.7 us -> 0.01 us
    psum x1 -> x0, waiting for transfers between devices: 170 us -> none  [on_device(): packed = lax.psum(packed, 'seq')]
    psum x1 -> x0, blocking collectives: 116 us -> none  [on_device(): lax.psum(jnp.where(seq_index == 0, lead_queries, jnp.zeros_like(lead_quer...]
    pmax x1 -> x0, blocking collectives: 56.1 us -> none  [on_device(): long_high = lax.pmax(long_top[:, :, 0], 'seq')]
    pallas_call x3 -> x2, Pallas kernels: 18 us -> 68.3 us  [the longest x1 49.9 us: gather_project(): pl.pallas_call(gather_kernel, in_specs=[vmem] * 8, out_specs=[vmem] * 6,...]
    all_gather x1 -> x0, waiting for transfers between devices: 34.2 us -> none  [on_device(): piece = lax.all_gather(normed, 'head', axis=0, tiled=True)]
    reduce_scatter x1, waiting for transfers between devices: 55.8 us -> 41.9 us  [on_device(): lax.psum_scatter(dot32(attended, w_out).astype(jnp.bfloat16), 'head', sca...]
    ppermute x3 -> x0, starting transfers between devices: 11.4 us -> none  [from_behind(): return lax.ppermute(block, axis, route)]
  transfers between devices with their start and end apart: 6 -> 1, of which waited for: 3 -> 1; matrix products, arithmetic and copies ran while one was open for 2% -> 0% of each run, Pallas kernels for 3% -> 0%
where the time goes in v2:
time: 168 us; the launch traced here: 167 us
  Pallas kernels  86.9 us (52%)
  waiting for transfers between devices  41.9 us (25%)
  between operations  13.5 us (8%)
  other arithmetic  12.8 us (8%)
  matrix products  6.45 us (4%)
  local copies, waits for them, and re-layouts  5.55 us (3%)
    pallas_call x1, Pallas kernels, gather_project(): pl.pallas_call(gather_kernel, in_specs=[vmem] * 8, out_specs=[vmem] * 6,...  49.9 us
    reduce_scatter x1, waiting for transfers between devices, on_device(): lax.psum_scatter(dot32(attended, w_out).astype(jnp.bfloat16), 'head', sca...  41.9 us
    pallas_call x1, Pallas kernels, local_attention(): pl.pallas_call(local_kernel, grid_spec=pltpu.PrefetchScalarGridSpec(num_s...  18.7 us
    pallas_call x1, Pallas kernels, long_part(): pl.pallas_call(long_kernel, in_specs=[pl.BlockSpec(memory_space=pltpu.VME...  18.4 us
    dot_general x1, matrix products, dot32(): return jnp.dot(a, b, preferred_element_type=jnp.float32)  6.45 us
  transfers between devices with their start and end apart: 1, of which 1 were waited for; matrix products, arithmetic and copies ran while one was open for 0% of the time, Pallas kernels for 0%

profile of v2, /device:TPU:1, one launch (start us, length us, event | category | flops | bytes accessed | tf_op | source)
XLA Modules:
  0.0 167.1 jit_solution(6871084164671330591)
XLA Ops:
  6.5 0.0 copy-start
  6.5 0.0 reduce-scatter.2.cloned.1.call-start
  6.6 1.5 fusion
  8.1 0.7 copy.40
  8.8 0.1 reduce-window.9
  8.9 0.1 add_reduce_fusion.1
  9.0 0.7 sub.60
  9.7 0.1 convert_reduce_fusion
  9.8 0.8 select_reduce_fusion
  10.6 0.1 slice.21
  10.7 0.5 and_select_fusion.first_ref
  11.3 0.1 stack.2
  11.4 1.0 copy.41.facts_ref
  12.4 2.3 %fusion.2 = bf16[128,3072]{1,0:T(8,128)(2,1)} fusion(bf16[128,3072]{1,0:T(8,128)(2,1)} %param.11, f32[3072]{0:T(1024)} %param.12, f32[128]{0:T(128)S(1)} %add_rsqrt_fusion), kind=kLoop, calls=%fused_computation.5 | loop fusion | flops 1572864 | bytes 1585664 | tf_op jit(solution)/shard_map/convert_element_type | solution.py:43
  14.6 1.9 %fusion.3 = (f32[1024,64]{1,0:T(8,128)S(1)}, f32[1024,64]{1,0:T(8,128)S(1)}, f32[1024,64]{1,0:T(8,128)S(1)}) fusion(f32[64]{0:T(128)S(1)} %multiply_exponential_fusion, f32[1024]{0:T(1024)S(1)} %get-tuple-element.38), kind=kLoop, calls=%fused_computation.14 | loop fusion | flops 131072 | bytes 790784 | tf_op jit(solution)/shard_map/neg | solution.py:54
  16.5 1.3 pad_maximum_fusion
  17.9 49.9 %gather_project.1 = (bf16[3,1024,128]{2,1,0:T(8,128)(2,1)}, bf16[2,1024,128]{2,1,0:T(8,128)(2,1)}, bf16[2,1024,128]{2,1,0:T(8,128)(2,1)}, bf16[2,256,128]{2,1,0:...) custom-call(bf16[2,64,3072]{2,1,0:T(8,128)(2,1)} %bitcast.29, bf16[3072,384]{1,0:T(8,128)(2,1)} %wq_ref.1, ...), custom_call_target="tpu_custom_call" | custom-call | tf_op jit(solution)/shard_map/gather_project/pallas_call | solution.py:376
  67.8 0.0 copy-done.1
  67.8 0.6 pad_add_fusion
  68.4 1.4 pad.4.q_ref
  69.8 18.4 %long_part.1 = (f32[128,256]{1,0:T(8,128)}, f32[8,256]{1,0:T(8,128)}) custom-call(bf16[256,128]{1,0:T(8,128)(2,1)} %pad.4.q_ref, bf16[2,1024,128]{2,1,0:T(8,128)(2,1)} %cache_ref.1), custom_call_target="tpu_custom_call" | custom-call | tf_op jit(solution)/shard_map/long_part/pallas_call | solution.py:662
  88.2 0.8 slice_reduce_fusion.1
  89.0 1.0 copy.43
  90.0 0.2 reshape_squeeze.9
  90.2 0.2 reshape_squeeze.8
  90.4 18.7 %local_attention.1 = (bf16[1024,384]{1,0:T(8,128)(2,1)}, f32[3,64,128]{2,1,0:T(8,128)}, f32[3,64,128]{2,1,0:T(8,128)}, f32[3,64,128]{2,1,0:T(8,128)}) custom-call(s32[4]{0:T(128)} %and_select_fusion.first_ref, bf16[3,1024,128]{2,1,0:T(8,128)(2,1)} %get-tuple-element.17.q_ref, bf16[2,1024,128]{2,1,0:T(8,128)(2,1)} %get-tuple-element.18.before_ref, ...), custom_call_target="tpu_custom_call" | custom-call | flops 2415919104 | bytes 3145728 | tf_op jit(solution)/shard_map/local_attention/pallas_call | solution.py:496
  109.1 1.1 fusion.11
  110.2 1.7 %fusion.8 = bf16[1024,384]{1,0:T(8,128)(2,1)} fusion(bf16[1024,384]{1,0:T(8,128)(2,1)} %get-tuple-element.22, pred[]{:T(512)S(6)} %eq.34, f32[3,64]{1,0:T(4,128)S(1)} %get-tuple-element.30, f32[128,3,64]{0,2,1:T(8,128)S(1)} %bitcast.30, f32[3,64]{1,0:T(4,128)S(1)} %get-tuple-element.31, f32[3,64,128]{2,1,0:T(8,128)} %get-tuple-element.23, ...), kind=kLoop, calls=%fused_computation.24 | loop fusion | flops 147456 | bytes 297217 | tf_op jit(solution)/shard_map/dynamic_update_slice | solution.py:733
  111.9 0.0 copy-done
  111.9 6.4 %convolution_convert_fusion = bf16[1024,3072]{1,0:T(8,128)(2,1)} fusion(bf16[1024,384]{1,0:T(8,128)(2,1)} %fusion.8, bf16[384,3072]{1,0:T(8,128)(2,1)S(1)} %copy-done), kind=kOutput, calls=%fused_computation | convolution fusion | flops 2419064832 | bytes 9437184 | tf_op jit(solution)/shard_map/dot_general | solution.py:59
  118.3 0.0 reduce-scatter.2.cloned.1.call-update
  118.4 41.9 %reduce-scatter.2.cloned.1.call-done = bf16[128,3072]{1,0:T(8,128)(2,1)} async-done(((bf16[1024,3072]{1,0:T(8,128)(2,1)}), bf16[128,3072]{1,0:T(8,128)(2,1)}) %reduce-scatter.2.cloned.1.call-update) | async-done | bytes 786448 | tf_op jit(solution)/shard_map/reduce_scatter | solution.py:734
  (8 shorter events, 0.1 us)
Async XLA Ops:
  6.5 105.4 %copy-start = (bf16[384,3072]{1,0:T(8,128)(2,1)S(1)}, bf16[384,3072]{1,0:T(8,128)(2,1)}, u32[]{:S(2)}) copy-start(bf16[384,3072]{1,0:T(8,128)(2,1)} %param.16) | copy-start | bytes 7077892
  6.5 153.7 %reduce-scatter.2.cloned.1.call-start = ((), (), s32[]{:S(2)}) async-start(), calls=%async_computation.1 | async-start | bytes 7077888 | tf_op jit(solution)/shard_map/reduce_scatter | solution.py:734
  17.9 50.0 %copy-start.1 = (s32[256]{0:T(256)S(1)}, s32[256]{0:T(256)}, u32[]{:S(2)}) copy-start(s32[256]{0:T(256)} %param.19) | copy-start | bytes 3076
Sparse Core Ops, SparseCore 0:
  118.5 41.7 reduce-scatter.1

commit v3 on v2

--- a/solution.py
+++ b/solution.py
@@ -541,23 +541,60 @@
     return into * keep + part * add, highest, total * keep + part_total * add
 
 
-def long_kernel(q_ref, cache_ref, mix_ref, stat_ref, mix_out, stat_out, mix_in, stat_in, sends, recvs):
-    seq, head, _, _ = place()
+PIECES = 4
+
+
+def scatter_kernel(
+    attended_ref,
+    w_ref,
+    q_ref,
+    cache_ref,
+    near_mix_ref,
+    near_top_ref,
+    near_sum_ref,
+    out_ref,
+    pair_out,
+    pair_in,
+    own,
+    ring_out,
+    ring_in,
+    mix_out,
+    stat_out,
+    mix_in,
+    stat_in,
+    pair_send,
+    pair_recv,
+    ring_send,
+    ring_recv,
+    sends,
+    recvs,
+):
+    seq, head, y, core = place()
     n_x = lax.axis_size("seq") // Z
     x, z = seq // Z, lax.rem(seq, Z)
+    way = 1 - 2 * core
+    right = (seq, lax.rem(y + way + Y, Y) * 2 + core)
+    left = (seq, lax.rem(y - way + Y, Y) * 2 + core)
+    pair = (seq, head + way)
+    half = ring_out.shape[2]
+    heads = q_ref.shape[0]
+    width = w_ref.shape[1] // PIECES
     barrier = pltpu.get_barrier_semaphore()
 
+    for device in (right, left, pair):
+        greet(device)
+
     @pl.when(z > 0)
     def _():
         greet((x * Z, head))
-        pl.semaphore_wait(barrier, 1)
+        pl.semaphore_wait(barrier, 3 + 1)
 
     @pl.when((z == 0) & (x > 0))
     def _():
         for at in range(1, Z):
             greet((x * Z + at, head))
         greet((0, head))
-        pl.semaphore_wait(barrier, Z)
+        pl.semaphore_wait(barrier, 3 + Z)
 
     @pl.when(seq == 0)
     def _():
@@ -565,12 +602,74 @@
             greet((at, head))
         for at in range(1, n_x):
             greet((at * Z, head))
-        pl.semaphore_wait(barrier, Z - 1 + n_x - 1)
-
-    scores = dot_t(cache_ref[0], q_ref[...]) * SCALE
+        pl.semaphore_wait(barrier, 3 + Z - 1 + n_x - 1)
+
+    def columns(piece):
+        return pl.ds(piece * width, width)
+
+    def rows_of(chip, of_core, later):
+        return attended_ref[pl.ds(pl.multiple_of(chip * (4 * half) + of_core * (2 * half) + later * half, half), half), :]
+
+    def stack(later):
+        parts = [rows_of(lax.rem(y - k * way + 2 * Y * 2, Y), 1 - core, later) for k in range(Y)]
+        parts += [rows_of(lax.rem(y + k * way + 2 * Y * 2, Y), core, later) for k in range(Y)]
+        return jnp.concatenate(parts, axis=0)
+
+    def pair_copy(later, piece):
+        return pltpu.make_async_remote_copy(
+            src_ref=pair_out.at[later, :, columns(piece)],
+            dst_ref=pair_in.at[later, :, columns(piece)],
+            send_sem=pair_send.at[later, piece],
+            recv_sem=pair_recv.at[later, piece],
+            device_id=pair,
+            device_id_type=MESH,
+        )
+
+    def ring_copy(later, step, piece):
+        return pltpu.make_async_remote_copy(
+            src_ref=ring_out.at[later, step, :, columns(piece)],
+            dst_ref=ring_in.at[later, step, :, columns(piece)],
+            send_sem=ring_send.at[later, step, piece],
+            recv_sem=ring_recv.at[later, step, piece],
+            device_id=left if (later, step) == (0, 2) else right,
+            device_id_type=MESH,
+        )
+
+    def project(rows, later, piece):
+        product = dot32(rows, w_ref[:, columns(piece)]).astype(jnp.bfloat16)
+        pair_out[later, :, columns(piece)] = product[: Y * half]
+        own[later, :, columns(piece)] = product[Y * half :]
+
+    def chip_sum(later, k, piece):
+        rows = pl.ds(k * half, half)
+        return own[later, rows, columns(piece)].astype(jnp.float32) + pair_in[
+            later, rows, columns(piece)
+        ].astype(jnp.float32)
+
+    def arrived(later, step, piece):
+        ring_copy(later, step, piece).wait_recv()
+        return ring_in[later, step, :, columns(piece)].astype(jnp.float32)
+
+    def pass_on(later, step, piece, value):
+        ring_out[later, step, :, columns(piece)] = value.astype(jnp.bfloat16)
+        ring_copy(later, step, piece).start()
+
+    def first_hop(piece):
+        pair_copy(1, piece).wait_recv()
+        pass_on(1, 0, piece, chip_sum(1, 3, piece))
+
+    rows = stack(1)
+    for piece in range(PIECES):
+        project(rows, 1, piece)
+        pair_copy(1, piece).start()
+        if piece:
+            first_hop(piece - 1)
+    first_hop(PIECES - 1)
+
+    queries = jnp.concatenate([q_ref[at] for at in range(heads)] + [q_ref[heads - 1]], axis=0)
+    scores = dot_t(cache_ref[0], queries) * SCALE
     top = jnp.max(scores, axis=0, keepdims=True)
     weights = jnp.exp(scores - top)
-    total = jnp.sum(weights, axis=0, keepdims=True)
     mixed = lax.dot_general(
         cache_ref[1],
         weights.astype(jnp.bfloat16),
@@ -583,7 +682,7 @@
         stat_out[0:1, :] = top
         stat_out[1:2, :] = total
 
-    def copies(slot, to):
+    def state_copies(slot, to):
         return [
             pltpu.make_async_remote_copy(
                 src_ref=source,
@@ -596,87 +695,142 @@
             for number, (source, target) in enumerate([(mix_out, mix_in), (stat_out, stat_in)])
         ]
 
-    def collect(slots, mixed, top, total):
+    def collect(slots):
+        state = (mix_out[...].astype(jnp.float32), stat_out[0:1, :], stat_out[1:2, :])
         for slot in slots:
-            for copy in copies(slot, jnp.int32(0)):
+            for copy in state_copies(slot, jnp.int32(0)):
                 copy.wait_recv()
-            mixed, top, total = merge(
-                mixed,
-                top,
-                total,
+            state = merge(
+                *state,
                 mix_in[slot].astype(jnp.float32),
                 stat_in[slot, 0:1, :],
                 stat_in[slot, 1:2, :],
             )
-        return mixed, top, total
+            state = (state[0], state[1], state[2])
+        return state
 
     stat_out[...] = jnp.zeros_like(stat_out)
-    keep_state(mixed, top, total)
-    mix_ref[...] = mixed
-    stat_ref[0:1, :] = top
-    stat_ref[1:2, :] = total
-
+    keep_state(mixed, top, jnp.sum(weights, axis=0, keepdims=True))
     for at in range(1, Z):
         @pl.when(z == at)
         def _():
-            for copy in copies(at - 1, x * Z):
+            for copy in state_copies(at - 1, x * Z):
                 copy.start()
-            for copy in copies(at - 1, x * Z):
-                copy.wait_send()
+
+    rows = stack(0)
+    for piece in range(PIECES):
+        project(rows, 0, piece)
+
+    for piece in range(PIECES):
+        pass_on(1, 1, piece, chip_sum(1, 2, piece) + arrived(1, 0, piece))
 
     @pl.when(z == 0)
     def _():
-        state = collect(range(Z - 1), mix_ref[...], stat_ref[0:1, :], stat_ref[1:2, :])
-
-        @pl.when(x > 0)
-        def _():
-            keep_state(*state)
-
-        mix_ref[...] = state[0]
-        stat_ref[0:1, :] = state[1]
-        stat_ref[1:2, :] = state[2]
+        keep_state(*collect(range(Z - 1)))
 
     for at in range(1, n_x):
         @pl.when((z == 0) & (x == at))
         def _():
-            for copy in copies(Z - 2 + at, jnp.int32(0)):
+            for copy in state_copies(Z - 2 + at, jnp.int32(0)):
                 copy.start()
-            for copy in copies(Z - 2 + at, jnp.int32(0)):
-                copy.wait_send()
+
+    for piece in range(PIECES):
+        pass_on(1, 2, piece, chip_sum(1, 1, piece) + arrived(1, 1, piece))
 
     @pl.when(seq == 0)
     def _():
-        state = collect(
-            range(Z - 1, Z + n_x - 2), mix_ref[...], stat_ref[0:1, :], stat_ref[1:2, :]
-        )
-        mix_ref[...] = state[0]
-        stat_ref[0:1, :] = state[1]
-        stat_ref[1:2, :] = state[2]
-
-
-def long_part(lead_queries, cache):
-    queries = lead_queries.shape[0]
+        mixed, top, total = collect(range(Z - 1, Z + n_x - 2))
+        mixed = jnp.transpose(mixed)
+        top = jnp.transpose(jnp.broadcast_to(top, mix_out.shape))
+        total = jnp.transpose(jnp.broadcast_to(total, mix_out.shape))
+        parts = []
+        for at in range(heads):
+            lead = slice(at * LEAD, (at + 1) * LEAD)
+            joined = merge(
+                near_mix_ref[at],
+                near_top_ref[at],
+                near_sum_ref[at],
+                mixed[lead],
+                top[lead],
+                total[lead],
+            )
+            parts.append((joined[0] / joined[2]).astype(jnp.bfloat16))
+        lead_rows = jnp.concatenate(parts, axis=1)
+        for piece in range(PIECES):
+            product = dot32(lead_rows, w_ref[:, columns(piece)]).astype(jnp.bfloat16)
+
+            @pl.when(core == 0)
+            def _():
+                at = pl.multiple_of(lax.rem(Y - y, Y) * half, half)
+                own[0, pl.ds(at, half), columns(piece)] = product
+
+            @pl.when(core == 1)
+            def _():
+                at = pl.multiple_of(lax.rem(Y - y, Y) * half, half)
+                pair_out[0, pl.ds(at, half), columns(piece)] = product
+
+    for piece in range(PIECES):
+        pair_copy(0, piece).start()
+    for piece in range(PIECES):
+        pair_copy(0, piece).wait_recv()
+        pass_on(0, 0, piece, chip_sum(0, 2, piece))
+        pass_on(0, 2, piece, chip_sum(0, 3, piece))
+    for piece in range(PIECES):
+        value = chip_sum(1, 0, piece) + arrived(1, 2, piece)
+        out_ref[pl.ds(half, half), columns(piece)] = value.astype(jnp.bfloat16)
+    for piece in range(PIECES):
+        pass_on(0, 1, piece, chip_sum(0, 1, piece) + arrived(0, 0, piece))
+    for piece in range(PIECES):
+        value = chip_sum(0, 0, piece) + arrived(0, 2, piece) + arrived(0, 1, piece)
+        out_ref[pl.ds(0, half), columns(piece)] = value.astype(jnp.bfloat16)
+
+    for later in range(2):
+        for piece in range(PIECES):
+            pair_copy(later, piece).wait_send()
+            for step in range(3):
+                ring_copy(later, step, piece).wait_send()
+
+    @pl.when(seq > 0)
+    def _():
+        for copy in state_copies(0, jnp.int32(0)):
+            copy.wait_send()
+
+
+def project_scatter(attended, w_out, lead_queries, cache, near_mix, near_top, near_sum):
+    rows, inner = attended.shape
+    width = w_out.shape[1]
+    half = LEAD
     slots = Z - 1 + 3
-    shape = jax.ShapeDtypeStruct
+    queries = (lead_queries.shape[0] + 1) * LEAD
+    vmem = pl.BlockSpec(memory_space=pltpu.VMEM)
     dma = pltpu.SemaphoreType.DMA
     return pl.pallas_call(
-        long_kernel,
-        in_specs=[pl.BlockSpec(memory_space=pltpu.VMEM)] * 2,
-        out_specs=[pl.BlockSpec(memory_space=pltpu.VMEM)] * 2,
-        out_shape=[shape((HD, queries), jnp.float32), shape((8, queries), jnp.float32)],
+        scatter_kernel,
+        in_specs=[vmem] * 7,
+        out_specs=vmem,
+        out_shape=jax.ShapeDtypeStruct((2 * half, width), jnp.bfloat16),
         scratch_shapes=[
+            pltpu.VMEM((2, Y * half, width), jnp.bfloat16),
+            pltpu.VMEM((2, Y * half, width), jnp.bfloat16),
+            pltpu.VMEM((2, Y * half, width), jnp.bfloat16),
+            pltpu.VMEM((2, 3, half, width), jnp.bfloat16),
+            pltpu.VMEM((2, 3, half, width), jnp.bfloat16),
             pltpu.VMEM((HD, queries), jnp.bfloat16),
             pltpu.VMEM((8, queries), jnp.float32),
             pltpu.VMEM((slots, HD, queries), jnp.bfloat16),
             pltpu.VMEM((slots, 8, queries), jnp.float32),
+            dma((2, PIECES)),
+            dma((2, PIECES)),
+            dma((2, 3, PIECES)),
+            dma((2, 3, PIECES)),
             dma((2,)),
             dma((2, slots)),
         ],
         compiler_params=pltpu.CompilerParams(
             collective_id=1, has_side_effects=True, vmem_limit_bytes=LIMIT
         ),
-        name="long_part",
-    )(lead_queries, cache)
+        name="project_scatter",
+    )(attended, w_out, lead_queries, cache, near_mix, near_top, near_sum)
 
 
 def on_device(
@@ -704,11 +858,6 @@
     queries, here, before, earlier_slots, earlier_owner, lead_queries = gather_project(
         normed, w_query, w_key, w_value, cosine, sine, short_cache, slot_owner[None, :]
     )
-    lead_queries = jnp.pad(lead_queries.reshape(heads * LEAD, HD), ((0, LEAD), (0, 0)))
-    long_mix, long_stat = long_part(lead_queries, long_cache)
-    long_mix = long_mix[:, : heads * LEAD].reshape(HD, heads, LEAD).transpose(1, 2, 0)
-    long_high = long_stat[0, : heads * LEAD].reshape(heads, LEAD)
-    long_sum = long_stat[1, : heads * LEAD].reshape(heads, LEAD)
 
     shift = (seq_index - 1) * rows
     window_begin = jnp.maximum(begin - shift, 0)
@@ -720,19 +869,8 @@
     attended, lead_mix, lead_top, lead_sum = local_attention(
         first, queries, before, here, earlier_slots, short_cache, owner, facts
     )
-    lead_top = lead_top[:, :, 0]
-    lead_sum = lead_sum[:, :, 0]
-    highest = jnp.maximum(lead_top, long_high)
-    scale_near = jnp.exp(lead_top - highest)
-    scale_long = jnp.exp(long_high - highest)
-    total = lead_sum * scale_near + long_sum * scale_long
-    mixture = lead_mix * scale_near[..., None] + long_mix * scale_long[..., None]
-    lead_out = (mixture / total[..., None]).astype(jnp.bfloat16)
-    lead_out = jnp.transpose(lead_out, (1, 0, 2)).reshape(LEAD, heads * HD)
-    lead_out = jnp.where(seq_index == 0, lead_out, attended[:LEAD])
-    attended = lax.dynamic_update_slice(attended, lead_out, (0, 0))
-    return lax.psum_scatter(
-        dot32(attended, w_out).astype(jnp.bfloat16), "head", scatter_dimension=0, tiled=True
+    return project_scatter(
+        attended, w_out, lead_queries, long_cache, lead_mix, lead_top, lead_sum
     )
 
 

time: 168 us -> 130 us (0.77)
  waiting for transfers between devices: 41.9 us -> 0 us
  Pallas kernels: 86.9 us -> 116 us
  between operations: 13.5 us -> 0.09 us
  matrix products: 6.45 us -> 0 us
  other arithmetic: 12.8 us -> 9.83 us
    reduce_scatter x1 -> x0, waiting for transfers between devices: 41.9 us -> none  [on_device(): lax.psum_scatter(dot32(attended, w_out).astype(jnp.bfloat16), 'head', sca...]
    pallas_call x1, Pallas kernels: 18.4 us -> 46.9 us  [project_scatter(): pl.pallas_call(scatter_kernel, in_specs=[vmem] * 7, out_specs=vmem, out_s...]
    dot_general x1 -> x0, matrix products: 6.45 us -> none  [dot32(): return jnp.dot(a, b, preferred_element_type=jnp.float32)]
    unnamed x4 -> x3, local copies, waits for them, and re-layouts: 0.01 us -> 2.07 us
    slice x2 -> x0, local copies, waits for them, and re-layouts: 1.79 us -> none  [the longest x1 1 us: on_device(): long_mix[:, :heads * LEAD].reshape(HD, heads, LEAD).transpose(1, 2, 0)]
    dynamic_update_slice x1 -> x0, other arithmetic: 1.7 us -> none  [on_device(): attended = lax.dynamic_update_slice(attended, lead_out, (0, 0))]
  transfers between devices with their start and end apart: 1 -> 0, of which waited for: 1 -> 0; matrix products, arithmetic and copies ran while one was open for 0% -> 0% of each run, Pallas kernels for 0% -> 0%
where the time goes in v3:
time: 130 us; the launch traced here: 129 us
  Pallas kernels  116 us (89%)
  other arithmetic  9.83 us (8%)
  local copies, waits for them, and re-layouts  3.98 us (3%)
    pallas_call x1, Pallas kernels, gather_project(): pl.pallas_call(gather_kernel, in_specs=[vmem] * 8, out_specs=[vmem] * 6,...  50 us
    pallas_call x1, Pallas kernels, project_scatter(): pl.pallas_call(scatter_kernel, in_specs=[vmem] * 7, out_specs=vmem, out_s...  46.9 us
    pallas_call x1, Pallas kernels, local_attention(): pl.pallas_call(local_kernel, grid_spec=pltpu.PrefetchScalarGridSpec(num_s...  18.6 us

profile of v3, /device:TPU:1, one launch (start us, length us, event | category | flops | bytes accessed | tf_op | source)
XLA Modules:
  0.0 129.4 jit_solution(15406462504633604184)
XLA Ops:
  0.0 0.7 copy.19
  0.7 0.1 reduce-window.9
  0.8 0.1 add_reduce_fusion
  1.0 0.7 sub.50
  1.6 0.1 convert_reduce_fusion
  1.7 0.8 select_reduce_fusion
  2.5 0.1 slice.3
  2.6 0.5 and_select_fusion.first_ref
  3.2 1.4 %fusion = f32[128]{0:T(128)S(1)} fusion(bf16[128,3072]{1,0:T(8,128)(2,1)} %param.11), kind=kLoop, calls=%fused_computation.2 | loop fusion | flops 1179520 | bytes 786944 | tf_op jit(solution)/shard_map/reduce_sum | solution.py:42
  4.5 2.3 %fusion.2 = bf16[128,3072]{1,0:T(8,128)(2,1)} fusion(bf16[128,3072]{1,0:T(8,128)(2,1)} %param.11, f32[3072]{0:T(1024)} %param.12, f32[128]{0:T(128)S(1)} %add_rsqrt_fusion), kind=kLoop, calls=%fused_computation.4 | loop fusion | flops 1572864 | bytes 1585664 | tf_op jit(solution)/shard_map/convert_element_type | solution.py:43
  6.8 1.9 %fusion.3 = (f32[1024,64]{1,0:T(8,128)S(1)}, f32[1024,64]{1,0:T(8,128)S(1)}, f32[1024,64]{1,0:T(8,128)S(1)}) fusion(f32[64]{0:T(128)S(1)} %multiply_exponential_fusion, f32[1024]{0:T(1024)S(1)} %get-tuple-element.29), kind=kLoop, calls=%fused_computation.13 | loop fusion | flops 131072 | bytes 790784 | tf_op jit(solution)/shard_map/neg | solution.py:54
  8.8 1.3 %pad_maximum_fusion = (f32[1024,128]{1,0:T(8,128)}, f32[1024,128]{1,0:T(8,128)}) fusion(f32[1024,64]{1,0:T(8,128)S(1)} %get-tuple-element.32, f32[1024,64]{1,0:T(8,128)S(1)} %get-tuple-element.31, f32[1024,64]{1,0:T(8,128)S(1)} %get-tuple-element.30), kind=kLoop, calls=%fused_computation.7 | loop fusion | flops 262144 | bytes 1835008 | tf_op jit(solution)/shard_map/concatenate | solution.py:53
  10.1 0.0 copy-start
  10.1 50.0 %gather_project.1 = (bf16[3,1024,128]{2,1,0:T(8,128)(2,1)}, bf16[2,1024,128]{2,1,0:T(8,128)(2,1)}, bf16[2,1024,128]{2,1,0:T(8,128)(2,1)}, bf16[2,256,128]{2,1,0:...) custom-call(bf16[2,64,3072]{2,1,0:T(8,128)(2,1)} %bitcast.7, bf16[3072,384]{1,0:T(8,128)(2,1)} %wq_ref.1, ...), custom_call_target="tpu_custom_call" | custom-call | tf_op jit(solution)/shard_map/gather_project/pallas_call | solution.py:376
  60.1 0.0 copy-done
  60.1 0.6 pad_add_fusion
  60.7 0.1 stack.2
  60.8 1.0 copy.20.facts_ref
  61.8 18.6 %local_attention.1 = (bf16[1024,384]{1,0:T(8,128)(2,1)}, f32[3,64,128]{2,1,0:T(8,128)}, f32[3,64,128]{2,1,0:T(8,128)}, f32[3,64,128]{2,1,0:T(8,128)}) custom-call(s32[4]{0:T(128)} %and_select_fusion.first_ref, bf16[3,1024,128]{2,1,0:T(8,128)(2,1)} %get-tuple-element.15.q_ref, bf16[2,1024,128]{2,1,0:T(8,128)(2,1)} %get-tuple-element.16.before_ref, ...), custom_call_target="tpu_custom_call" | custom-call | flops 2415919104 | bytes 3145728 | tf_op jit(solution)/shard_map/local_attention/pallas_call | solution.py:496
  80.4 46.9 %project_scatter.1 = bf16[128,3072]{1,0:T(8,128)(2,1)} custom-call(bf16[1024,384]{1,0:T(8,128)(2,1)} %get-tuple-element.20.attended_ref, bf16[384,3072]{1,0:T(8,128)(2,1)} %w_ref.1, bf16[3,64,128]{2,1,0:T(8,128)(2,1)} %get-tuple-element.21.q_ref, bf16[2,1024,128]{2,1,0:T(8,128)(2,1)} %cache_ref.1, f32[3,64,128]{2,1,0:T(8,128)} %get-tuple-element.22.near_mix_ref, ...), custom_call_target="tpu_custom_call" | custom-call | tf_op jit(solution)/shard_map/project_scatter/pallas_call | solution.py:807
  127.4 2.1 %copy.22 = bf16[128,3072]{1,0:T(8,128)(2,1)} copy(bf16[128,3072]{1,0:T(8,128)(2,1)} %project_scatter.1) | data formatting | bytes 1572864
  (7 shorter events, 0.1 us)
Async XLA Ops:
  10.1 50.0 %copy-start = (s32[256]{0:T(256)S(1)}, s32[256]{0:T(256)}, u32[]{:S(2)}) copy-start(s32[256]{0:T(256)} %param.19) | copy-start | bytes 3076

commit v4 on v3

--- a/solution.py
+++ b/solution.py
@@ -12,13 +12,6 @@
 THETA_LOG = math.log(500000.0)
 SCALE = 1.0 / math.sqrt(HD)
 LOW = -1e30
-TILE = 256
-
-
-def from_behind(block, axis, distance):
-    devices = range(lax.axis_size(axis))
-    route = [(i - distance, i) for i in devices if i - distance in devices]
-    return lax.ppermute(block, axis, route)
 
 
 def request_starts(new_len):
@@ -43,16 +36,11 @@
     return (values * lax.rsqrt(mean_square + 1e-05) * norm_gain).astype(jnp.bfloat16)
 
 
-def rotate_tables(position):
+def rotate_table(position):
     half = HD // 2
     frequency = jnp.exp(jnp.arange(half, dtype=jnp.float32) * (-2.0 * THETA_LOG / HD))
     angle = position.astype(jnp.float32)[:, None] * frequency[None, :]
-    cosine = jnp.cos(angle)
-    sine = jnp.sin(angle)
-    return (
-        jnp.concatenate([cosine, cosine], axis=1),
-        jnp.concatenate([-sine, sine], axis=1),
-    )
+    return jnp.concatenate([jnp.cos(angle), jnp.sin(angle)], axis=1)
 
 
 def dot32(a, b):
@@ -91,12 +79,12 @@
 
 
 def gather_kernel(
-    normed_ref,
+    tokens_ref,
+    gain_ref,
     wq_ref,
     wk_ref,
     wv_ref,
-    cos_ref,
-    sin_ref,
+    table_ref,
     slots_ref,
     owner_ref,
     q_ref,
@@ -105,6 +93,7 @@
     slots_before_ref,
     owner_before_ref,
     lead_ref,
+    normed_ref,
     held,
     ring_send,
     ring_recv,
@@ -150,6 +139,10 @@
     def _():
         greet((z, head))
 
+    for later in range(2):
+        normed_ref[later] = normalize(tokens_ref[later], gain_ref[...])
+        held[SLOT[(0, later)], core] = normed_ref[later]
+
     barrier = pltpu.get_barrier_semaphore()
     others = n_seq // Z - 1
 
@@ -253,9 +246,6 @@
     pairs[(0, 1)].start()
     for copy in side:
         copy.start()
-    for later in range(2):
-        held[SLOT[(0, later)], core] = normed_ref[later]
-
     def event_0():
         pairs[(0, 0)].wait_recv()
 
@@ -318,8 +308,11 @@
             pl.when(number == at)(event)
         block = held[number].reshape(2 * half, held.shape[3])
         starts = row_starts(number)
-        cosine = jnp.concatenate([cos_ref[pl.ds(start, half), :] for start in starts], axis=0)
-        sine = jnp.concatenate([sin_ref[pl.ds(start, half), :] for start in starts], axis=0)
+        table = jnp.concatenate([table_ref[pl.ds(start, half), :] for start in starts], axis=0)
+        swapped = pltpu.roll(table, HD // 2, 1)
+        low = lax.broadcasted_iota(jnp.int32, table.shape, 1) < HD // 2
+        cosine = jnp.where(low, table, swapped)
+        sine = jnp.where(low, -swapped, table)
 
         def turned(product):
             return (product * cosine + pltpu.roll(product, HD // 2, 1) * sine).astype(jnp.bfloat16)
@@ -366,10 +359,10 @@
         along_x[0].wait_recv()
 
 
-def gather_project(normed, w_query, w_key, w_value, cosine, sine, slots, owner):
-    rows, width = cosine.shape[0], normed.shape[-1]
+def gather_project(tokens, gain, w_query, w_key, w_value, table, slots, owner):
+    rows, width = table.shape[0], tokens.shape[-1]
     heads = w_query.shape[1] // HD
-    half = normed.shape[1]
+    half = tokens.shape[1]
     vmem = pl.BlockSpec(memory_space=pltpu.VMEM)
     dma = pltpu.SemaphoreType.DMA
     shape = jax.ShapeDtypeStruct
@@ -386,6 +379,7 @@
             shape((heads, LEAD, HD), jnp.bfloat16),
         ],
         scratch_shapes=[
+            pltpu.VMEM((2, half, width), jnp.bfloat16),
             pltpu.VMEM((len(UNITS), 2, half, width), jnp.bfloat16),
             dma((6,)),
             dma((len(UNITS),)),
@@ -402,22 +396,28 @@
             collective_id=0, has_side_effects=True, vmem_limit_bytes=LIMIT
         ),
         name="gather_project",
-    )(normed, w_query, w_key, w_value, cosine, sine, slots, owner)
+    )(tokens, gain, w_query, w_key, w_value, table, slots, owner)
 
 
 def local_kernel(
-    first_ref,
+    begin_smem,
     q_ref,
     before_ref,
     here_ref,
     slot_before_ref,
     slot_here_ref,
-    owner_ref,
-    facts_ref,
+    owner_before_ref,
+    owner_here_ref,
+    request_ref,
+    begin_ref,
+    lead_ref,
+    cache_ref,
     out_ref,
-    lead_mix_ref,
-    lead_top_ref,
-    lead_sum_ref,
+    near_mix_ref,
+    near_top_ref,
+    near_sum_ref,
+    long_mix_ref,
+    long_stat_ref,
     window,
     top_ref,
     sum_ref,
@@ -425,114 +425,138 @@
 ):
     step = pl.program_id(0)
     rows = here_ref.shape[1]
-    slots = slot_here_ref.shape[1]
     heads, tile, _ = q_ref.shape
+    chunk = 2 * tile
 
     @pl.when(step == 0)
     def _():
-        window[:, pl.ds(0, rows)] = before_ref[...]
-        window[:, pl.ds(rows, rows)] = here_ref[...]
-        window[:, pl.ds(2 * rows, slots)] = slot_before_ref[...]
-        window[:, pl.ds(2 * rows + slots, slots)] = slot_here_ref[...]
-
-    request = facts_ref[:, 0:1]
-    begin = facts_ref[:, 1:2]
-    index = facts_ref[:, 2:3]
+        window[:, pl.ds(0, tile)] = jnp.zeros((2, tile, HD), jnp.bfloat16)
+        window[:, pl.ds(tile, rows)] = before_ref[...]
+        window[:, pl.ds(tile + rows, rows)] = here_ref[...]
+        long_state(lead_ref, cache_ref, long_mix_ref, long_stat_ref)
+
+    def column(ref):
+        spread = jnp.broadcast_to(ref[...].astype(jnp.float32), (tile, tile))
+        return jnp.concatenate([jnp.transpose(spread).astype(jnp.int32)] * 2, axis=1)
+
+    request = column(request_ref)
+    begin = column(begin_ref)
+    lanes = lax.broadcasted_iota(jnp.int32, (tile, chunk), 1)
+    index = rows + step * tile + lax.broadcasted_iota(jnp.int32, (tile, chunk), 0)
 
     def take(keys, values, valid, fresh):
-        for head in range(heads):
-            scores = jnp.where(valid, dot_t(q_ref[head], keys) * SCALE, LOW)
-            top = jnp.max(scores, axis=1, keepdims=True)
-            if not fresh:
-                old = top_ref[head]
-                top = jnp.maximum(top, old)
-                keep = jnp.exp(old - top)
-            weights = jnp.exp(scores - top)
-            total = jnp.sum(weights, axis=1, keepdims=True)
-            mixed = dot32(weights.astype(jnp.bfloat16), values)
-            top_ref[head] = top
-            if fresh:
-                sum_ref[head] = total
-                mix_ref[head] = mixed
-            else:
-                sum_ref[head] = sum_ref[head] * keep + total
-                mix_ref[head] = mix_ref[head] * keep + mixed
+        scores = dot_t(q_ref[...].reshape(heads * tile, HD), keys) * SCALE
+        scores = jnp.where(jnp.concatenate([valid] * heads, axis=0), scores, LOW)
+        top = jnp.max(scores, axis=1, keepdims=True)
+        if not fresh:
+            old = top_ref[...]
+            top = jnp.maximum(top, old)
+            keep = jnp.exp(old - top)
+        weights = jnp.exp(scores - top)
+        total = jnp.sum(weights, axis=1, keepdims=True)
+        mixed = dot32(weights.astype(jnp.bfloat16), values)
+        top_ref[...] = top
+        if fresh:
+            sum_ref[...] = total
+            mix_ref[...] = mixed
+        else:
+            sum_ref[...] = sum_ref[...] * keep + total
+            mix_ref[...] = mix_ref[...] * keep + mixed
+
+    end = rows + (step + 1) * tile
 
     def new_chunk(number, fresh):
-        at = pl.multiple_of(number * tile, tile)
-        key_at = at + lax.broadcasted_iota(jnp.int32, (tile, tile), 1)
+        key = end - (number + 1) * chunk
+        key_at = key + lanes
         valid = (key_at >= begin) & (key_at <= index)
-        take(window[0, pl.ds(at, tile), :], window[1, pl.ds(at, tile), :], valid, fresh)
-
-    last = rows // tile + step
-    new_chunk(last, True)
-    first = first_ref[step]
-
-    @pl.loop(first, last)
+        at = pl.multiple_of(key + tile, tile)
+        take(window[0, pl.ds(at, chunk), :], window[1, pl.ds(at, chunk), :], valid, fresh)
+
+    first = begin_smem[step * tile]
+    last = begin_smem[step * tile + tile - 1]
+    new_chunk(0, True)
+
+    @pl.loop(1, (end - first + chunk - 1) // chunk)
     def _(number):
         new_chunk(number, False)
 
-    valid = owner_ref[...] == request
-    take(window[0, pl.ds(2 * rows, 2 * slots), :], window[1, pl.ds(2 * rows, 2 * slots), :], valid, False)
+    @pl.when(first < rows)
+    def _():
+        take(slot_before_ref[0], slot_before_ref[1], owner_before_ref[...] == request, False)
+
+    @pl.when(last >= rows)
+    def _():
+        take(slot_here_ref[0], slot_here_ref[1], owner_here_ref[...] == request, False)
+
+    mixed = mix_ref[...] / sum_ref[...]
     for head in range(heads):
-        out_ref[:, head * HD : (head + 1) * HD] = (mix_ref[head] / sum_ref[head]).astype(jnp.bfloat16)
+        out_ref[:, head * HD : (head + 1) * HD] = mixed[head * tile : (head + 1) * tile].astype(
+            jnp.bfloat16
+        )
 
     @pl.when(step == 0)
     def _():
-        lead_mix_ref[...] = mix_ref[:, pl.ds(0, LEAD), :]
-        lead_top_ref[...] = jnp.broadcast_to(top_ref[:, pl.ds(0, LEAD), :], lead_top_ref.shape)
-        lead_sum_ref[...] = jnp.broadcast_to(sum_ref[:, pl.ds(0, LEAD), :], lead_sum_ref.shape)
-
-
-def local_attention(first, queries, before, here, slot_before, slot_here, owner, facts):
+        for head in range(heads):
+            lead = pl.ds(head * tile, LEAD)
+            near_mix_ref[head] = mix_ref[lead, :]
+            near_top_ref[head] = jnp.broadcast_to(top_ref[lead, :], (LEAD, HD))
+            near_sum_ref[head] = jnp.broadcast_to(sum_ref[lead, :], (LEAD, HD))
+
+
+def long_state(q_ref, cache_ref, mix_ref, stat_ref):
+    heads = q_ref.shape[0]
+    queries = jnp.concatenate([q_ref[at] for at in range(heads)] + [q_ref[heads - 1]], axis=0)
+    scores = dot_t(cache_ref[0], queries) * SCALE
+    top = jnp.max(scores, axis=0, keepdims=True)
+    weights = jnp.exp(scores - top)
+    mixed = lax.dot_general(
+        cache_ref[1],
+        weights.astype(jnp.bfloat16),
+        (((0,), (0,)), ((), ())),
+        preferred_element_type=jnp.float32,
+    )
+    mix_ref[...] = mixed.astype(jnp.bfloat16)
+    stat_ref[...] = jnp.zeros_like(stat_ref)
+    stat_ref[0:1, :] = top
+    stat_ref[1:2, :] = jnp.sum(weights, axis=0, keepdims=True)
+
+
+def local_attention(
+    begin, queries, before, here, slot_before, slot_here, owner_before, owner_here, request, lead, cache
+):
     heads, rows, _ = queries.shape
-    slots = slot_here.shape[1]
-    tile = TILE
+    tile = HD
+    columns = (heads + 1) * LEAD
 
     def whole(array):
-        return pl.BlockSpec(array.shape, lambda i, first: (0,) * array.ndim)
-
-    lead_shape = jax.ShapeDtypeStruct((heads, LEAD, HD), jnp.float32)
+        return pl.BlockSpec(array.shape, lambda i, first: (0,) * len(array.shape))
+
+    shape = jax.ShapeDtypeStruct
+    near = shape((heads, LEAD, HD), jnp.float32)
+    long_mix = shape((HD, columns), jnp.bfloat16)
+    long_stat = shape((8, columns), jnp.float32)
+    row = pl.BlockSpec((1, tile), lambda i, first: (0, i))
+    kept = [before, here, slot_before, slot_here, owner_before, owner_here]
     return pl.pallas_call(
         local_kernel,
         grid_spec=pltpu.PrefetchScalarGridSpec(
             num_scalar_prefetch=1,
             grid=(rows // tile,),
-            in_specs=[
-                pl.BlockSpec((heads, tile, HD), lambda i, first: (0, i, 0)),
-                whole(before),
-                whole(here),
-                whole(slot_before),
-                whole(slot_here),
-                whole(owner),
-                pl.BlockSpec((tile, facts.shape[1]), lambda i, first: (i, 0)),
-            ],
-            out_specs=[
-                pl.BlockSpec((tile, heads * HD), lambda i, first: (i, 0)),
-                whole(lead_shape),
-                whole(lead_shape),
-                whole(lead_shape),
-            ],
+            in_specs=[pl.BlockSpec((heads, tile, HD), lambda i, first: (0, i, 0))]
+            + [whole(array) for array in kept]
+            + [row, row, whole(lead), whole(cache)],
+            out_specs=[pl.BlockSpec((tile, heads * HD), lambda i, first: (i, 0))]
+            + [whole(array) for array in (near, near, near, long_mix, long_stat)],
             scratch_shapes=[
-                pltpu.VMEM((2, 2 * rows + 2 * slots, HD), jnp.bfloat16),
-                pltpu.VMEM((heads, tile, 1), jnp.float32),
-                pltpu.VMEM((heads, tile, 1), jnp.float32),
-                pltpu.VMEM((heads, tile, HD), jnp.float32),
+                pltpu.VMEM((2, tile + 2 * rows, HD), jnp.bfloat16),
+                pltpu.VMEM((heads * tile, 1), jnp.float32),
+                pltpu.VMEM((heads * tile, 1), jnp.float32),
+                pltpu.VMEM((heads * tile, HD), jnp.float32),
             ],
         ),
-        out_shape=[
-            jax.ShapeDtypeStruct((rows, heads * HD), jnp.bfloat16),
-            lead_shape,
-            lead_shape,
-            lead_shape,
-        ],
-        cost_estimate=pl.CostEstimate(
-            flops=4 * heads * rows * (rows + 2 * slots) * HD,
-            bytes_accessed=8 * rows * HD * heads,
-            transcendentals=heads * rows * (rows + 2 * slots),
-        ),
+        out_shape=[shape((rows, heads * HD), jnp.bfloat16), near, near, near, long_mix, long_stat],
         name="local_attention",
-    )(first, queries, before, here, slot_before, slot_here, owner, facts)
+    )(begin, queries, *kept, request[None, :], begin[None, :], lead, cache)
 
 
 def merge(into, top, total, part, part_top, part_total):
@@ -547,8 +571,8 @@
 def scatter_kernel(
     attended_ref,
     w_ref,
-    q_ref,
-    cache_ref,
+    long_mix_ref,
+    long_stat_ref,
     near_mix_ref,
     near_top_ref,
     near_sum_ref,
@@ -577,7 +601,7 @@
     left = (seq, lax.rem(y - way + Y, Y) * 2 + core)
     pair = (seq, head + way)
     half = ring_out.shape[2]
-    heads = q_ref.shape[0]
+    heads = near_mix_ref.shape[0]
     width = w_ref.shape[1] // PIECES
     barrier = pltpu.get_barrier_semaphore()
 
@@ -658,31 +682,12 @@
         pair_copy(1, piece).wait_recv()
         pass_on(1, 0, piece, chip_sum(1, 3, piece))
 
-    rows = stack(1)
-    for piece in range(PIECES):
-        project(rows, 1, piece)
-        pair_copy(1, piece).start()
-        if piece:
-            first_hop(piece - 1)
-    first_hop(PIECES - 1)
-
-    queries = jnp.concatenate([q_ref[at] for at in range(heads)] + [q_ref[heads - 1]], axis=0)
-    scores = dot_t(cache_ref[0], queries) * SCALE
-    top = jnp.max(scores, axis=0, keepdims=True)
-    weights = jnp.exp(scores - top)
-    mixed = lax.dot_general(
-        cache_ref[1],
-        weights.astype(jnp.bfloat16),
-        (((0,), (0,)), ((), ())),
-        preferred_element_type=jnp.float32,
-    )
-
     def keep_state(mixed, top, total):
         mix_out[...] = mixed.astype(jnp.bfloat16)
         stat_out[0:1, :] = top
         stat_out[1:2, :] = total
 
-    def state_copies(slot, to):
+    def state_copies(slot, to, sources):
         return [
             pltpu.make_async_remote_copy(
                 src_ref=source,
@@ -692,13 +697,14 @@
                 device_id=(to, head),
                 device_id_type=MESH,
             )
-            for number, (source, target) in enumerate([(mix_out, mix_in), (stat_out, stat_in)])
+            for number, (source, target) in enumerate(zip(sources, (mix_in, stat_in)))
         ]
 
-    def collect(slots):
-        state = (mix_out[...].astype(jnp.float32), stat_out[0:1, :], stat_out[1:2, :])
+    def collect(slots, sources):
+        mix, stat = sources
+        state = (mix[...].astype(jnp.float32), stat[0:1, :], stat[1:2, :])
         for slot in slots:
-            for copy in state_copies(slot, jnp.int32(0)):
+            for copy in state_copies(slot, jnp.int32(0), sources):
                 copy.wait_recv()
             state = merge(
                 *state,
@@ -706,16 +712,23 @@
                 stat_in[slot, 0:1, :],
                 stat_in[slot, 1:2, :],
             )
-            state = (state[0], state[1], state[2])
         return state
 
-    stat_out[...] = jnp.zeros_like(stat_out)
-    keep_state(mixed, top, jnp.sum(weights, axis=0, keepdims=True))
+    computed = (long_mix_ref, long_stat_ref)
+    merged = (mix_out, stat_out)
     for at in range(1, Z):
         @pl.when(z == at)
         def _():
-            for copy in state_copies(at - 1, x * Z):
+            for copy in state_copies(at - 1, x * Z, computed):
                 copy.start()
+
+    rows = stack(1)
+    for piece in range(PIECES):
+        project(rows, 1, piece)
+        pair_copy(1, piece).start()
+        if piece:
+            first_hop(piece - 1)
+    first_hop(PIECES - 1)
 
     rows = stack(0)
     for piece in range(PIECES):
@@ -726,12 +739,13 @@
 
     @pl.when(z == 0)
     def _():
-        keep_state(*collect(range(Z - 1)))
+        stat_out[...] = jnp.zeros_like(stat_out)
+        keep_state(*collect(range(Z - 1), computed))
 
     for at in range(1, n_x):
         @pl.when((z == 0) & (x == at))
         def _():
-            for copy in state_copies(Z - 2 + at, jnp.int32(0)):
+            for copy in state_copies(Z - 2 + at, jnp.int32(0), merged):
                 copy.start()
 
     for piece in range(PIECES):
@@ -739,7 +753,7 @@
 
     @pl.when(seq == 0)
     def _():
-        mixed, top, total = collect(range(Z - 1, Z + n_x - 2))
+        mixed, top, total = collect(range(Z - 1, Z + n_x - 2), merged)
         mixed = jnp.transpose(mixed)
         top = jnp.transpose(jnp.broadcast_to(top, mix_out.shape))
         total = jnp.transpose(jnp.broadcast_to(total, mix_out.shape))
@@ -792,16 +806,16 @@
 
     @pl.when(seq > 0)
     def _():
-        for copy in state_copies(0, jnp.int32(0)):
+        for copy in state_copies(0, jnp.int32(0), merged):
             copy.wait_send()
 
 
-def project_scatter(attended, w_out, lead_queries, cache, near_mix, near_top, near_sum):
+def project_scatter(attended, w_out, long_mix, long_stat, near_mix, near_top, near_sum):
     rows, inner = attended.shape
     width = w_out.shape[1]
     half = LEAD
     slots = Z - 1 + 3
-    queries = (lead_queries.shape[0] + 1) * LEAD
+    queries = long_mix.shape[1]
     vmem = pl.BlockSpec(memory_space=pltpu.VMEM)
     dma = pltpu.SemaphoreType.DMA
     return pl.pallas_call(
@@ -830,7 +844,7 @@
             collective_id=1, has_side_effects=True, vmem_limit_bytes=LIMIT
         ),
         name="project_scatter",
-    )(attended, w_out, lead_queries, cache, near_mix, near_top, near_sum)
+    )(attended, w_out, long_mix, long_stat, near_mix, near_top, near_sum)
 
 
 def on_device(
@@ -848,30 +862,37 @@
 ):
     seq_index = lax.axis_index("seq")
     long_len = long_cache.shape[1] * lax.axis_size("seq")
-    heads = w_query.shape[1] // HD
     rows = tokens.shape[0] * lax.axis_size("head")
     starts = request_starts(new_len)
     token_index = seq_index * rows + jnp.arange(rows, dtype=jnp.int32)
     request, begin, position = token_facts(token_index, starts, cache_len, long_len)
-    cosine, sine = rotate_tables(position)
-    normed = normalize(tokens, norm_gain).reshape(2, LEAD, tokens.shape[1])
+    table = rotate_table(position)
     queries, here, before, earlier_slots, earlier_owner, lead_queries = gather_project(
-        normed, w_query, w_key, w_value, cosine, sine, short_cache, slot_owner[None, :]
+        tokens.reshape(2, LEAD, tokens.shape[1]),
+        norm_gain[None, :],
+        w_query,
+        w_key,
+        w_value,
+        table,
+        short_cache,
+        slot_owner[None, :],
     )
-
     shift = (seq_index - 1) * rows
-    window_begin = jnp.maximum(begin - shift, 0)
-    window_index = token_index - shift
-    window_begin = jnp.where(request == starts.shape[0], -shift, window_begin)
-    facts = jnp.stack([request, window_begin, window_index] + [window_index] * 5, axis=1)
-    owner = jnp.concatenate([jnp.where(seq_index > 0, earlier_owner[0], -1), slot_owner])[None, :]
-    first = window_begin[::TILE] // TILE
-    attended, lead_mix, lead_top, lead_sum = local_attention(
-        first, queries, before, here, earlier_slots, short_cache, owner, facts
+    window_begin = jnp.where(request == starts.shape[0], rows, jnp.maximum(begin - shift, 0))
+    attended, near_mix, near_top, near_sum, long_mix, long_stat = local_attention(
+        window_begin,
+        queries,
+        before,
+        here,
+        earlier_slots,
+        short_cache,
+        earlier_owner,
+        slot_owner[None, :],
+        request,
+        lead_queries,
+        long_cache,
     )
-    return project_scatter(
-        attended, w_out, lead_queries, long_cache, lead_mix, lead_top, lead_sum
-    )
+    return project_scatter(attended, w_out, long_mix, long_stat, near_mix, near_top, near_sum)
 
 
 def solution(mesh):

time: 130 us -> 123 us (0.946)
  other arithmetic: 9.83 us -> 5.84 us
  Pallas kernels: 116 us -> 114 us
    pallas_call x1, Pallas kernels: 46.9 us -> 43.6 us  [project_scatter(): pl.pallas_call(scatter_kernel, in_specs=[vmem] * 7, out_specs=vmem, out_s...]
    convert_element_type x1 -> x0, other arithmetic: 2.28 us -> none  [normalize(): (values * lax.rsqrt(mean_square + 1e-05) * norm_gain).astype(jnp.bfloat16)]
    pallas_call x1, Pallas kernels: 18.6 us -> 20.9 us  [local_attention(): pl.pallas_call(local_kernel, grid_spec=pltpu.PrefetchScalarGridSpec(num_s...]
    neg x1 -> x0, other arithmetic: 1.9 us -> none  [rotate_tables(): -sine]
    cos x0 -> x1, other arithmetic: none -> 1.88 us  [rotate_table(): return jnp.concatenate([jnp.cos(angle), jnp.sin(angle)], axis=1)]
    reduce_sum x1 -> x0, other arithmetic: 1.37 us -> none  [normalize(): mean_square = jnp.mean(values * values, axis=-1, keepdims=True)]
where the time goes in v4:
time: 123 us
  Pallas kernels  114 us (93%)
  other arithmetic  5.84 us (5%)
  local copies, waits for them, and re-layouts  2.81 us (2%)
    pallas_call x1, Pallas kernels, gather_project(): pl.pallas_call(gather_kernel, in_specs=[vmem] * 8, out_specs=[vmem] * 6,...  49.8 us
    pallas_call x1, Pallas kernels, project_scatter(): pl.pallas_call(scatter_kernel, in_specs=[vmem] * 7, out_specs=vmem, out_s...  43.6 us
    pallas_call x1, Pallas kernels, local_attention(): pl.pallas_call(local_kernel, grid_spec=pltpu.PrefetchScalarGridSpec(num_s...  20.9 us

profile of v4, /device:TPU:1, one launch (start us, length us, event | category | flops | bytes accessed | tf_op | source)
XLA Modules:
  0.0 123.0 jit_solution(13338745527577772624)
XLA Ops:
  0.0 0.7 copy.14
  0.8 0.1 reduce-window.9
  0.9 0.1 add_reduce_fusion
  1.0 0.7 sub.33
  1.6 0.1 convert_reduce_fusion
  1.8 0.8 select_reduce_fusion
  2.5 0.6 fusion.2
  3.1 0.6 compare_select_fusion.1
  3.7 1.9 %multiply_cosine_fusion = (f32[1024,64]{1,0:T(8,128)S(1)}, f32[1024,64]{1,0:T(8,128)S(1)}) fusion(f32[64]{0:T(128)S(1)} %multiply_exponential_fusion, f32[1024]{0:T(1024)S(1)} %get-tuple-element.33), kind=kLoop, calls=%fused_computation.1 | loop fusion | flops 65536 | bytes 528640 | tf_op jit(solution)/shard_map/cos | solution.py:43
  5.6 1.0 pad_maximum_fusion.table_ref
  6.6 49.8 %gather_project.1 = (bf16[3,1024,128]{2,1,0:T(8,128)(2,1)}, bf16[2,1024,128]{2,1,0:T(8,128)(2,1)}, bf16[2,1024,128]{2,1,0:T(8,128)(2,1)}, bf16[2,256,128]{2,1,0:...) custom-call(bf16[2,64,3072]{2,1,0:T(8,128)(2,1)} %bitcast.6, f32[1,3072]{1,0:T(1,128)} %bitcast.9, ...), custom_call_target="tpu_custom_call" | custom-call | tf_op jit(solution)/shard_map/gather_project/pallas_call | solution.py:369
  56.4 20.9 %local_attention.1 = (bf16[1024,384]{1,0:T(8,128)(2,1)}, f32[3,64,128]{2,1,0:T(8,128)}, f32[3,64,128]{2,1,0:T(8,128)}, f32[3,64,128]{2,1,0:T(8,128)}, bf16[128,256]{1,0:T(8,128)(2,1)}, /*index=5*/f32[8,256]{1,0:T(8,128)}) custom-call(s32[1024]{0:T(1024)} %get-tuple-element.31.begin_smem, bf16[3,1024,128]{2,1,0:T(8,128)(2,1)} %get-tuple-element.17.q_ref, ...), custom_call_target="tpu_custom_call" | custom-call | tf_op jit(solution)/shard_map/local_attention/pallas_call | solution.py:540
  77.4 43.6 %project_scatter.1 = bf16[128,3072]{1,0:T(8,128)(2,1)} custom-call(bf16[1024,384]{1,0:T(8,128)(2,1)} %get-tuple-element.23.attended_ref, bf16[384,3072]{1,0:T(8,128)(2,1)} %w_ref.1, bf16[128,256]{1,0:T(8,128)(2,1)} %get-tuple-element.24.long_mix_ref, f32[8,256]{1,0:T(8,128)} %get-tuple-element.25.long_stat_ref, ...), custom_call_target="tpu_custom_call" | custom-call | tf_op jit(solution)/shard_map/project_scatter/pallas_call | solution.py:821
  120.9 2.1 %copy.16 = bf16[128,3072]{1,0:T(8,128)(2,1)} copy(bf16[128,3072]{1,0:T(8,128)(2,1)} %project_scatter.1) | data formatting | bytes 1572864
  (3 shorter events, 0.0 us)

commit v5 on v4

--- a/solution.py
+++ b/solution.py
@@ -414,8 +414,7 @@
     cache_ref,
     out_ref,
     near_mix_ref,
-    near_top_ref,
-    near_sum_ref,
+    near_stat_ref,
     long_mix_ref,
     long_stat_ref,
     window,
@@ -435,26 +434,28 @@
         window[:, pl.ds(tile + rows, rows)] = here_ref[...]
         long_state(lead_ref, cache_ref, long_mix_ref, long_stat_ref)
 
-    def column(ref):
-        spread = jnp.broadcast_to(ref[...].astype(jnp.float32), (tile, tile))
-        return jnp.concatenate([jnp.transpose(spread).astype(jnp.int32)] * 2, axis=1)
-
-    request = column(request_ref)
-    begin = column(begin_ref)
-    lanes = lax.broadcasted_iota(jnp.int32, (tile, chunk), 1)
-    index = rows + step * tile + lax.broadcasted_iota(jnp.int32, (tile, chunk), 0)
+    request = request_ref[...]
+    begin = begin_ref[...]
+    down = lax.broadcasted_iota(jnp.int32, (chunk, tile), 0)
+    index = rows + step * tile + lax.broadcasted_iota(jnp.int32, (1, tile), 1)
+    queries = q_ref[...].reshape(heads * tile, HD)
 
     def take(keys, values, valid, fresh):
-        scores = dot_t(q_ref[...].reshape(heads * tile, HD), keys) * SCALE
-        scores = jnp.where(jnp.concatenate([valid] * heads, axis=0), scores, LOW)
-        top = jnp.max(scores, axis=1, keepdims=True)
+        scores = dot_t(keys, queries) * SCALE
+        scores = jnp.where(jnp.concatenate([valid] * heads, axis=1), scores, LOW)
+        top = jnp.max(scores, axis=0, keepdims=True)
         if not fresh:
             old = top_ref[...]
             top = jnp.maximum(top, old)
             keep = jnp.exp(old - top)
         weights = jnp.exp(scores - top)
-        total = jnp.sum(weights, axis=1, keepdims=True)
-        mixed = dot32(weights.astype(jnp.bfloat16), values)
+        total = jnp.sum(weights, axis=0, keepdims=True)
+        mixed = lax.dot_general(
+            values,
+            weights.astype(jnp.bfloat16),
+            (((0,), (0,)), ((), ())),
+            preferred_element_type=jnp.float32,
+        )
         top_ref[...] = top
         if fresh:
             sum_ref[...] = total
@@ -463,11 +464,15 @@
             sum_ref[...] = sum_ref[...] * keep + total
             mix_ref[...] = mix_ref[...] * keep + mixed
 
+    def owner_column(ref):
+        spread = jnp.broadcast_to(ref[...].astype(jnp.float32), (tile, ref.shape[1]))
+        return jnp.transpose(spread).astype(jnp.int32)
+
     end = rows + (step + 1) * tile
 
     def new_chunk(number, fresh):
         key = end - (number + 1) * chunk
-        key_at = key + lanes
+        key_at = key + down
         valid = (key_at >= begin) & (key_at <= index)
         at = pl.multiple_of(key + tile, tile)
         take(window[0, pl.ds(at, chunk), :], window[1, pl.ds(at, chunk), :], valid, fresh)
@@ -482,25 +487,27 @@
 
     @pl.when(first < rows)
     def _():
-        take(slot_before_ref[0], slot_before_ref[1], owner_before_ref[...] == request, False)
+        take(slot_before_ref[0], slot_before_ref[1], owner_column(owner_before_ref) == request, False)
 
     @pl.when(last >= rows)
     def _():
-        take(slot_here_ref[0], slot_here_ref[1], owner_here_ref[...] == request, False)
+        take(slot_here_ref[0], slot_here_ref[1], owner_column(owner_here_ref) == request, False)
 
     mixed = mix_ref[...] / sum_ref[...]
     for head in range(heads):
-        out_ref[:, head * HD : (head + 1) * HD] = mixed[head * tile : (head + 1) * tile].astype(
-            jnp.bfloat16
-        )
+        span = slice(head * tile, (head + 1) * tile)
+        out_ref[:, span] = jnp.transpose(mixed[:, span]).astype(jnp.bfloat16)
 
     @pl.when(step == 0)
     def _():
-        for head in range(heads):
-            lead = pl.ds(head * tile, LEAD)
-            near_mix_ref[head] = mix_ref[lead, :]
-            near_top_ref[head] = jnp.broadcast_to(top_ref[lead, :], (LEAD, HD))
-            near_sum_ref[head] = jnp.broadcast_to(sum_ref[lead, :], (LEAD, HD))
+        def leads(ref):
+            parts = [ref[:, head * tile : head * tile + LEAD] for head in range(heads)]
+            return jnp.concatenate(parts + parts[-1:], axis=1)
+
+        near_mix_ref[...] = leads(mix_ref)
+        near_stat_ref[...] = jnp.zeros_like(near_stat_ref)
+        near_stat_ref[0:1, :] = leads(top_ref)
+        near_stat_ref[1:2, :] = leads(sum_ref)
 
 
 def long_state(q_ref, cache_ref, mix_ref, stat_ref):
@@ -532,7 +539,7 @@
         return pl.BlockSpec(array.shape, lambda i, first: (0,) * len(array.shape))
 
     shape = jax.ShapeDtypeStruct
-    near = shape((heads, LEAD, HD), jnp.float32)
+    near_mix = shape((HD, columns), jnp.float32)
     long_mix = shape((HD, columns), jnp.bfloat16)
     long_stat = shape((8, columns), jnp.float32)
     row = pl.BlockSpec((1, tile), lambda i, first: (0, i))
@@ -546,15 +553,15 @@
             + [whole(array) for array in kept]
             + [row, row, whole(lead), whole(cache)],
             out_specs=[pl.BlockSpec((tile, heads * HD), lambda i, first: (i, 0))]
-            + [whole(array) for array in (near, near, near, long_mix, long_stat)],
+            + [whole(array) for array in (near_mix, long_stat, long_mix, long_stat)],
             scratch_shapes=[
                 pltpu.VMEM((2, tile + 2 * rows, HD), jnp.bfloat16),
-                pltpu.VMEM((heads * tile, 1), jnp.float32),
-                pltpu.VMEM((heads * tile, 1), jnp.float32),
-                pltpu.VMEM((heads * tile, HD), jnp.float32),
+                pltpu.VMEM((1, heads * tile), jnp.float32),
+                pltpu.VMEM((1, heads * tile), jnp.float32),
+                pltpu.VMEM((HD, heads * tile), jnp.float32),
             ],
         ),
-        out_shape=[shape((rows, heads * HD), jnp.bfloat16), near, near, near, long_mix, long_stat],
+        out_shape=[shape((rows, heads * HD), jnp.bfloat16), near_mix, long_stat, long_mix, long_stat],
         name="local_attention",
     )(begin, queries, *kept, request[None, :], begin[None, :], lead, cache)
 
@@ -574,8 +581,7 @@
     long_mix_ref,
     long_stat_ref,
     near_mix_ref,
-    near_top_ref,
-    near_sum_ref,
+    near_stat_ref,
     out_ref,
     pair_out,
     pair_in,
@@ -601,7 +607,7 @@
     left = (seq, lax.rem(y - way + Y, Y) * 2 + core)
     pair = (seq, head + way)
     half = ring_out.shape[2]
-    heads = near_mix_ref.shape[0]
+    heads = w_ref.shape[0] // HD
     width = w_ref.shape[1] // PIECES
     barrier = pltpu.get_barrier_semaphore()
 
@@ -753,22 +759,10 @@
 
     @pl.when(seq == 0)
     def _():
-        mixed, top, total = collect(range(Z - 1, Z + n_x - 2), merged)
-        mixed = jnp.transpose(mixed)
-        top = jnp.transpose(jnp.broadcast_to(top, mix_out.shape))
-        total = jnp.transpose(jnp.broadcast_to(total, mix_out.shape))
-        parts = []
-        for at in range(heads):
-            lead = slice(at * LEAD, (at + 1) * LEAD)
-            joined = merge(
-                near_mix_ref[at],
-                near_top_ref[at],
-                near_sum_ref[at],
-                mixed[lead],
-                top[lead],
-                total[lead],
-            )
-            parts.append((joined[0] / joined[2]).astype(jnp.bfloat16))
+        near = (near_mix_ref[...], near_stat_ref[0:1, :], near_stat_ref[1:2, :])
+        mixed, _, total = merge(*near, *collect(range(Z - 1, Z + n_x - 2), merged))
+        mixed = jnp.transpose(mixed / total).astype(jnp.bfloat16)
+        parts = [mixed[at * LEAD : (at + 1) * LEAD] for at in range(heads)]
         lead_rows = jnp.concatenate(parts, axis=1)
         for piece in range(PIECES):
             product = dot32(lead_rows, w_ref[:, columns(piece)]).astype(jnp.bfloat16)
@@ -810,7 +804,7 @@
             copy.wait_send()
 
 
-def project_scatter(attended, w_out, long_mix, long_stat, near_mix, near_top, near_sum):
+def project_scatter(attended, w_out, long_mix, long_stat, near_mix, near_stat):
     rows, inner = attended.shape
     width = w_out.shape[1]
     half = LEAD
@@ -820,7 +814,7 @@
     dma = pltpu.SemaphoreType.DMA
     return pl.pallas_call(
         scatter_kernel,
-        in_specs=[vmem] * 7,
+        in_specs=[vmem] * 6,
         out_specs=vmem,
         out_shape=jax.ShapeDtypeStruct((2 * half, width), jnp.bfloat16),
         scratch_shapes=[
@@ -844,7 +838,7 @@
             collective_id=1, has_side_effects=True, vmem_limit_bytes=LIMIT
         ),
         name="project_scatter",
-    )(attended, w_out, long_mix, long_stat, near_mix, near_top, near_sum)
+    )(attended, w_out, long_mix, long_stat, near_mix, near_stat)
 
 
 def on_device(
@@ -879,7 +873,7 @@
     )
     shift = (seq_index - 1) * rows
     window_begin = jnp.where(request == starts.shape[0], rows, jnp.maximum(begin - shift, 0))
-    attended, near_mix, near_top, near_sum, long_mix, long_stat = local_attention(
+    attended, near_mix, near_stat, long_mix, long_stat = local_attention(
         window_begin,
         queries,
         before,
@@ -892,7 +886,7 @@
         lead_queries,
         long_cache,
     )
-    return project_scatter(attended, w_out, long_mix, long_stat, near_mix, near_top, near_sum)
+    return project_scatter(attended, w_out, long_mix, long_stat, near_mix, near_stat)
 
 
 def solution(mesh):

time: 123 us -> 114 us (0.927)
  Pallas kernels: 114 us -> 105 us
    pallas_call x1, Pallas kernels: 20.9 us -> 16.1 us  [local_attention(): pl.pallas_call(local_kernel, grid_spec=pltpu.PrefetchScalarGridSpec(num_s...]
    pallas_call x1, Pallas kernels: 43.6 us -> 39.5 us  [project_scatter(): pl.pallas_call(scatter_kernel, in_specs=[vmem] * 6, out_specs=vmem, out_s...]
where the time goes in v5:
time: 114 us
  Pallas kernels  105 us (92%)
  other arithmetic  5.86 us (5%)
  local copies, waits for them, and re-layouts  2.81 us (2%)
    pallas_call x1, Pallas kernels, gather_project(): pl.pallas_call(gather_kernel, in_specs=[vmem] * 8, out_specs=[vmem] * 6,...  49.8 us
    pallas_call x1, Pallas kernels, project_scatter(): pl.pallas_call(scatter_kernel, in_specs=[vmem] * 6, out_specs=vmem, out_s...  39.5 us
    pallas_call x1, Pallas kernels, local_attention(): pl.pallas_call(local_kernel, grid_spec=pltpu.PrefetchScalarGridSpec(num_s...  16.1 us

profile of v5, /device:TPU:1, one launch (start us, length us, event | category | flops | bytes accessed | tf_op | source)
XLA Modules:
  0.0 114.2 jit_solution(17426182912836859304)
XLA Ops:
  0.0 0.7 copy.14
  0.8 0.1 reduce-window.9
  0.9 0.1 add_reduce_fusion
  1.0 0.7 sub.33
  1.6 0.1 convert_reduce_fusion
  1.8 0.8 select_reduce_fusion
  2.5 0.6 fusion.2
  3.2 0.6 compare_select_fusion.1
  3.8 1.9 %multiply_cosine_fusion = (f32[1024,64]{1,0:T(8,128)S(1)}, f32[1024,64]{1,0:T(8,128)S(1)}) fusion(f32[64]{0:T(128)S(1)} %multiply_exponential_fusion, f32[1024]{0:T(1024)S(1)} %get-tuple-element.31), kind=kLoop, calls=%fused_computation.1 | loop fusion | flops 65536 | bytes 528640 | tf_op jit(solution)/shard_map/cos | solution.py:43
  5.6 1.0 pad_maximum_fusion.table_ref
  6.6 49.8 %gather_project.1 = (bf16[3,1024,128]{2,1,0:T(8,128)(2,1)}, bf16[2,1024,128]{2,1,0:T(8,128)(2,1)}, bf16[2,1024,128]{2,1,0:T(8,128)(2,1)}, bf16[2,256,128]{2,1,0:...) custom-call(bf16[2,64,3072]{2,1,0:T(8,128)(2,1)} %bitcast.6, f32[1,3072]{1,0:T(1,128)} %bitcast.9, ...), custom_call_target="tpu_custom_call" | custom-call | tf_op jit(solution)/shard_map/gather_project/pallas_call | solution.py:369
  56.5 16.1 %local_attention.1 = (bf16[1024,384]{1,0:T(8,128)(2,1)}, f32[128,256]{1,0:T(8,128)}, f32[8,256]{1,0:T(8,128)}, bf16[128,256]{1,0:T(8,128)(2,1)}, f32[8,256]{1,0:T(8,128)}) custom-call(s32[1024]{0:T(1024)} %get-tuple-element.29.begin_smem, bf16[3,1024,128]{2,1,0:T(8,128)(2,1)} %get-tuple-element.16.q_ref, bf16[2,1024,128]{2,1,0:T(8,128)(2,1)} %get-tuple-element.17.before_ref, ...), custom_call_target="tpu_custom_call" | custom-call | tf_op jit(solution)/shard_map/local_attention/pallas_call | solution.py:547
  72.6 39.5 %project_scatter.1 = bf16[128,3072]{1,0:T(8,128)(2,1)} custom-call(bf16[1024,384]{1,0:T(8,128)(2,1)} %get-tuple-element.22.attended_ref, bf16[384,3072]{1,0:T(8,128)(2,1)} %w_ref.1, bf16[128,256]{1,0:T(8,128)(2,1)} %get-tuple-element.23.long_mix_ref, f32[8,256]{1,0:T(8,128)} %get-tuple-element.24.long_stat_ref, f32[128,256]{1,0:T(8,128)} %get-tuple-element.25.near_mix_ref, ...), custom_call_target="tpu_custom_call" | custom-call | tf_op jit(solution)/shard_map/project_scatter/pallas_call | solution.py:815
  112.1 2.1 %copy.16 = bf16[128,3072]{1,0:T(8,128)(2,1)} copy(bf16[128,3072]{1,0:T(8,128)(2,1)} %project_scatter.1) | data formatting | bytes 1572864
  (3 shorter events, 0.0 us)

commit v6 on v5

--- a/solution.py
+++ b/solution.py
@@ -14,35 +14,12 @@
 LOW = -1e30
 
 
-def request_starts(new_len):
-    return LEAD + jnp.cumsum(new_len) - new_len
-
-
-def token_facts(token_index, starts, cache_len, long_len):
-    number = starts.shape[0]
-    passed = (starts[None, :] <= token_index[:, None]).astype(jnp.int32)
-    request = jnp.sum(passed, axis=1) - 1
-    select = jnp.arange(number, dtype=jnp.int32)[None, :] == request[:, None]
-    begin = jnp.sum(jnp.where(select, starts[None, :], 0), axis=1)
-    cached = jnp.sum(jnp.where(select, cache_len[None, :], 0), axis=1)
-    lead = request < 0
-    position = jnp.where(lead, token_index + long_len, token_index - begin + cached)
-    return jnp.where(lead, number, request), begin, position
-
-
 def normalize(tokens, norm_gain):
     values = tokens.astype(jnp.float32)
     mean_square = jnp.mean(values * values, axis=-1, keepdims=True)
     return (values * lax.rsqrt(mean_square + 1e-05) * norm_gain).astype(jnp.bfloat16)
 
 
-def rotate_table(position):
-    half = HD // 2
-    frequency = jnp.exp(jnp.arange(half, dtype=jnp.float32) * (-2.0 * THETA_LOG / HD))
-    angle = position.astype(jnp.float32)[:, None] * frequency[None, :]
-    return jnp.concatenate([jnp.cos(angle), jnp.sin(angle)], axis=1)
-
-
 def dot32(a, b):
     return jnp.dot(a, b, preferred_element_type=jnp.float32)
 
@@ -55,6 +32,7 @@
 LIMIT = 60 * 1024 * 1024
 Z = 8
 Y = 4
+LONG_ROWS = 1024
 UNITS = [(0, 0), (0, 1), (1, 0), (3, 0), (1, 1), (2, 0), (2, 1), (3, 1)]
 SLOT = {unit: number for number, unit in enumerate(UNITS)}
 
@@ -78,13 +56,46 @@
     )
 
 
+def token_facts(seq, new_len_ref, cache_len_ref, request_ref, begin_ref, place_ref):
+    number = new_len_ref.shape[0]
+    shape = request_ref.shape
+    rows = shape[0] * shape[1]
+    token = (
+        seq * rows
+        + lax.broadcasted_iota(jnp.int32, shape, 0) * shape[1]
+        + lax.broadcasted_iota(jnp.int32, shape, 1)
+    )
+
+    def step(at, carry):
+        start, request, begin, cached = carry
+        passed = token >= start
+        return (
+            start + new_len_ref[at],
+            jnp.where(passed, at, request),
+            jnp.where(passed, start, begin),
+            jnp.where(passed, cache_len_ref[at], cached),
+        )
+
+    zero = jnp.zeros(shape, jnp.int32)
+    _, request, begin, cached = lax.fori_loop(
+        0, number, step, (jnp.int32(LEAD), zero + number, zero, zero)
+    )
+    lead = request == number
+    long_len = lax.axis_size("seq") * LONG_ROWS
+    position = jnp.where(lead, token + long_len, token - begin + cached)
+    place_ref[...] = position.astype(jnp.float32)
+    request_ref[...] = request
+    begin_ref[...] = jnp.where(lead, rows, jnp.maximum(begin - (seq - 1) * rows, 0))
+
+
 def gather_kernel(
     tokens_ref,
     gain_ref,
-    wq_ref,
-    wk_ref,
-    wv_ref,
-    table_ref,
+    wq_hbm,
+    wk_hbm,
+    wv_hbm,
+    new_len_ref,
+    cache_len_ref,
     slots_ref,
     owner_ref,
     q_ref,
@@ -93,7 +104,13 @@
     slots_before_ref,
     owner_before_ref,
     lead_ref,
+    request_ref,
+    begin_ref,
     normed_ref,
+    wq_ref,
+    wkv_ref,
+    table_ref,
+    place_ref,
     held,
     ring_send,
     ring_recv,
@@ -105,8 +122,16 @@
     slot_recv,
     lead_send,
     lead_recv,
+    weight_sem,
 ):
     seq, head, y, core = place()
+    weights = [
+        pltpu.make_async_copy(wk_hbm, wkv_ref.at[:, pl.ds(0, HD)], weight_sem.at[0]),
+        pltpu.make_async_copy(wv_hbm, wkv_ref.at[:, pl.ds(HD, HD)], weight_sem.at[1]),
+        pltpu.make_async_copy(wq_hbm, wq_ref, weight_sem.at[2]),
+    ]
+    for copy in weights:
+        copy.start()
     n_seq = lax.axis_size("seq")
     x, z = seq // Z, lax.rem(seq, Z)
     way = 1 - 2 * core
@@ -246,6 +271,22 @@
     pairs[(0, 1)].start()
     for copy in side:
         copy.start()
+
+    token_facts(seq, new_len_ref, cache_len_ref, request_ref, begin_ref, place_ref)
+    half_head = HD // 2
+    lane = lax.broadcasted_iota(jnp.int32, (HD, HD), 1)
+    entry = jnp.where(lane < half_head, lane, lane - half_head)
+    frequency = jnp.exp(entry.astype(jnp.float32) * (-2.0 * THETA_LOG / HD))
+
+    @pl.loop(0, place_ref.shape[0])
+    def _(number):
+        spread = jnp.broadcast_to(place_ref[pl.ds(number, 1), :], (HD, HD))
+        angle = jnp.transpose(spread) * frequency
+        at = pl.multiple_of(number * HD, HD)
+        table_ref[pl.ds(at, HD), :] = jnp.where(lane < half_head, jnp.cos(angle), jnp.sin(angle))
+
+    for copy in weights:
+        copy.wait()
     def event_0():
         pairs[(0, 0)].wait_recv()
 
@@ -321,7 +362,7 @@
             for part, start in enumerate(starts):
                 ref[at, pl.ds(start, half), :] = rows[part * half : (part + 1) * half]
 
-        both = dot32(block, jnp.concatenate([wk_ref[...], wv_ref[...]], axis=1))
+        both = dot32(block, wkv_ref[...])
         put(kv_ref, 0, turned(both[:, :HD]))
         put(kv_ref, 1, both[:, HD:].astype(jnp.bfloat16))
         product = dot32(block, wq_ref[...])
@@ -359,17 +400,20 @@
         along_x[0].wait_recv()
 
 
-def gather_project(tokens, gain, w_query, w_key, w_value, table, slots, owner):
-    rows, width = table.shape[0], tokens.shape[-1]
+def gather_project(tokens, gain, w_query, w_key, w_value, new_len, cache_len, slots, owner):
+    half, width = tokens.shape[1:]
+    rows = 2 * half * lax.axis_size("head")
     heads = w_query.shape[1] // HD
-    half = tokens.shape[1]
     vmem = pl.BlockSpec(memory_space=pltpu.VMEM)
+    smem = pl.BlockSpec(memory_space=pltpu.SMEM)
+    hbm = pl.BlockSpec(memory_space=pl.ANY)
     dma = pltpu.SemaphoreType.DMA
     shape = jax.ShapeDtypeStruct
+    facts = (rows // HD, HD)
     return pl.pallas_call(
         gather_kernel,
-        in_specs=[vmem] * 8,
-        out_specs=[vmem] * 6,
+        in_specs=[vmem, vmem, hbm, hbm, hbm, smem, smem, vmem, vmem],
+        out_specs=[vmem] * 8,
         out_shape=[
             shape((heads, rows, HD), jnp.bfloat16),
             shape((2, rows, HD), jnp.bfloat16),
@@ -377,9 +421,15 @@
             shape(slots.shape, jnp.bfloat16),
             shape(owner.shape, jnp.int32),
             shape((heads, LEAD, HD), jnp.bfloat16),
+            shape(facts, jnp.int32),
+            shape(facts, jnp.int32),
         ],
         scratch_shapes=[
             pltpu.VMEM((2, half, width), jnp.bfloat16),
+            pltpu.VMEM(w_query.shape, jnp.bfloat16),
+            pltpu.VMEM((width, 2 * HD), jnp.bfloat16),
+            pltpu.VMEM((rows, HD), jnp.float32),
+            pltpu.VMEM(facts, jnp.float32),
             pltpu.VMEM((len(UNITS), 2, half, width), jnp.bfloat16),
             dma((6,)),
             dma((len(UNITS),)),
@@ -391,12 +441,13 @@
             dma((2,)),
             dma((Z + 2,)),
             dma,
+            dma((3,)),
         ],
         compiler_params=pltpu.CompilerParams(
             collective_id=0, has_side_effects=True, vmem_limit_bytes=LIMIT
         ),
         name="gather_project",
-    )(tokens, gain, w_query, w_key, w_value, table, slots, owner)
+    )(tokens, gain, w_query, w_key, w_value, new_len, cache_len, slots, owner)
 
 
 def local_kernel(
@@ -418,6 +469,7 @@
     long_mix_ref,
     long_stat_ref,
     window,
+    owners,
     top_ref,
     sum_ref,
     mix_ref,
@@ -432,10 +484,13 @@
         window[:, pl.ds(0, tile)] = jnp.zeros((2, tile, HD), jnp.bfloat16)
         window[:, pl.ds(tile, rows)] = before_ref[...]
         window[:, pl.ds(tile + rows, rows)] = here_ref[...]
+        for at, ref in enumerate((owner_before_ref, owner_here_ref)):
+            spread = jnp.broadcast_to(ref[...].astype(jnp.float32), (tile, ref.shape[1]))
+            owners[at] = jnp.transpose(spread).astype(jnp.int32)
         long_state(lead_ref, cache_ref, long_mix_ref, long_stat_ref)
 
-    request = request_ref[...]
-    begin = begin_ref[...]
+    request = request_ref[pl.ds(step, 1), :]
+    begin = begin_ref[pl.ds(step, 1), :]
     down = lax.broadcasted_iota(jnp.int32, (chunk, tile), 0)
     index = rows + step * tile + lax.broadcasted_iota(jnp.int32, (1, tile), 1)
     queries = q_ref[...].reshape(heads * tile, HD)
@@ -464,34 +519,28 @@
             sum_ref[...] = sum_ref[...] * keep + total
             mix_ref[...] = mix_ref[...] * keep + mixed
 
-    def owner_column(ref):
-        spread = jnp.broadcast_to(ref[...].astype(jnp.float32), (tile, ref.shape[1]))
-        return jnp.transpose(spread).astype(jnp.int32)
-
     end = rows + (step + 1) * tile
 
-    def new_chunk(number, fresh):
+    def new_chunk(number):
         key = end - (number + 1) * chunk
         key_at = key + down
         valid = (key_at >= begin) & (key_at <= index)
         at = pl.multiple_of(key + tile, tile)
-        take(window[0, pl.ds(at, chunk), :], window[1, pl.ds(at, chunk), :], valid, fresh)
-
-    first = begin_smem[step * tile]
-    last = begin_smem[step * tile + tile - 1]
-    new_chunk(0, True)
+        return window[0, pl.ds(at, chunk), :], window[1, pl.ds(at, chunk), :], valid
+
+    def join(*parts):
+        return [jnp.concatenate(pair, axis=0) for pair in zip(*parts)]
+
+    first = begin_smem[step, 0]
+    take(*join(new_chunk(0), (slot_here_ref[0], slot_here_ref[1], owners[1] == request)), True)
 
     @pl.loop(1, (end - first + chunk - 1) // chunk)
     def _(number):
-        new_chunk(number, False)
+        take(*new_chunk(number), False)
 
     @pl.when(first < rows)
     def _():
-        take(slot_before_ref[0], slot_before_ref[1], owner_column(owner_before_ref) == request, False)
-
-    @pl.when(last >= rows)
-    def _():
-        take(slot_here_ref[0], slot_here_ref[1], owner_column(owner_here_ref) == request, False)
+        take(slot_before_ref[0], slot_before_ref[1], owners[0] == request, False)
 
     mixed = mix_ref[...] / sum_ref[...]
     for head in range(heads):
@@ -542,20 +591,19 @@
     near_mix = shape((HD, columns), jnp.float32)
     long_mix = shape((HD, columns), jnp.bfloat16)
     long_stat = shape((8, columns), jnp.float32)
-    row = pl.BlockSpec((1, tile), lambda i, first: (0, i))
-    kept = [before, here, slot_before, slot_here, owner_before, owner_here]
+    kept = [before, here, slot_before, slot_here, owner_before, owner_here, request, begin, lead, cache]
     return pl.pallas_call(
         local_kernel,
         grid_spec=pltpu.PrefetchScalarGridSpec(
             num_scalar_prefetch=1,
             grid=(rows // tile,),
             in_specs=[pl.BlockSpec((heads, tile, HD), lambda i, first: (0, i, 0))]
-            + [whole(array) for array in kept]
-            + [row, row, whole(lead), whole(cache)],
+            + [whole(array) for array in kept],
             out_specs=[pl.BlockSpec((tile, heads * HD), lambda i, first: (i, 0))]
             + [whole(array) for array in (near_mix, long_stat, long_mix, long_stat)],
             scratch_shapes=[
                 pltpu.VMEM((2, tile + 2 * rows, HD), jnp.bfloat16),
+                pltpu.VMEM((2, slot_here.shape[1], tile), jnp.int32),
                 pltpu.VMEM((1, heads * tile), jnp.float32),
                 pltpu.VMEM((1, heads * tile), jnp.float32),
                 pltpu.VMEM((HD, heads * tile), jnp.float32),
@@ -563,7 +611,7 @@
         ),
         out_shape=[shape((rows, heads * HD), jnp.bfloat16), near_mix, long_stat, long_mix, long_stat],
         name="local_attention",
-    )(begin, queries, *kept, request[None, :], begin[None, :], lead, cache)
+    )(begin, queries, *kept)
 
 
 def merge(into, top, total, part, part_top, part_total):
@@ -854,36 +902,29 @@
     new_len,
     cache_len,
 ):
-    seq_index = lax.axis_index("seq")
-    long_len = long_cache.shape[1] * lax.axis_size("seq")
-    rows = tokens.shape[0] * lax.axis_size("head")
-    starts = request_starts(new_len)
-    token_index = seq_index * rows + jnp.arange(rows, dtype=jnp.int32)
-    request, begin, position = token_facts(token_index, starts, cache_len, long_len)
-    table = rotate_table(position)
-    queries, here, before, earlier_slots, earlier_owner, lead_queries = gather_project(
+    owner = slot_owner[None, :]
+    queries, here, before, earlier_slots, earlier_owner, lead, request, begin = gather_project(
         tokens.reshape(2, LEAD, tokens.shape[1]),
         norm_gain[None, :],
         w_query,
         w_key,
         w_value,
-        table,
+        new_len,
+        cache_len,
         short_cache,
-        slot_owner[None, :],
+        owner,
     )
-    shift = (seq_index - 1) * rows
-    window_begin = jnp.where(request == starts.shape[0], rows, jnp.maximum(begin - shift, 0))
     attended, near_mix, near_stat, long_mix, long_stat = local_attention(
-        window_begin,
+        begin,
         queries,
         before,
         here,
         earlier_slots,
         short_cache,
         earlier_owner,
-        slot_owner[None, :],
+        owner,
         request,
-        lead_queries,
+        lead,
         long_cache,
     )
     return project_scatter(attended, w_out, long_mix, long_stat, near_mix, near_stat)

time: 114 us -> 108 us (0.947)
  other arithmetic: 5.86 us -> 0 us
    pallas_call x1, Pallas kernels: 39.5 us -> 43.7 us  [project_scatter(): pl.pallas_call(scatter_kernel, in_specs=[vmem] * 6, out_specs=vmem, out_s...]
    pallas_call x1, Pallas kernels: 16.1 us -> 13.8 us  [local_attention(): pl.pallas_call(local_kernel, grid_spec=pltpu.PrefetchScalarGridSpec(num_s...]
    cos x1 -> x0, other arithmetic: 1.88 us -> none  [rotate_table(): return jnp.concatenate([jnp.cos(angle), jnp.sin(angle)], axis=1)]
    pallas_call x1, Pallas kernels: 49.8 us -> 48.6 us  [gather_project(): pl.pallas_call(gather_kernel, in_specs=[vmem, vmem, hbm, hbm, hbm, smem,...]
    select_n x2 -> x0, other arithmetic: 1.21 us -> none  [on_device(): jnp.where(request == starts.shape[0], rows, jnp.maximum(begin - shift, 0))]
where the time goes in v6:
time: 108 us
  Pallas kernels  106 us (98%)
  local copies, waits for them, and re-layouts  2.06 us (2%)
    pallas_call x1, Pallas kernels, gather_project(): pl.pallas_call(gather_kernel, in_specs=[vmem, vmem, hbm, hbm, hbm, smem,...  48.6 us
    pallas_call x1, Pallas kernels, project_scatter(): pl.pallas_call(scatter_kernel, in_specs=[vmem] * 6, out_specs=vmem, out_s...  43.7 us
    pallas_call x1, Pallas kernels, local_attention(): pl.pallas_call(local_kernel, grid_spec=pltpu.PrefetchScalarGridSpec(num_s...  13.8 us

profile of v6, /device:TPU:1, one launch (start us, length us, event | category | flops | bytes accessed | tf_op | source)
XLA Modules:
  0.0 108.1 jit_solution(3896433272531219176)
XLA Ops:
  0.0 48.6 %gather_project.1 = (bf16[3,1024,128]{2,1,0:T(8,128)(2,1)}, bf16[2,1024,128]{2,1,0:T(8,128)(2,1)}, bf16[2,1024,128]{2,1,0:T(8,128)(2,1)}, bf16[2,256,128]{2,1,0:...) custom-call(bf16[2,64,3072]{2,1,0:T(8,128)(2,1)} %bitcast.3, ...), custom_call_target="tpu_custom_call" | custom-call | tf_op jit(solution)/shard_map/gather_project/pallas_call | solution.py:413
  48.6 13.8 %local_attention.1 = (bf16[1024,384]{1,0:T(8,128)(2,1)}, f32[128,256]{1,0:T(8,128)}, f32[8,256]{1,0:T(8,128)}, bf16[128,256]{1,0:T(8,128)(2,1)}, f32[8,256]{1,0:T(8,128)}) custom-call(s32[8,128]{1,0:T(8,128)} %get-tuple-element.18.begin_smem.begin_ref, bf16[3,1024,128]{2,1,0:T(8,128)(2,1)} %get-tuple-element.19.q_ref, ...), custom_call_target="tpu_custom_call" | custom-call | tf_op jit(solution)/shard_map/local_attention/pallas_call | solution.py:595
  62.4 43.7 %project_scatter.1 = bf16[128,3072]{1,0:T(8,128)(2,1)} custom-call(bf16[1024,384]{1,0:T(8,128)(2,1)} %get-tuple-element.26.attended_ref, bf16[384,3072]{1,0:T(8,128)(2,1)} %w_ref.1, bf16[128,256]{1,0:T(8,128)(2,1)} %get-tuple-element.27.long_mix_ref, f32[8,256]{1,0:T(8,128)} %get-tuple-element.28.long_stat_ref, f32[128,256]{1,0:T(8,128)} %get-tuple-element.29.near_mix_ref, ...), custom_call_target="tpu_custom_call" | custom-call | tf_op jit(solution)/shard_map/project_scatter/pallas_call | solution.py:863
  106.0 2.1 %copy.13 = bf16[128,3072]{1,0:T(8,128)(2,1)} copy(bf16[128,3072]{1,0:T(8,128)(2,1)} %project_scatter.1) | data formatting | bytes 1572864

commit v7 on v6

--- a/solution.py
+++ b/solution.py
@@ -33,6 +33,7 @@
 Z = 8
 Y = 4
 LONG_ROWS = 1024
+PARTS = 2
 UNITS = [(0, 0), (0, 1), (1, 0), (3, 0), (1, 1), (2, 0), (2, 1), (3, 1)]
 SLOT = {unit: number for number, unit in enumerate(UNITS)}
 
@@ -183,30 +184,56 @@
     def _():
         pl.semaphore_wait(barrier, 5 + 1)
 
+    def split(source):
+        size = half // PARTS
+        return [source.at[pl.ds(part * size, size), :] for part in range(PARTS)]
+
     def ring(number, source, to, unit):
         slot = SLOT[unit]
-        return pltpu.make_async_remote_copy(
-            src_ref=source,
-            dst_ref=held.at[slot, core],
-            send_sem=ring_send.at[number],
-            recv_sem=ring_recv.at[slot],
-            device_id=to,
-            device_id_type=MESH,
-        )
+        return [
+            pltpu.make_async_remote_copy(
+                src_ref=here,
+                dst_ref=there,
+                send_sem=ring_send.at[number, part],
+                recv_sem=ring_recv.at[slot, part],
+                device_id=to,
+                device_id_type=MESH,
+            )
+            for part, (here, there) in enumerate(zip(split(source), split(held.at[slot, core])))
+        ]
 
     def mine(unit):
         return held.at[SLOT[unit], core]
 
     def to_pair(unit):
         slot = SLOT[unit]
-        return pltpu.make_async_remote_copy(
-            src_ref=normed_ref.at[unit[1]] if unit[0] == 0 else mine(unit),
-            dst_ref=held.at[slot, core],
-            send_sem=pair_send.at[slot],
-            recv_sem=pair_recv.at[slot],
-            device_id=pair,
-            device_id_type=MESH,
-        )
+        source = normed_ref.at[unit[1]] if unit[0] == 0 else mine(unit)
+        return [
+            pltpu.make_async_remote_copy(
+                src_ref=here,
+                dst_ref=there,
+                send_sem=pair_send.at[slot, part],
+                recv_sem=pair_recv.at[slot, part],
+                device_id=pair,
+                device_id_type=MESH,
+            )
+            for part, (here, there) in enumerate(zip(split(source), split(held.at[slot, core])))
+        ]
+
+    def start(copies):
+        for copy in copies:
+            copy.start()
+
+    def await_pair(unit):
+        for copy in pairs[unit]:
+            copy.wait_recv()
+
+    def take_on(number, unit, further=None):
+        for part in range(PARTS):
+            rings[number][part].wait_recv()
+            if further is not None:
+                rings[further][part].start()
+            pairs[unit][part].start()
 
     rings = [
         ring(0, normed_ref.at[0], right, (1, 0)),
@@ -254,21 +281,21 @@
     def kv_copies(number):
         return [
             pltpu.make_async_remote_copy(
-                src_ref=kv_ref.at[:, pl.ds(start, half), :],
-                dst_ref=before_ref.at[:, pl.ds(start, half), :],
+                src_ref=kv_ref.at[:, pl.ds(first, half), :],
+                dst_ref=before_ref.at[:, pl.ds(first, half), :],
                 send_sem=kv_send.at[2 * number + part],
                 recv_sem=kv_recv.at[2 * number + part],
                 device_id=following,
                 device_id_type=MESH,
             )
-            for part, start in enumerate(row_starts(number))
+            for part, first in enumerate(row_starts(number))
         ]
 
-    rings[0].start()
-    pairs[(0, 0)].start()
-    rings[1].start()
-    rings[2].start()
-    pairs[(0, 1)].start()
+    start(rings[0])
+    start(pairs[(0, 0)])
+    start(rings[1])
+    start(rings[2])
+    start(pairs[(0, 1)])
     for copy in side:
         copy.start()
 
@@ -288,58 +315,46 @@
     for copy in weights:
         copy.wait()
     def event_0():
-        pairs[(0, 0)].wait_recv()
+        await_pair((0, 0))
 
     def event_1():
-        pairs[(0, 1)].wait_recv()
+        await_pair((0, 1))
 
     def event_2():
-        rings[0].wait_recv()
-        rings[3].start()
-        pairs[(1, 0)].start()
-        pairs[(1, 0)].wait_recv()
+        take_on(0, (1, 0), 3)
+        await_pair((1, 0))
 
     def event_3():
-        rings[1].wait_recv()
-        pairs[(3, 0)].start()
-        rings[2].wait_recv()
-        rings[4].start()
-        pairs[(1, 1)].start()
-        pairs[(3, 0)].wait_recv()
+        take_on(1, (3, 0))
+        take_on(2, (1, 1), 4)
+        await_pair((3, 0))
 
     def event_4():
-        pairs[(1, 1)].wait_recv()
+        await_pair((1, 1))
 
     def event_5():
-        rings[3].wait_recv()
-        pairs[(2, 0)].start()
-        pairs[(2, 0)].wait_recv()
+        take_on(3, (2, 0))
+        await_pair((2, 0))
 
     def event_6():
         @pl.when(seq == 0)
         def _():
             lead_ref[...] = q_ref[:, pl.ds(0, LEAD), :]
-            for copy in along_z:
-                copy.start()
-            for copy in along_x:
-                copy.start()
-
-        rings[4].wait_recv()
-        rings[5].start()
-        pairs[(2, 1)].start()
-        pairs[(2, 1)].wait_recv()
+            start(along_z)
+            start(along_x)
+
+        take_on(4, (2, 1), 5)
+        await_pair((2, 1))
 
     def event_7():
-        rings[5].wait_recv()
-        pairs[(3, 1)].start()
+        take_on(5, (3, 1))
 
         @pl.when((x == 0) & (z > 0))
         def _():
             along_z[0].wait_recv()
-            for copy in along_x:
-                copy.start()
-
-        pairs[(3, 1)].wait_recv()
+            start(along_x)
+
+        await_pair((3, 1))
 
     events = [event_0, event_1, event_2, event_3, event_4, event_5, event_6, event_7]
 
@@ -349,7 +364,7 @@
             pl.when(number == at)(event)
         block = held[number].reshape(2 * half, held.shape[3])
         starts = row_starts(number)
-        table = jnp.concatenate([table_ref[pl.ds(start, half), :] for start in starts], axis=0)
+        table = jnp.concatenate([table_ref[pl.ds(first, half), :] for first in starts], axis=0)
         swapped = pltpu.roll(table, HD // 2, 1)
         low = lax.broadcasted_iota(jnp.int32, table.shape, 1) < HD // 2
         cosine = jnp.where(low, table, swapped)
@@ -359,17 +374,16 @@
             return (product * cosine + pltpu.roll(product, HD // 2, 1) * sine).astype(jnp.bfloat16)
 
         def put(ref, at, rows):
-            for part, start in enumerate(starts):
-                ref[at, pl.ds(start, half), :] = rows[part * half : (part + 1) * half]
+            for part, first in enumerate(starts):
+                ref[at, pl.ds(first, half), :] = rows[part * half : (part + 1) * half]
 
         both = dot32(block, wkv_ref[...])
         put(kv_ref, 0, turned(both[:, :HD]))
         put(kv_ref, 1, both[:, HD:].astype(jnp.bfloat16))
         product = dot32(block, wq_ref[...])
+        start(kv_copies(number))
         for at in range(heads):
             put(q_ref, at, turned(product[:, at * HD : (at + 1) * HD]))
-        for copy in kv_copies(number):
-            copy.start()
 
     @pl.loop(0, len(UNITS))
     def _(number):
@@ -377,10 +391,8 @@
             copy.wait_recv()
             copy.wait_send()
 
-    for copy in rings:
+    for copy in sum(rings, []) + sum(pairs.values(), []):
         copy.wait_send()
-    for unit in UNITS:
-        pairs[unit].wait_send()
     for copy in side:
         copy.wait_recv()
         copy.wait_send()
@@ -431,10 +443,10 @@
             pltpu.VMEM((rows, HD), jnp.float32),
             pltpu.VMEM(facts, jnp.float32),
             pltpu.VMEM((len(UNITS), 2, half, width), jnp.bfloat16),
-            dma((6,)),
-            dma((len(UNITS),)),
-            dma((len(UNITS),)),
-            dma((len(UNITS),)),
+            dma((6, PARTS)),
+            dma((len(UNITS), PARTS)),
+            dma((len(UNITS), PARTS)),
+            dma((len(UNITS), PARTS)),
             dma((2 * len(UNITS),)),
             dma((2 * len(UNITS),)),
             dma((2,)),
@@ -624,8 +636,8 @@
 
 
 def scatter_kernel(
-    attended_ref,
-    w_ref,
+    attended_hbm,
+    w_hbm,
     long_mix_ref,
     long_stat_ref,
     near_mix_ref,
@@ -646,8 +658,17 @@
     ring_recv,
     sends,
     recvs,
+    attended_ref,
+    w_ref,
+    load_sem,
 ):
     seq, head, y, core = place()
+    loads = [
+        pltpu.make_async_copy(attended_hbm, attended_ref, load_sem.at[0]),
+        pltpu.make_async_copy(w_hbm, w_ref, load_sem.at[1]),
+    ]
+    for copy in loads:
+        copy.start()
     n_x = lax.axis_size("seq") // Z
     x, z = seq // Z, lax.rem(seq, Z)
     way = 1 - 2 * core
@@ -776,6 +797,8 @@
             for copy in state_copies(at - 1, x * Z, computed):
                 copy.start()
 
+    for copy in loads:
+        copy.wait()
     rows = stack(1)
     for piece in range(PIECES):
         project(rows, 1, piece)
@@ -862,7 +885,7 @@
     dma = pltpu.SemaphoreType.DMA
     return pl.pallas_call(
         scatter_kernel,
-        in_specs=[vmem] * 6,
+        in_specs=[pl.BlockSpec(memory_space=pl.ANY)] * 2 + [vmem] * 4,
         out_specs=vmem,
         out_shape=jax.ShapeDtypeStruct((2 * half, width), jnp.bfloat16),
         scratch_shapes=[
@@ -881,6 +904,9 @@
             dma((2, 3, PIECES)),
             dma((2,)),
             dma((2, slots)),
+            pltpu.VMEM(attended.shape, jnp.bfloat16),
+            pltpu.VMEM(w_out.shape, jnp.bfloat16),
+            dma((2,)),
         ],
         compiler_params=pltpu.CompilerParams(
             collective_id=1, has_side_effects=True, vmem_limit_bytes=LIMIT

time: 108 us -> 103 us (0.954)
  Pallas kernels: 106 us -> 101 us
    pallas_call x1, Pallas kernels: 43.7 us -> 40.6 us  [project_scatter(): pl.pallas_call(scatter_kernel, in_specs=[pl.BlockSpec(memory_space=pl.ANY...]
    pallas_call x1, Pallas kernels: 48.6 us -> 47.2 us  [gather_project(): pl.pallas_call(gather_kernel, in_specs=[vmem, vmem, hbm, hbm, hbm, smem,...]
where the time goes in v7:
time: 103 us
  Pallas kernels  101 us (98%)
  local copies, waits for them, and re-layouts  2.06 us (2%)
    pallas_call x1, Pallas kernels, gather_project(): pl.pallas_call(gather_kernel, in_specs=[vmem, vmem, hbm, hbm, hbm, smem,...  47.2 us
    pallas_call x1, Pallas kernels, project_scatter(): pl.pallas_call(scatter_kernel, in_specs=[pl.BlockSpec(memory_space=pl.ANY...  40.6 us
    pallas_call x1, Pallas kernels, local_attention(): pl.pallas_call(local_kernel, grid_spec=pltpu.PrefetchScalarGridSpec(num_s...  13.3 us
    unnamed x1, local copies, waits for them, and re-layouts  2.06 us

profile of v7, /device:TPU:1, one launch (start us, length us, event | category | flops | bytes accessed | tf_op | source)
XLA Modules:
  0.0 103.1 jit_solution(15632843911561462391)
XLA Ops:
  0.0 47.2 %gather_project.1 = (bf16[3,1024,128]{2,1,0:T(8,128)(2,1)}, bf16[2,1024,128]{2,1,0:T(8,128)(2,1)}, bf16[2,1024,128]{2,1,0:T(8,128)(2,1)}, bf16[2,256,128]{2,1,0:...) custom-call(bf16[2,64,3072]{2,1,0:T(8,128)(2,1)} %bitcast.3, ...), custom_call_target="tpu_custom_call" | custom-call | tf_op jit(solution)/shard_map/gather_project/pallas_call | solution.py:425
  47.2 13.3 %local_attention.1 = (bf16[1024,384]{1,0:T(8,128)(2,1)}, f32[128,256]{1,0:T(8,128)}, f32[8,256]{1,0:T(8,128)}, bf16[128,256]{1,0:T(8,128)(2,1)}, f32[8,256]{1,0:T(8,128)}) custom-call(s32[8,128]{1,0:T(8,128)} %get-tuple-element.18.begin_smem.begin_ref, bf16[3,1024,128]{2,1,0:T(8,128)(2,1)} %get-tuple-element.19.q_ref, ...), custom_call_target="tpu_custom_call" | custom-call | tf_op jit(solution)/shard_map/local_attention/pallas_call | solution.py:607
  60.4 40.6 %project_scatter.1 = bf16[128,3072]{1,0:T(8,128)(2,1)} custom-call(bf16[1024,384]{1,0:T(8,128)(2,1)} %get-tuple-element.26.attended_hbm, bf16[384,3072]{1,0:T(8,128)(2,1)} %w_hbm.1, bf16[128,256]{1,0:T(8,128)(2,1)} %get-tuple-element.27.long_mix_ref, f32[8,256]{1,0:T(8,128)} %get-tuple-element.28.long_stat_ref, f32[128,256]{1,0:T(8,128)} %get-tuple-element.29.near_mix_ref, ...), custom_call_target="tpu_custom_call" | custom-call | tf_op jit(solution)/shard_map/project_scatter/pallas_call | solution.py:886
  101.0 2.1 %copy.13 = bf16[128,3072]{1,0:T(8,128)(2,1)} copy(bf16[128,3072]{1,0:T(8,128)(2,1)} %project_scatter.1) | data formatting | bytes 1572864

commit v8 on v7

--- a/solution.py
+++ b/solution.py
@@ -714,12 +714,16 @@
         parts += [rows_of(lax.rem(y + k * way + 2 * Y * 2, Y), core, later) for k in range(Y)]
         return jnp.concatenate(parts, axis=0)
 
-    def pair_copy(later, piece):
+    def pair_copy(later, number):
+        if later:
+            at = (later, slice(None), columns(number))
+        else:
+            at = (later, pl.ds(number * half, half), slice(None))
         return pltpu.make_async_remote_copy(
-            src_ref=pair_out.at[later, :, columns(piece)],
-            dst_ref=pair_in.at[later, :, columns(piece)],
-            send_sem=pair_send.at[later, piece],
-            recv_sem=pair_recv.at[later, piece],
+            src_ref=pair_out.at[at],
+            dst_ref=pair_in.at[at],
+            send_sem=pair_send.at[later, number],
+            recv_sem=pair_recv.at[later, number],
             device_id=pair,
             device_id_type=MESH,
         )
@@ -811,6 +815,12 @@
     for piece in range(PIECES):
         project(rows, 0, piece)
 
+    lead_block = jnp.where(seq == 0, lax.rem(Y - y, Y), -1)
+    for k in range(Y):
+        @pl.when((core == 0) | (lead_block != k))
+        def _():
+            pair_copy(0, k).start()
+
     for piece in range(PIECES):
         pass_on(1, 1, piece, chip_sum(1, 2, piece) + arrived(1, 0, piece))
 
@@ -827,6 +837,16 @@
 
     for piece in range(PIECES):
         pass_on(1, 2, piece, chip_sum(1, 1, piece) + arrived(1, 1, piece))
+
+    def early_hop(step, k):
+        pair_copy(0, k).wait_recv()
+        for piece in range(PIECES):
+            pass_on(0, step, piece, chip_sum(0, k, piece))
+
+    for step, k in ((0, 2), (2, 3)):
+        @pl.when((core == 1) | (lead_block != k))
+        def _():
+            early_hop(step, k)
 
     @pl.when(seq == 0)
     def _():
@@ -848,17 +868,23 @@
                 at = pl.multiple_of(lax.rem(Y - y, Y) * half, half)
                 pair_out[0, pl.ds(at, half), columns(piece)] = product
 
-    for piece in range(PIECES):
-        pair_copy(0, piece).start()
-    for piece in range(PIECES):
-        pair_copy(0, piece).wait_recv()
-        pass_on(0, 0, piece, chip_sum(0, 2, piece))
-        pass_on(0, 2, piece, chip_sum(0, 3, piece))
+    for k in range(Y):
+        @pl.when((core == 1) & (lead_block == k))
+        def _():
+            pair_copy(0, k).start()
+
+    for step, k in ((0, 2), (2, 3)):
+        @pl.when((core == 0) & (lead_block == k))
+        def _():
+            early_hop(step, k)
+
     for piece in range(PIECES):
         value = chip_sum(1, 0, piece) + arrived(1, 2, piece)
         out_ref[pl.ds(half, half), columns(piece)] = value.astype(jnp.bfloat16)
+    pair_copy(0, 1).wait_recv()
     for piece in range(PIECES):
         pass_on(0, 1, piece, chip_sum(0, 1, piece) + arrived(0, 0, piece))
+    pair_copy(0, 0).wait_recv()
     for piece in range(PIECES):
         value = chip_sum(0, 0, piece) + arrived(0, 2, piece) + arrived(0, 1, piece)
         out_ref[pl.ds(0, half), columns(piece)] = value.astype(jnp.bfloat16)

time: 103 us -> 103 us (level)
  no operation moved by 1% of the time
where the time goes in v8:
time: 103 us
  Pallas kernels  101 us (98%)
  local copies, waits for them, and re-layouts  2.06 us (2%)
    pallas_call x1, Pallas kernels, gather_project(): pl.pallas_call(gather_kernel, in_specs=[vmem, vmem, hbm, hbm, hbm, smem,...  47.2 us
    pallas_call x1, Pallas kernels, project_scatter(): pl.pallas_call(scatter_kernel, in_specs=[pl.BlockSpec(memory_space=pl.ANY...  40.9 us
    pallas_call x1, Pallas kernels, local_attention(): pl.pallas_call(local_kernel, grid_spec=pltpu.PrefetchScalarGridSpec(num_s...  12.8 us
    unnamed x1, local copies, waits for them, and re-layouts  2.06 us

profile of v8, /device:TPU:1, one launch (start us, length us, event | category | flops | bytes accessed | tf_op | source)
XLA Modules:
  0.0 102.9 jit_solution(4252145248026223010)
XLA Ops:
  0.0 47.2 %gather_project.1 = (bf16[3,1024,128]{2,1,0:T(8,128)(2,1)}, bf16[2,1024,128]{2,1,0:T(8,128)(2,1)}, bf16[2,1024,128]{2,1,0:T(8,128)(2,1)}, bf16[2,256,128]{2,1,0:...) custom-call(bf16[2,64,3072]{2,1,0:T(8,128)(2,1)} %bitcast.3, ...), custom_call_target="tpu_custom_call" | custom-call | tf_op jit(solution)/shard_map/gather_project/pallas_call | solution.py:425
  47.2 12.8 %local_attention.1 = (bf16[1024,384]{1,0:T(8,128)(2,1)}, f32[128,256]{1,0:T(8,128)}, f32[8,256]{1,0:T(8,128)}, bf16[128,256]{1,0:T(8,128)(2,1)}, f32[8,256]{1,0:T(8,128)}) custom-call(s32[8,128]{1,0:T(8,128)} %get-tuple-element.18.begin_smem.begin_ref, bf16[3,1024,128]{2,1,0:T(8,128)(2,1)} %get-tuple-element.19.q_ref, ...), custom_call_target="tpu_custom_call" | custom-call | tf_op jit(solution)/shard_map/local_attention/pallas_call | solution.py:607
  60.0 40.9 %project_scatter.1 = bf16[128,3072]{1,0:T(8,128)(2,1)} custom-call(bf16[1024,384]{1,0:T(8,128)(2,1)} %get-tuple-element.26.attended_hbm, bf16[384,3072]{1,0:T(8,128)(2,1)} %w_hbm.1, bf16[128,256]{1,0:T(8,128)(2,1)} %get-tuple-element.27.long_mix_ref, f32[8,256]{1,0:T(8,128)} %get-tuple-element.28.long_stat_ref, f32[128,256]{1,0:T(8,128)} %get-tuple-element.29.near_mix_ref, ...), custom_call_target="tpu_custom_call" | custom-call | tf_op jit(solution)/shard_map/project_scatter/pallas_call | solution.py:912
  100.9 2.1 %copy.13 = bf16[128,3072]{1,0:T(8,128)(2,1)} copy(bf16[128,3072]{1,0:T(8,128)(2,1)} %project_scatter.1) | data formatting | bytes 1572864

commit v9 on v8

--- a/solution.py
+++ b/solution.py
@@ -33,7 +33,7 @@
 Z = 8
 Y = 4
 LONG_ROWS = 1024
-PARTS = 2
+PARTS = 4
 UNITS = [(0, 0), (0, 1), (1, 0), (3, 0), (1, 1), (2, 0), (2, 1), (3, 1)]
 SLOT = {unit: number for number, unit in enumerate(UNITS)}
 

time: 103 us -> 106 us (1.029); the launches traced: 103 us -> 104 us
  no operation moved by 1% of the time
where the time goes in v9:
time: 106 us; the launch traced here: 104 us
  Pallas kernels  102 us (96%)
  local copies, waits for them, and re-layouts  2.06 us (2%)
    pallas_call x1, Pallas kernels, gather_project(): pl.pallas_call(gather_kernel, in_specs=[vmem, vmem, hbm, hbm, hbm, smem,...  47.6 us
    pallas_call x1, Pallas kernels, project_scatter(): pl.pallas_call(scatter_kernel, in_specs=[pl.BlockSpec(memory_space=pl.ANY...  41.2 us
    pallas_call x1, Pallas kernels, local_attention(): pl.pallas_call(local_kernel, grid_spec=pltpu.PrefetchScalarGridSpec(num_s...  13.3 us

profile of v9, /device:TPU:1, one launch (start us, length us, event | category | flops | bytes accessed | tf_op | source)
XLA Modules:
  0.0 104.1 jit_solution(11815170849416606391)
XLA Ops:
  0.0 47.6 %gather_project.1 = (bf16[3,1024,128]{2,1,0:T(8,128)(2,1)}, bf16[2,1024,128]{2,1,0:T(8,128)(2,1)}, bf16[2,1024,128]{2,1,0:T(8,128)(2,1)}, bf16[2,256,128]{2,1,0:...) custom-call(bf16[2,64,3072]{2,1,0:T(8,128)(2,1)} %bitcast.3, ...), custom_call_target="tpu_custom_call" | custom-call | tf_op jit(solution)/shard_map/gather_project/pallas_call | solution.py:425
  47.6 13.3 %local_attention.1 = (bf16[1024,384]{1,0:T(8,128)(2,1)}, f32[128,256]{1,0:T(8,128)}, f32[8,256]{1,0:T(8,128)}, bf16[128,256]{1,0:T(8,128)(2,1)}, f32[8,256]{1,0:T(8,128)}) custom-call(s32[8,128]{1,0:T(8,128)} %get-tuple-element.18.begin_smem.begin_ref, bf16[3,1024,128]{2,1,0:T(8,128)(2,1)} %get-tuple-element.19.q_ref, ...), custom_call_target="tpu_custom_call" | custom-call | tf_op jit(solution)/shard_map/local_attention/pallas_call | solution.py:607
  60.9 41.2 %project_scatter.1 = bf16[128,3072]{1,0:T(8,128)(2,1)} custom-call(bf16[1024,384]{1,0:T(8,128)(2,1)} %get-tuple-element.26.attended_hbm, bf16[384,3072]{1,0:T(8,128)(2,1)} %w_hbm.1, bf16[128,256]{1,0:T(8,128)(2,1)} %get-tuple-element.27.long_mix_ref, f32[8,256]{1,0:T(8,128)} %get-tuple-element.28.long_stat_ref, f32[128,256]{1,0:T(8,128)} %get-tuple-element.29.near_mix_ref, ...), custom_call_target="tpu_custom_call" | custom-call | tf_op jit(solution)/shard_map/project_scatter/pallas_call | solution.py:912
  102.0 2.1 %copy.13 = bf16[128,3072]{1,0:T(8,128)(2,1)} copy(bf16[128,3072]{1,0:T(8,128)(2,1)} %project_scatter.1) | data formatting | bytes 1572864
